TPU v7x, 32 devices: a whole 2x2x4 slice. The times are simulated.
32 devices in a mesh: ctx: 8 (over y, x, core), fsdp: 4 (over z).
Axes of the slice: x: 2, y: 2, z: 4, core: 2. Of those that a mesh axis runs over, the one named last changes fastest.
Arguments:
- tokens: bfloat16 [4, 2, 8, 64, 2048], P('fsdp', None, 'ctx'), may hold values from -6 to 6
- segment_ids: int32 [4, 1024], P('fsdp'), may hold values from 0 to 2, never falling along the last dimension, each value on 1 to 512 neighbouring positions
- cotangent: bfloat16 [4, 2, 8, 64, 2048], P('fsdp', None, 'ctx'), may hold values from -6 to 6
- norm_attn: bfloat16 [2048], P('fsdp'), may hold values from 0.25 to 1.75
- w_query: bfloat16 [2048, 2048], P('fsdp'), may hold values from -0.125 to 0.125
- w_key: bfloat16 [2048, 1024], P('fsdp'), may hold values from -0.125 to 0.125
- w_value: bfloat16 [2048, 1024], P('fsdp'), may hold values from -0.125 to 0.125
- q_gain: bfloat16 [128], P('fsdp'), may hold values from 0.25 to 1.75
- k_gain: bfloat16 [128], P('fsdp'), may hold values from 0.25 to 1.75
- w_out: bfloat16 [2048, 2048], P('fsdp'), may hold values from -1 to 1
- norm_ffn: bfloat16 [2048], P('fsdp'), may hold values from 0.25 to 1.75
- w_gate: bfloat16 [2048, 6144], P('fsdp'), may hold values from -0.125 to 0.125
- w_up: bfloat16 [2048, 6144], P('fsdp'), may hold values from -0.125 to 0.125
- w_down: bfloat16 [6144, 2048], P('fsdp'), may hold values from -0.078125 to 0.078125
Outputs:
- block_out: bfloat16 [4, 2, 8, 64, 2048], P('fsdp', None, 'ctx')
- input_grad: float32 [4, 2, 8, 64, 2048], P('fsdp', None, 'ctx')
- grad_norm_attn: float32 [2048], P(('ctx', 'fsdp'))
- grad_query: float32 [2048, 2048], P(('ctx', 'fsdp'))
- grad_key: float32 [2048, 1024], P(('ctx', 'fsdp'))
- grad_value: float32 [2048, 1024], P(('ctx', 'fsdp'))
- grad_q_gain: float32 [128], P(('ctx', 'fsdp'))
- grad_k_gain: float32 [128], P(('ctx', 'fsdp'))
- grad_out_proj: float32 [2048, 2048], P(('ctx', 'fsdp'))
- grad_norm_ffn: float32 [2048], P(('ctx', 'fsdp'))
- grad_gate: float32 [2048, 6144], P(('ctx', 'fsdp'))
- grad_up: float32 [2048, 6144], P(('ctx', 'fsdp'))
- grad_down: float32 [6144, 2048], P(('ctx', 'fsdp'))
All inputs are finite; a program needn't handle non-finite values.
Results may differ from a plain program's by a relative error of at most 0.02.
Values may be sent and summed in bfloat16 or wider, within the bound.
No kernel may reach another device: no remote copies, remote signals or barrier semaphores. Data moves between devices by JAX's collectives and lax.ppermute only.
A program may use at most 448 MiB of HBM per device.

v0:
```python
import jax
import jax.numpy as jnp
from jax import lax
from jax.sharding import PartitionSpec as P

D = 2048
H = 16
KVH = 8
HD = 128
BLOCK = 64
QD = 2048
KVD = 1024


epsilon = 1e-06
theta_base = 1000000.0


def doc_places(segments):
    length = segments.shape[0]
    row_index = jnp.arange(length, dtype=jnp.int32)
    before = jnp.concatenate([jnp.full((1,), -1, jnp.int32), segments[:-1]])
    starts = jnp.where(segments != before, row_index, jnp.zeros_like(row_index))
    return row_index - lax.cummax(starts, axis=0)


def rope_tables(places):
    frequency = theta_base ** (-(jnp.arange(HD // 2, dtype=jnp.float32) * 2.0) / HD)
    angles = places.astype(jnp.float32)[..., None] * frequency
    angles = jnp.concatenate([angles, angles], axis=-1)
    return (jnp.cos(angles), jnp.sin(angles))


def rotate_half(values):
    middle_index = values.shape[-1] // 2
    return jnp.concatenate([-values[..., middle_index:], values[..., :middle_index]], axis=-1)


def rotate_back(values):
    middle_index = values.shape[-1] // 2
    return jnp.concatenate([values[..., middle_index:], -values[..., :middle_index]], axis=-1)


def rms_scale(values, gain):
    factor = lax.rsqrt(jnp.mean(values * values, axis=-1, keepdims=True) + epsilon)
    return (values * factor * gain, factor)


def rms_back(values, factor, gain, upstream):
    scaled = gain * upstream
    inner = jnp.mean(values * scaled, axis=-1, keepdims=True)
    lead_axes = tuple(range(upstream.ndim - 1))
    return (
        factor * scaled - values * factor**3 * inner,
        jnp.sum(upstream * values * factor, axis=lead_axes),
    )


def local(
    tokens,
    segment_ids,
    cotangent,
    norm_attn,
    w_query,
    w_key,
    w_value,
    q_gain,
    k_gain,
    w_out,
    norm_ffn,
    w_gate,
    w_up,
    w_down,
):
    ctx_size = lax.axis_size("ctx")
    ctx_index = lax.axis_index("ctx")
    local_seqs = tokens.shape[0]
    seq_rows = 2 * BLOCK
    row_count = local_seqs * seq_rows
    group_size = H // KVH
    score_scale = HD ** (-0.5)
    features = tokens.reshape(row_count, D).astype(jnp.float32)
    places = jax.vmap(doc_places)(segment_ids)
    offsets = jnp.arange(BLOCK, dtype=jnp.int32)
    query_index = jnp.concatenate(
        [ctx_index * BLOCK + offsets, (2 * ctx_size - 1 - ctx_index) * BLOCK + offsets]
    )
    owner_index = jnp.arange(ctx_size, dtype=jnp.int32)[:, None, None]
    side_index = jnp.arange(2, dtype=jnp.int32)[None, :, None]
    key_index = (
        jnp.where(side_index == 0, owner_index, 2 * ctx_size - 1 - owner_index) * BLOCK
        + offsets[None, None, :]
    ).reshape(-1)
    query_segs = jnp.take(segment_ids, query_index, axis=1)
    key_segs = jnp.take(segment_ids, key_index, axis=1)
    visible = (query_segs[:, :, None] == key_segs[:, None, :]) & (
        key_index[None, None, :] <= query_index[None, :, None]
    )
    cosine_table, sine_table = rope_tables(jnp.take(places, query_index, axis=1))
    cosine_table = cosine_table.reshape(row_count, 1, HD)
    sine_table = sine_table.reshape(row_count, 1, HD)
    gathered = (
        lax.all_gather(norm_attn, "fsdp", axis=0, tiled=True),
        lax.all_gather(w_query, "fsdp", axis=0, tiled=True),
        lax.all_gather(w_key, "fsdp", axis=0, tiled=True),
        lax.all_gather(w_value, "fsdp", axis=0, tiled=True),
        lax.all_gather(q_gain, "fsdp", axis=0, tiled=True),
        lax.all_gather(k_gain, "fsdp", axis=0, tiled=True),
        lax.all_gather(w_out, "fsdp", axis=0, tiled=True),
        lax.all_gather(norm_ffn, "fsdp", axis=0, tiled=True),
        lax.all_gather(w_gate, "fsdp", axis=0, tiled=True),
        lax.all_gather(w_up, "fsdp", axis=0, tiled=True),
        lax.all_gather(w_down, "fsdp", axis=0, tiled=True),
    )
    gain_attn = gathered[0].astype(jnp.float32)
    query_w, key_w, value_w = (gathered[1], gathered[2], gathered[3])
    query_gain = gathered[4].astype(jnp.float32)
    key_gain = gathered[5].astype(jnp.float32)
    out_w = gathered[6]
    gain_ffn = gathered[7].astype(jnp.float32)
    gate_w, up_w, down_w = (gathered[8], gathered[9], gathered[10])
    normed_attn, factor_attn = rms_scale(features, gain_attn)
    normed_low = normed_attn.astype(jnp.bfloat16)
    query_raw = jnp.dot(normed_low, query_w, preferred_element_type=jnp.float32).reshape(
        row_count, H, HD
    )
    key_raw = jnp.dot(normed_low, key_w, preferred_element_type=jnp.float32).reshape(
        row_count, KVH, HD
    )
    value_low = jnp.dot(normed_low, value_w, preferred_element_type=jnp.float32).astype(
        jnp.bfloat16
    )
    query_norm, query_factor = rms_scale(query_raw, query_gain)
    key_norm, key_factor = rms_scale(key_raw, key_gain)
    query_low = (query_norm * cosine_table + rotate_half(query_norm) * sine_table).astype(
        jnp.bfloat16
    )
    key_low = (key_norm * cosine_table + rotate_half(key_norm) * sine_table).astype(jnp.bfloat16)
    key_rows, value_rows = (
        lax.all_gather(key_low.reshape(local_seqs, 1, 2, BLOCK, KVD), "ctx", axis=1, tiled=True),
        lax.all_gather(value_low.reshape(local_seqs, 1, 2, BLOCK, KVD), "ctx", axis=1, tiled=True),
    )
    key_rows = key_rows.reshape(local_seqs, -1, KVH, HD)
    value_rows = value_rows.reshape(local_seqs, -1, KVH, HD)
    key_total = key_rows.shape[1]
    query_groups = query_low.reshape(local_seqs, seq_rows, KVH, group_size, HD)

    def head_scores(head, query_block):
        key_block = lax.dynamic_index_in_dim(key_rows, head, 2, keepdims=False)
        scores = (
            jnp.einsum("stgd,skd->sgtk", query_block, key_block, preferred_element_type=jnp.float32)
            * score_scale
        )
        return (jnp.where(visible[:, None], scores, -jnp.inf), key_block)

    def attend(head, carry):
        mixed_out, log_totals = carry
        query_block = lax.dynamic_index_in_dim(query_groups, head, 2, keepdims=False)
        scores, key_block = head_scores(head, query_block)
        row_peak = jnp.max(scores, axis=-1, keepdims=True)
        powers = jnp.exp(scores - row_peak)
        totals = jnp.sum(powers, axis=-1, keepdims=True)
        probs_low = (powers / totals).astype(jnp.bfloat16)
        value_block = lax.dynamic_index_in_dim(value_rows, head, 2, keepdims=False)
        mixed_block = jnp.einsum(
            "sgtk,skd->stgd", probs_low, value_block, preferred_element_type=jnp.float32
        ).astype(jnp.bfloat16)
        mixed_out = lax.dynamic_update_index_in_dim(mixed_out, mixed_block, head, 2)
        log_totals = lax.dynamic_update_index_in_dim(
            log_totals, (row_peak + jnp.log(totals))[..., 0], head, 0
        )
        return (mixed_out, log_totals)

    mixed_start = jnp.zeros((local_seqs, seq_rows, KVH, group_size, HD), jnp.bfloat16)
    totals_start = jnp.zeros((KVH, local_seqs, group_size, seq_rows), jnp.float32)
    mixed_out, log_totals = lax.fori_loop(0, KVH, attend, (mixed_start, totals_start))
    attended = mixed_out.reshape(row_count, QD)
    middle = features + jnp.dot(attended, out_w, preferred_element_type=jnp.float32)
    normed_ffn, factor_ffn = rms_scale(middle, gain_ffn)
    ffn_low = normed_ffn.astype(jnp.bfloat16)
    gate_proj = jnp.dot(ffn_low, gate_w, preferred_element_type=jnp.float32)
    up_proj = jnp.dot(ffn_low, up_w, preferred_element_type=jnp.float32)
    sigmoid_gate = jax.nn.sigmoid(gate_proj)
    silu_gate = gate_proj * sigmoid_gate
    hidden_low = (silu_gate * up_proj).astype(jnp.bfloat16)
    block_sum = middle + jnp.dot(hidden_low, down_w, preferred_element_type=jnp.float32)
    block_out = block_sum.astype(jnp.bfloat16).reshape(tokens.shape)
    regathered = (
        lax.all_gather(w_query, "fsdp", axis=0, tiled=True),
        lax.all_gather(w_key, "fsdp", axis=0, tiled=True),
        lax.all_gather(w_value, "fsdp", axis=0, tiled=True),
        lax.all_gather(w_out, "fsdp", axis=0, tiled=True),
        lax.all_gather(w_gate, "fsdp", axis=0, tiled=True),
        lax.all_gather(w_up, "fsdp", axis=0, tiled=True),
        lax.all_gather(w_down, "fsdp", axis=0, tiled=True),
    )
    query_w, key_w, value_w, out_w = (regathered[0], regathered[1], regathered[2], regathered[3])
    gate_w, up_w, down_w = (regathered[4], regathered[5], regathered[6])
    upstream = cotangent.reshape(row_count, D).astype(jnp.float32)
    upstream_low = upstream.astype(jnp.bfloat16)
    grad_down = jnp.einsum(
        "tf,td->fd", hidden_low, upstream_low, preferred_element_type=jnp.float32
    )
    grad_hidden = jnp.einsum("td,fd->tf", upstream_low, down_w, preferred_element_type=jnp.float32)
    slope = sigmoid_gate * (1.0 + gate_proj * (1.0 - sigmoid_gate))
    gate_grad_low = (grad_hidden * up_proj * slope).astype(jnp.bfloat16)
    up_grad_low = (grad_hidden * silu_gate).astype(jnp.bfloat16)
    grad_gate = jnp.einsum("td,tf->df", ffn_low, gate_grad_low, preferred_element_type=jnp.float32)
    grad_up = jnp.einsum("td,tf->df", ffn_low, up_grad_low, preferred_element_type=jnp.float32)
    grad_normed_ffn = jnp.einsum(
        "tf,df->td", gate_grad_low, gate_w, preferred_element_type=jnp.float32
    )
    grad_normed_ffn = grad_normed_ffn + jnp.einsum(
        "tf,df->td", up_grad_low, up_w, preferred_element_type=jnp.float32
    )
    middle_part, grad_gain_ffn = rms_back(middle, factor_ffn, gain_ffn, grad_normed_ffn)
    grad_middle = upstream + middle_part
    middle_low = grad_middle.astype(jnp.bfloat16)
    grad_out = jnp.einsum("tq,td->qd", attended, middle_low, preferred_element_type=jnp.float32)
    attended_grad = jnp.einsum(
        "td,qd->tq", middle_low, out_w, preferred_element_type=jnp.float32
    ).astype(jnp.bfloat16)
    attended_grad = attended_grad.reshape(local_seqs, seq_rows, KVH, group_size, HD)

    def attend_back(head, carry):
        query_grads, key_grads, value_grads = carry
        query_block = lax.dynamic_index_in_dim(query_groups, head, 2, keepdims=False)
        scores, key_block = head_scores(head, query_block)
        value_block = lax.dynamic_index_in_dim(value_rows, head, 2, keepdims=False)
        grad_block = lax.dynamic_index_in_dim(attended_grad, head, 2, keepdims=False)
        log_block = lax.dynamic_index_in_dim(log_totals, head, 0, keepdims=False)
        probs = jnp.exp(scores - log_block[..., None])
        grad_probs = jnp.einsum(
            "stgd,skd->sgtk", grad_block, value_block, preferred_element_type=jnp.float32
        )
        inner = jnp.sum(probs * grad_probs, axis=-1, keepdims=True)
        score_grads = (probs * (grad_probs - inner)).astype(jnp.bfloat16)
        query_part = (
            jnp.einsum("sgtk,skd->stgd", score_grads, key_block, preferred_element_type=jnp.float32)
            * score_scale
        )
        key_part = (
            jnp.einsum(
                "sgtk,stgd->skd", score_grads, query_block, preferred_element_type=jnp.float32
            )
            * score_scale
        )
        value_part = jnp.einsum(
            "sgtk,stgd->skd",
            probs.astype(jnp.bfloat16),
            grad_block,
            preferred_element_type=jnp.float32,
        )
        query_grads = lax.dynamic_update_index_in_dim(query_grads, query_part, head, 2)
        key_grads = lax.dynamic_update_index_in_dim(key_grads, key_part, head, 2)
        value_grads = lax.dynamic_update_index_in_dim(value_grads, value_part, head, 2)
        return (query_grads, key_grads, value_grads)

    query_start = jnp.zeros((local_seqs, seq_rows, KVH, group_size, HD), jnp.float32)
    key_start = jnp.zeros((local_seqs, key_total, KVH, HD), jnp.float32)
    query_grads, key_grads, value_grads = lax.fori_loop(
        0, KVH, attend_back, (query_start, key_start, key_start)
    )
    key_sum, value_sum = (
        lax.psum_scatter(
            key_grads.reshape(local_seqs, ctx_size, 2, BLOCK, KVD).astype(jnp.bfloat16),
            "ctx",
            scatter_dimension=1,
            tiled=True,
        ).astype(jnp.float32),
        lax.psum_scatter(
            value_grads.reshape(local_seqs, ctx_size, 2, BLOCK, KVD).astype(jnp.bfloat16),
            "ctx",
            scatter_dimension=1,
            tiled=True,
        ).astype(jnp.float32),
    )
    key_final = key_sum.reshape(row_count, KVH, HD)
    value_grad_low = value_sum.reshape(row_count, KVD).astype(jnp.bfloat16)
    query_final = query_grads.reshape(row_count, H, HD)
    query_rot = query_final * cosine_table + rotate_back(query_final * sine_table)
    key_rot = key_final * cosine_table + rotate_back(key_final * sine_table)
    query_pre, grad_query_gain = rms_back(query_raw, query_factor, query_gain, query_rot)
    key_pre, grad_key_gain = rms_back(key_raw, key_factor, key_gain, key_rot)
    query_grad_low = query_pre.reshape(row_count, QD).astype(jnp.bfloat16)
    key_grad_low = key_pre.reshape(row_count, KVD).astype(jnp.bfloat16)
    grad_query = jnp.einsum(
        "td,tq->dq", normed_low, query_grad_low, preferred_element_type=jnp.float32
    )
    grad_key = jnp.einsum("td,tq->dq", normed_low, key_grad_low, preferred_element_type=jnp.float32)
    grad_value = jnp.einsum(
        "td,tq->dq", normed_low, value_grad_low, preferred_element_type=jnp.float32
    )
    grad_normed_attn = jnp.einsum(
        "tq,dq->td", query_grad_low, query_w, preferred_element_type=jnp.float32
    )
    grad_normed_attn = grad_normed_attn + jnp.einsum(
        "tq,dq->td", key_grad_low, key_w, preferred_element_type=jnp.float32
    )
    grad_normed_attn = grad_normed_attn + jnp.einsum(
        "tq,dq->td", value_grad_low, value_w, preferred_element_type=jnp.float32
    )
    input_part, grad_gain_attn = rms_back(features, factor_attn, gain_attn, grad_normed_attn)
    input_grad = (grad_middle + input_part).reshape(tokens.shape)
    summed = (
        lax.psum_scatter(grad_gain_attn, ("ctx", "fsdp"), scatter_dimension=0, tiled=True),
        lax.psum_scatter(grad_query, ("ctx", "fsdp"), scatter_dimension=0, tiled=True),
        lax.psum_scatter(grad_key, ("ctx", "fsdp"), scatter_dimension=0, tiled=True),
        lax.psum_scatter(grad_value, ("ctx", "fsdp"), scatter_dimension=0, tiled=True),
        lax.psum_scatter(grad_query_gain, ("ctx", "fsdp"), scatter_dimension=0, tiled=True),
        lax.psum_scatter(grad_key_gain, ("ctx", "fsdp"), scatter_dimension=0, tiled=True),
        lax.psum_scatter(grad_out, ("ctx", "fsdp"), scatter_dimension=0, tiled=True),
        lax.psum_scatter(grad_gain_ffn, ("ctx", "fsdp"), scatter_dimension=0, tiled=True),
        lax.psum_scatter(grad_gate, ("ctx", "fsdp"), scatter_dimension=0, tiled=True),
        lax.psum_scatter(grad_up, ("ctx", "fsdp"), scatter_dimension=0, tiled=True),
        lax.psum_scatter(grad_down, ("ctx", "fsdp"), scatter_dimension=0, tiled=True),
    )
    return (
        block_out,
        input_grad,
        summed[0],
        summed[1],
        summed[2],
        summed[3],
        summed[4],
        summed[5],
        summed[6],
        summed[7],
        summed[8],
        summed[9],
        summed[10],
    )


def solution(mesh):
    in_specs = (
        P("fsdp", None, "ctx", None, None),
        P("fsdp", None),
        P("fsdp", None, "ctx", None, None),
        P("fsdp"),
        P("fsdp", None),
        P("fsdp", None),
        P("fsdp", None),
        P("fsdp"),
        P("fsdp"),
        P("fsdp", None),
        P("fsdp"),
        P("fsdp", None),
        P("fsdp", None),
        P("fsdp", None),
    )
    out_specs = (
        P("fsdp", None, "ctx", None, None),
        P("fsdp", None, "ctx", None, None),
        P(("ctx", "fsdp")),
        P(("ctx", "fsdp"), None),
        P(("ctx", "fsdp"), None),
        P(("ctx", "fsdp"), None),
        P(("ctx", "fsdp")),
        P(("ctx", "fsdp")),
        P(("ctx", "fsdp"), None),
        P(("ctx", "fsdp")),
        P(("ctx", "fsdp"), None),
        P(("ctx", "fsdp"), None),
        P(("ctx", "fsdp"), None),
    )
    return jax.shard_map(local, mesh=mesh, in_specs=in_specs, out_specs=out_specs, check_vma=False)
```

profile of v0, /device:TPU:0, one launch (start us, length us, event | category | flops | bytes accessed | tf_op | source)
XLA Modules:
  0.0 4445.0 jit_solution(11172973280617200361)
XLA Ops:
  25.6 67.5 %all-gather.12.cloned.1.call-done = bf16[2048,1024]{1,0:T(8,128)(2,1)} async-done(((bf16[512,1024]{1,0:T(8,128)(2,1)}), bf16[2048,1024]{1,0:T(8,128)(2,1)}) %all-gather.12.cloned.1.call-update) | async-done | bytes 4194320 | tf_op jit(solution)/shard_map/all_gather | solution.py:106
  111.6 62.4 %all-gather.16.cloned.1.call-done = bf16[2048,1024]{1,0:T(8,128)(2,1)} async-done(((bf16[512,1024]{1,0:T(8,128)(2,1)}), bf16[2048,1024]{1,0:T(8,128)(2,1)}) %all-gather.16.cloned.1.call-update) | async-done | bytes 4194320 | tf_op jit(solution)/shard_map/all_gather | solution.py:105
  213.9 19.3 all-gather.18.cloned.1.call-done
  237.0 147.2 %all-gather.20.cloned.1.call-done = bf16[2048,2048]{1,0:T(8,128)(2,1)} async-done(((bf16[512,2048]{1,0:T(8,128)(2,1)}), bf16[2048,2048]{1,0:T(8,128)(2,1)}) %all-gather.20.cloned.1.call-update) | async-done | bytes 8388624 | tf_op jit(solution)/shard_map/all_gather | solution.py:104
  406.0 30.2 while.34
  436.2 97.3 %all-gather.22.cloned.1.call-done = bf16[2048,2048]{1,0:T(8,128)(2,1)} async-done(((bf16[512,2048]{1,0:T(8,128)(2,1)}), bf16[2048,2048]{1,0:T(8,128)(2,1)}) %all-gather.22.cloned.1.call-update) | async-done | bytes 8388624 | tf_op jit(solution)/shard_map/all_gather | solution.py:109
  538.7 419.9 %all-gather.24.cloned.1.call-done = bf16[2048,6144]{1,0:T(8,128)(2,1)} async-done(((bf16[512,6144]{1,0:T(8,128)(2,1)}), bf16[2048,6144]{1,0:T(8,128)(2,1)}) %all-gather.24.cloned.1.call-update) | async-done | bytes 25165840 | tf_op jit(solution)/shard_map/all_gather | solution.py:111
  973.2 410.4 %all-gather.26.cloned.1.call-done = bf16[2048,6144]{1,0:T(8,128)(2,1)} async-done(((bf16[512,6144]{1,0:T(8,128)(2,1)}), bf16[2048,6144]{1,0:T(8,128)(2,1)}) %all-gather.26.cloned.1.call-update) | async-done | bytes 25165840 | tf_op jit(solution)/shard_map/all_gather | solution.py:112
  1398.2 410.4 %all-gather.28.cloned.1.call-done = bf16[6144,2048]{1,0:T(8,128)(2,1)} async-done(((bf16[1536,2048]{1,0:T(8,128)(2,1)}), bf16[6144,2048]{1,0:T(8,128)(2,1)}) %all-gather.28.cloned.1.call-update) | async-done | bytes 25165840 | tf_op jit(solution)/shard_map/all_gather | solution.py:113
  1808.6 16.7 multiply_convert_fusion.1
  1864.7 63.4 %while.35 = (s32[]{:T(128)}, f32[1,128,8,2,128]{1,4,3,2,0:T(8,128)}, bf16[1,1024,8,128]{3,1,2,0:T(8,128)(2,1)}, bf16[1,1024,8,128]{3,1,2,0:T(8,128)(2,1)}, bf16[...) while((s32[]{:T(128)}, ...), condition=%wide.region_13.15_spmd.clone, body=%wide.region_11.14_spmd.clone.sunk | while | flops 338460416 | bytes 10503325 | solution.py:261
  1945.5 30.7 reduce-scatter.10.cloned.1.call-done
  1986.0 35.1 reduce-scatter.12.cloned.1.call-done
  2046.6 21.1 fusion.79
  2067.8 21.1 fusion.80
  2090.4 19.7 fusion.81
  2132.9 42.5 all-reduce.6
  2179.2 31.5 reduce-scatter.16.cloned.1.call-done
  2210.7 186.4 %reduce-scatter.18.cloned.1.call-done = f32[64,1024]{1,0:T(8,128)} async-done(((f32[2048,1024]{1,0:T(8,128)}), f32[64,1024]{1,0:T(8,128)}) %reduce-scatter.18.cloned.1.call-update) | async-done | bytes 262160 | tf_op jit(solution)/shard_map/reduce_scatter | solution.py:309
  2397.1 364.6 %reduce-scatter.14.cloned.1.call-done = f32[64,2048]{1,0:T(8,128)} async-done(((f32[2048,2048]{1,0:T(8,128)}), f32[64,2048]{1,0:T(8,128)}) %reduce-scatter.14.cloned.1.call-update) | async-done | bytes 524304 | tf_op jit(solution)/shard_map/reduce_scatter | solution.py:307
  2761.7 364.9 %reduce-scatter.20.cloned.1.call-done = f32[64,2048]{1,0:T(8,128)} async-done(((f32[2048,2048]{1,0:T(8,128)}), f32[64,2048]{1,0:T(8,128)}) %reduce-scatter.20.cloned.1.call-update) | async-done | bytes 524304 | tf_op jit(solution)/shard_map/reduce_scatter | solution.py:312
  3126.6 436.4 %reduce-scatter.22.cloned.1.call-done = f32[64,6144]{1,0:T(8,128)} async-done(((f32[2048,6144]{1,0:T(8,128)}), f32[64,6144]{1,0:T(8,128)}) %reduce-scatter.22.cloned.1.call-update) | async-done | bytes 1572880 | tf_op jit(solution)/shard_map/reduce_scatter | solution.py:314
  3562.9 437.5 %reduce-scatter.24.cloned.1.call-done = f32[64,6144]{1,0:T(8,128)} async-done(((f32[2048,6144]{1,0:T(8,128)}), f32[64,6144]{1,0:T(8,128)}) %reduce-scatter.24.cloned.1.call-update) | async-done | bytes 1572880 | tf_op jit(solution)/shard_map/reduce_scatter | solution.py:315
  4000.4 437.5 %reduce-scatter.26.cloned.1.call-done = f32[192,2048]{1,0:T(8,128)} async-done(((f32[6144,2048]{1,0:T(8,128)}), f32[192,2048]{1,0:T(8,128)}) %reduce-scatter.26.cloned.1.call-update) | async-done | bytes 1572880 | tf_op jit(solution)/shard_map/reduce_scatter | solution.py:316
  (332 shorter events, 348.5 us)
Async XLA Ops:
  7.2 85.9 %all-gather.12.cloned.1.call-start = ((), (), s32[]{:S(2)}) async-start(), calls=%async_computation.9 | async-start | bytes 5242880 | tf_op jit(solution)/shard_map/all_gather | solution.py:106
  7.9 166.1 %all-gather.16.cloned.1.call-start = ((), (), s32[]{:S(2)}) async-start(), calls=%async_computation.11 | async-start | bytes 5242880 | tf_op jit(solution)/shard_map/all_gather | solution.py:105
  8.7 198.3 %all-gather.14.cloned.1.call-start = ((), (), s32[]{:S(2)}) async-start(), calls=%async_computation.10 | async-start | bytes 2359296 | tf_op jit(solution)/shard_map/all_gather | solution.py:141
  22.9 88.5 %copy-start.19 = (f32[4,1,512]{2,1,0:T(1,128)}, f32[4,1,512]{2,1,0:T(1,128)S(1)}, u32[]{:S(2)}) copy-start(f32[4,1,512]{2,1,0:T(1,128)S(1)} %convert_element_type.190) | copy-start | bytes 24580
  24.3 83.4 %copy-start = (s32[1,1024]{1,0:T(1,128)S(1)}, s32[1,1024]{1,0:T(1,128)}, u32[]{:S(2)}) copy-start(s32[1,1024]{1,0:T(1,128)} %param.21) | copy-start | bytes 12292
  25.6 85.9 %copy-start.3 = (bf16[1,2,1,64,2048]{4,3,2,1,0:T(8,128)(2,1)S(1)}, bf16[1,2,1,64,2048]{4,3,2,1,0:T(8,128)(2,1)}, u32[]{:S(2)}) copy-start(bf16[1,2,1,64,2048]{4,3,2,1,0:T(8,128)(2,1)} %param.20) | copy-start | bytes 1572868
  96.7 136.4 %all-gather.18.cloned.1.call-start = ((), (), s32[]{:S(2)}) async-start(), calls=%async_computation.12 | async-start | bytes 2359296 | tf_op jit(solution)/shard_map/all_gather | solution.py:140
  186.5 197.8 %all-gather.20.cloned.1.call-start = ((), (), s32[]{:S(2)}) async-start(), calls=%async_computation.13 | async-start | bytes 10485760 | tf_op jit(solution)/shard_map/all_gather | solution.py:104
  187.1 346.5 %all-gather.22.cloned.1.call-start = ((), (), s32[]{:S(2)}) async-start(), calls=%async_computation.14 | async-start | bytes 10485760 | tf_op jit(solution)/shard_map/all_gather | solution.py:109
  187.7 771.0 %all-gather.24.cloned.1.call-start = ((), (), s32[]{:S(2)}) async-start(), calls=%async_computation.15 | async-start | bytes 31457280 | tf_op jit(solution)/shard_map/all_gather | solution.py:111
  188.4 1195.2 %all-gather.26.cloned.1.call-start = ((), (), s32[]{:S(2)}) async-start(), calls=%async_computation.16 | async-start | bytes 31457280 | tf_op jit(solution)/shard_map/all_gather | solution.py:112
  189.2 1619.4 %all-gather.28.cloned.1.call-start = ((), (), s32[]{:S(2)}) async-start(), calls=%async_computation.17 | async-start | bytes 31457280 | tf_op jit(solution)/shard_map/all_gather | solution.py:113
  189.9 1786.3 %reduce-scatter.10.cloned.1.call-start = ((), (), s32[]{:S(2)}) async-start(), calls=%async_computation.18 | async-start | bytes 2359296 | tf_op jit(solution)/shard_map/reduce_scatter | solution.py:265
  190.3 213.3 %copy-start.26 = (f32[128]{0:T(128)}, f32[128]{0:T(128)S(1)}, u32[]{:S(2)}) copy-start(f32[128]{0:T(128)S(1)} %convert_element_type.169) | copy-start | bytes 1540
  436.2 97.4 %copy-start.14 = (bf16[1,128,8,2,128]{4,1,3,2,0:T(8,128)(2,1)}, bf16[1,128,8,2,128]{4,1,3,2,0:T(8,128)(2,1)S(1)}, u32[]{:S(2)}) copy-start(bf16[1,128,8,2,128]{4,1,3,2,0:T(8,128)(2,1)S(1)} %get-tuple-element.853) | copy-start | bytes 1572868
  538.5 1316.9 %copy-start.1 = (f32[128,2048]{1,0:T(8,128)}, f32[128,2048]{1,0:T(8,128)S(1)}, u32[]{:S(2)}) copy-start(f32[128,2048]{1,0:T(8,128)S(1)} %get-tuple-element.575) | copy-start | bytes 3145732
  1936.6 84.5 %reduce-scatter.12.cloned.1.call-start = ((), (), s32[]{:S(2)}) async-start(), calls=%async_computation.19 | async-start | bytes 2359296 | tf_op jit(solution)/shard_map/reduce_scatter | solution.py:271
  1945.5 265.3 %reduce-scatter.16.cloned.1.call-start = ((), (), s32[]{:S(2)}) async-start(), calls=%async_computation.21 | async-start | bytes 8650752 | tf_op jit(solution)/shard_map/reduce_scatter | solution.py:308
  1985.9 411.2 %reduce-scatter.18.cloned.1.call-start = ((), (), s32[]{:S(2)}) async-start(), calls=%async_computation.22 | async-start | bytes 8650752 | tf_op jit(solution)/shard_map/reduce_scatter | solution.py:309
  2026.7 735.0 %reduce-scatter.14.cloned.1.call-start = ((), (), s32[]{:S(2)}) async-start(), calls=%async_computation.20 | async-start | bytes 17301504 | tf_op jit(solution)/shard_map/reduce_scatter | solution.py:307
  2037.1 1089.4 %reduce-scatter.20.cloned.1.call-start = ((), (), s32[]{:S(2)}) async-start(), calls=%async_computation.23 | async-start | bytes 17301504 | tf_op jit(solution)/shard_map/reduce_scatter | solution.py:312
  2046.6 1516.4 %reduce-scatter.22.cloned.1.call-start = ((), (), s32[]{:S(2)}) async-start(), calls=%async_computation.24 | async-start | bytes 51904512 | tf_op jit(solution)/shard_map/reduce_scatter | solution.py:314
  2067.7 1932.7 %reduce-scatter.24.cloned.1.call-start = ((), (), s32[]{:S(2)}) async-start(), calls=%async_computation.25 | async-start | bytes 51904512 | tf_op jit(solution)/shard_map/reduce_scatter | solution.py:315
  2088.9 2349.1 %reduce-scatter.26.cloned.1.call-start = ((), (), s32[]{:S(2)}) async-start(), calls=%async_computation.26 | async-start | bytes 51904512 | tf_op jit(solution)/shard_map/reduce_scatter | solution.py:316
  (29 other events, 499.2 us)
Sparse Core Ops, SparseCore 0:
  9.6 83.4 all-gather.11
  94.6 79.3 all-gather.15
  176.5 26.3 all-gather.13
  205.2 27.8 all-gather.17
  234.6 149.6 all-gather.19
  385.7 147.8 all-gather.21
  535.2 423.3 all-gather.23
  960.2 423.3 all-gather.25
  1385.2 423.3 all-gather.27
  1936.7 39.4 reduce-scatter.9
  1979.8 41.2 reduce-scatter.11
  2023.8 186.8 reduce-scatter.15
  2213.6 183.4 reduce-scatter.17
  2399.8 361.8 reduce-scatter.13
  2764.4 362.1 reduce-scatter.19
  3133.4 429.4 reduce-scatter.21
  3569.8 430.6 reduce-scatter.23
  4007.3 430.6 reduce-scatter.25
where the time goes:
time: 4450 us
  waiting for transfers between devices  3960 us (89%)
  matrix products  294 us (7%)
  blocking collectives  77.2 us (2%)
  local copies, waits for them, and re-layouts  71.1 us (2%)
    reduce_scatter x1, waiting for transfers between devices, local(): lax.psum_scatter(grad_down, ('ctx', 'fsdp'), scatter_dimension=0, tiled=T...  438 us
    reduce_scatter x1, waiting for transfers between devices, local(): lax.psum_scatter(grad_up, ('ctx', 'fsdp'), scatter_dimension=0, tiled=True)  437 us
    reduce_scatter x1, waiting for transfers between devices, local(): lax.psum_scatter(grad_gate, ('ctx', 'fsdp'), scatter_dimension=0, tiled=T...  436 us
    all_gather x1, waiting for transfers between devices, local(): lax.all_gather(w_gate, 'fsdp', axis=0, tiled=True)  420 us
    all_gather x1, waiting for transfers between devices, local(): lax.all_gather(w_up, 'fsdp', axis=0, tiled=True)  410 us
    all_gather x1, waiting for transfers between devices, local(): lax.all_gather(w_down, 'fsdp', axis=0, tiled=True)  410 us
    reduce_scatter x1, waiting for transfers between devices, local(): lax.psum_scatter(grad_out, ('ctx', 'fsdp'), scatter_dimension=0, tiled=True)  365 us
    reduce_scatter x1, waiting for transfers between devices, local(): lax.psum_scatter(grad_query, ('ctx', 'fsdp'), scatter_dimension=0, tiled=...  365 us
  transfers between devices with their start and end apart: 18, of which 17 were waited for; matrix products, arithmetic and copies ran while one was open for 6% of the time, Pallas kernels for 0%

commit v1 on v0

v1 whole, which is shorter than its diff:
```python
import functools

import jax
import jax.numpy as jnp
from jax import lax
from jax.experimental import pallas as pl
from jax.experimental.pallas import tpu as pltpu
from jax.sharding import PartitionSpec as P

H = 16
KVH = 8
HD = 128
BLOCK = 64
TILE = 256

epsilon = 1e-06
theta_base = 1000000.0
score_scale = HD ** (-0.5)
low = jnp.bfloat16
high = jnp.float32
vmem_bytes = 48 << 20


def dot(left, right):
    return jnp.dot(left, right, preferred_element_type=high)


def dot_t(left, right):
    return lax.dot_general(left, right, (((1,), (1,)), ((), ())), preferred_element_type=high)


def t_dot(left, right):
    return lax.dot_general(left, right, (((0,), (0,)), ((), ())), preferred_element_type=high)


def mean_last(values):
    return jnp.mean(values, axis=-1, keepdims=True)


def rms_factor(values):
    return lax.rsqrt(mean_last(values * values) + epsilon)


def head_cols(head):
    return slice(head * HD, (head + 1) * HD)


def visible_tile(segc_ref, segr_ref, first, keys):
    rows = lax.broadcasted_iota(jnp.int32, (TILE, keys), 0) + first
    cols = lax.broadcasted_iota(jnp.int32, (TILE, keys), 1)
    same = segc_ref[first : first + TILE, :] == segr_ref[:, :keys]
    return same & (cols <= rows)


def attend_kernel(
    sources_ref,
    places_ref,
    raw_ref,
    cos_ref,
    sin_ref,
    qg_ref,
    kg_ref,
    segc_ref,
    segr_ref,
    rel_ref,
    abs_ref,
    q_ref,
    k_ref,
    v_ref,
    log_ref,
):
    total = q_ref.shape[0]
    heads = q_ref.shape[1] // HD
    blocks = total // BLOCK

    def prepare(index, carry):
        source = pl.multiple_of(sources_ref[index] * BLOCK, BLOCK)
        target = pl.multiple_of(index * BLOCK, BLOCK)
        raw = raw_ref[pl.ds(source, BLOCK), :]
        cosine = cos_ref[pl.ds(target, BLOCK), :]
        sine = sin_ref[pl.ds(target, BLOCK), :]
        for head in range(heads + 1):
            values = raw[:, head_cols(head)]
            gain = qg_ref[...] if head < heads else kg_ref[...]
            normed = values * rms_factor(values) * gain
            turned = (normed * cosine + pltpu.roll(normed, HD // 2, 1) * sine).astype(low)
            if head < heads:
                q_ref[pl.ds(target, BLOCK), head_cols(head)] = turned
            else:
                k_ref[pl.ds(target, BLOCK), :] = turned
        v_ref[pl.ds(target, BLOCK), :] = raw[:, head_cols(heads + 1)].astype(low)
        return carry

    lax.fori_loop(0, blocks, prepare, 0)
    for tile in range(total // TILE):
        first = tile * TILE
        keys = first + TILE
        visible = visible_tile(segc_ref, segr_ref, first, keys)
        for head in range(heads):
            scores = dot_t(q_ref[first : first + TILE, head_cols(head)], k_ref[:keys, :])
            scores = jnp.where(visible, scores * score_scale, -jnp.inf)
            peak = jnp.max(scores, axis=-1, keepdims=True)
            powers = jnp.exp(scores - peak)
            sums = jnp.sum(powers, axis=-1, keepdims=True)
            probs = (powers / sums).astype(low)
            mixed = dot(probs, v_ref[:keys, :]).astype(low)
            log_ref[first : first + TILE, head : head + 1] = peak + jnp.log(sums)
            for part in range(TILE // BLOCK):
                index = first // BLOCK + part
                piece = mixed[part * BLOCK : (part + 1) * BLOCK, :]
                target = pl.multiple_of(sources_ref[index] * BLOCK, BLOCK)
                rel_ref[pl.ds(target, BLOCK), head_cols(head)] = piece
                target = pl.multiple_of(places_ref[index] * BLOCK, BLOCK)
                abs_ref[pl.ds(target, BLOCK), head_cols(head)] = piece


def attend_back_kernel(
    sources_ref,
    places_ref,
    raw_ref,
    cos_ref,
    sin_ref,
    qg_ref,
    kg_ref,
    segc_ref,
    segr_ref,
    q_ref,
    k_ref,
    v_ref,
    log_ref,
    up_ref,
    out_ref,
    gains_ref,
    dq_ref,
    dk_ref,
    dv_ref,
):
    total = q_ref.shape[0]
    heads = q_ref.shape[1] // HD
    blocks = total // BLOCK
    dk_ref[...] = jnp.zeros_like(dk_ref)
    dv_ref[...] = jnp.zeros_like(dv_ref)
    for tile in range(total // TILE):
        first = tile * TILE
        keys = first + TILE
        visible = visible_tile(segc_ref, segr_ref, first, keys)
        for head in range(heads):
            pieces = []
            for part in range(TILE // BLOCK):
                source = pl.multiple_of(places_ref[first // BLOCK + part] * BLOCK, BLOCK)
                pieces.append(up_ref[pl.ds(source, BLOCK), head_cols(head)])
            upstream = jnp.concatenate(pieces, axis=0)
            query = q_ref[first : first + TILE, head_cols(head)]
            key = k_ref[:keys, :]
            scores = dot_t(query, key) * score_scale
            shifted = scores - log_ref[first : first + TILE, head : head + 1]
            probs = jnp.exp(jnp.where(visible, shifted, -jnp.inf))
            dprobs = dot_t(upstream, v_ref[:keys, :])
            inner = jnp.sum(probs * dprobs, axis=-1, keepdims=True)
            dscores = (probs * (dprobs - inner)).astype(low)
            dq_ref[first : first + TILE, head_cols(head)] = dot(dscores, key) * score_scale
            dk_ref[:keys, :] += t_dot(dscores, query) * score_scale
            dv_ref[:keys, :] += t_dot(probs.astype(low), upstream)

    def finish(index, carry):
        target = pl.multiple_of(sources_ref[index] * BLOCK, BLOCK)
        source = pl.multiple_of(index * BLOCK, BLOCK)
        raw = raw_ref[pl.ds(target, BLOCK), :]
        cosine = cos_ref[pl.ds(source, BLOCK), :]
        sine = sin_ref[pl.ds(source, BLOCK), :]
        gains = list(carry)
        for head in range(heads + 1):
            values = raw[:, head_cols(head)]
            if head < heads:
                upstream, gain, slot = dq_ref[pl.ds(source, BLOCK), head_cols(head)], qg_ref[...], 0
            else:
                upstream, gain, slot = dk_ref[pl.ds(source, BLOCK), :], kg_ref[...], 1
            upstream = upstream * cosine - pltpu.roll(upstream, HD // 2, 1) * sine
            factor = rms_factor(values)
            gains[slot] = gains[slot] + jnp.sum(upstream * values * factor, axis=0, keepdims=True)
            scaled = gain * upstream
            inner = mean_last(values * scaled)
            back = factor * scaled - values * (factor * factor * factor) * inner
            out_ref[pl.ds(target, BLOCK), head_cols(head)] = back.astype(low)
        out_ref[pl.ds(target, BLOCK), head_cols(heads + 1)] = dv_ref[pl.ds(source, BLOCK), :].astype(low)
        return tuple(gains)

    zero = jnp.zeros((1, HD), high)
    query_gain, key_gain = lax.fori_loop(0, blocks, finish, (zero, zero))
    gains_ref[0:1, :] = query_gain
    gains_ref[1:2, :] = key_gain


def in_memory(kinds):
    return [pl.BlockSpec(memory_space=kind) for kind in kinds]


def attend(total, heads, *operands):
    shapes = (
        jax.ShapeDtypeStruct((total, heads * HD), low),
        jax.ShapeDtypeStruct((total, heads * HD), low),
        jax.ShapeDtypeStruct((total, heads * HD), low),
        jax.ShapeDtypeStruct((total, HD), low),
        jax.ShapeDtypeStruct((total, HD), low),
        jax.ShapeDtypeStruct((total, HD), high),
    )
    return pl.pallas_call(
        attend_kernel,
        out_shape=shapes,
        in_specs=in_memory([pltpu.SMEM] * 2 + [pltpu.VMEM] * (len(operands) - 2)),
        out_specs=in_memory([pltpu.VMEM] * len(shapes)),
        compiler_params=pltpu.CompilerParams(vmem_limit_bytes=vmem_bytes),
        name="attend",
    )(*operands)


def attend_back(total, heads, *operands):
    shapes = (
        jax.ShapeDtypeStruct((total, (heads + 2) * HD), low),
        jax.ShapeDtypeStruct((2, HD), high),
    )
    return pl.pallas_call(
        attend_back_kernel,
        out_shape=shapes,
        in_specs=in_memory([pltpu.SMEM] * 2 + [pltpu.VMEM] * (len(operands) - 2)),
        out_specs=in_memory([pltpu.VMEM] * len(shapes)),
        scratch_shapes=[
            pltpu.VMEM((total, heads * HD), high),
            pltpu.VMEM((total, HD), high),
            pltpu.VMEM((total, HD), high),
        ],
        compiler_params=pltpu.CompilerParams(vmem_limit_bytes=vmem_bytes),
        name="attend_back",
    )(*operands)


def swap(values, mask):
    size = lax.axis_size("ctx")
    return lax.ppermute(values, "ctx", [(i, i ^ mask) for i in range(size)])


def gather_ctx(values):
    size = lax.axis_size("ctx")
    half = [values] + [swap(values, mask) for mask in range(2, size, 2)]
    half = jnp.concatenate(half, axis=0)
    return jnp.concatenate([half, swap(half, 1)], axis=0)


def scatter_ctx(keep, give):
    size = lax.axis_size("ctx")
    chips = size // 2
    rows = keep.shape[0] // chips
    got = swap(give, 1)
    keep = keep.reshape(chips, rows, -1)
    got = got.reshape(chips, rows, -1)
    sums = [keep[i].astype(high) + got[i].astype(high) for i in range(chips)]
    total = sums[0]
    for i in range(1, chips):
        total = total + swap(sums[i].astype(low), 2 * i).astype(high)
    return total


def halves(values):
    middle = values.shape[0] // 2
    return values[:middle], values[middle:]


def partial_rows(left, right, product):
    keep, give = halves(left)
    give = product(give, right).astype(low)
    keep = product(keep, right).astype(low)
    return scatter_ctx(keep, give)


def columns_of(values, index, width):
    return lax.dynamic_slice_in_dim(values, index * width, width, axis=1)


def gather_rows(values):
    return lax.all_gather(values, "fsdp", axis=0, tiled=True)


def scatter_rows(values):
    return lax.psum_scatter(values.astype(low), "fsdp", scatter_dimension=0, tiled=True)


def local(
    tokens,
    segment_ids,
    cotangent,
    norm_attn,
    w_query,
    w_key,
    w_value,
    q_gain,
    k_gain,
    w_out,
    norm_ffn,
    w_gate,
    w_up,
    w_down,
):
    n = lax.axis_size("ctx")
    m = lax.axis_size("fsdp")
    me = lax.axis_index("ctx")
    layer = lax.axis_index("fsdp")
    width = tokens.shape[-1]
    own = 2 * BLOCK
    total = n * own
    heads = H // n
    repeat = n // KVH
    qw = heads * HD
    hidden = w_gate.shape[1] // n
    piece = hidden // m
    assert tokens.shape[0] == 1 and heads * n == H and repeat * KVH == n

    own_tokens = tokens.reshape(own, width)
    own_cotangent = cotangent.reshape(own, width)
    all_tokens = gather_ctx(own_tokens)

    small = jnp.concatenate([norm_attn, norm_ffn, q_gain, k_gain]).reshape(1, -1)
    small = lax.all_to_all(jnp.broadcast_to(small, (m, small.shape[1])), "fsdp", 0, 0, tiled=True)
    part, gain_part = norm_attn.shape[0], q_gain.shape[0]
    small = small.astype(high)
    gain_attn = small[:, :part].reshape(-1)
    gain_ffn = small[:, part : 2 * part].reshape(-1)
    query_gain = small[:, 2 * part : 2 * part + gain_part].reshape(1, HD)
    key_gain = small[:, 2 * part + gain_part :].reshape(1, HD)

    qkv_w = gather_rows(
        jnp.concatenate(
            [
                columns_of(w_query, me, qw),
                columns_of(w_key, me // repeat, HD),
                columns_of(w_value, me // repeat, HD),
            ],
            axis=1,
        )
    )
    out_cols = width // n
    out_w = gather_rows(columns_of(w_out, me, out_cols))

    def hidden_columns(weights):
        starts = [i * n * piece + me * piece for i in range(m)]
        return [lax.dynamic_slice_in_dim(weights, start, piece, axis=1) for start in starts]

    gate_up_w = gather_rows(jnp.concatenate(hidden_columns(w_gate) + hidden_columns(w_up), axis=1))
    down_w = gather_rows(lax.dynamic_slice_in_dim(w_down, me * piece, piece, axis=0))

    def slot_of(owner):
        mask = owner ^ me
        return (mask >> 1) + (mask & 1) * (n // 2)

    out_w = gather_ctx(out_w).reshape(n, -1, out_cols)

    natural = jnp.arange(2 * n, dtype=jnp.int32)
    side = (natural >= n).astype(jnp.int32)
    owner = jnp.where(side == 0, natural, 2 * n - 1 - natural)
    sources = 2 * slot_of(owner) + side
    places = 2 * owner + side

    segments = segment_ids.reshape(total)
    starts = jnp.sum((segments[None, :] < segments[:, None]).astype(jnp.int32), axis=1)
    place = jnp.arange(total, dtype=jnp.int32) - starts
    frequency = theta_base ** (-(jnp.arange(HD // 2, dtype=high) * 2.0) / HD)
    angles = place.astype(high)[:, None] * frequency
    cosine = jnp.cos(angles)
    sine = jnp.sin(angles)
    cosine = jnp.concatenate([cosine, cosine], axis=1)
    sine = jnp.concatenate([-sine, sine], axis=1)
    segment_column = segments.reshape(total, 1)
    segment_row = segments.reshape(1, total)

    features = all_tokens.astype(high)
    normed_low = (features * rms_factor(features) * gain_attn).astype(low)
    qkv_raw = dot(normed_low, qkv_w)
    tables = (cosine, sine, query_gain, key_gain, segment_column, segment_row)
    mixed_rel, mixed_abs, query, key, value, logs = attend(
        total, heads, sources, places, qkv_raw, *tables
    )
    mixed = lax.all_to_all(mixed_abs.reshape(n, own, qw), "ctx", 0, 0, tiled=True)
    mixed = mixed.transpose(1, 0, 2).reshape(own, n * qw)
    own_features = own_tokens.astype(high)
    branch = [dot(mixed, out_w[i]) for i in range(n)]
    branch = jnp.stack(branch)
    branch = [lax.dynamic_index_in_dim(branch, slot_of(i), axis=0, keepdims=False) for i in range(n)]
    middle = own_features + jnp.concatenate(branch, axis=1)
    factor_ffn = rms_factor(middle)
    ffn_low = gather_ctx((middle * factor_ffn * gain_ffn).astype(low))
    upstream_low = gather_ctx(own_cotangent)

    gate_up = dot(ffn_low, gate_up_w)
    gate, up = gate_up[:, :hidden], gate_up[:, hidden:]
    sigmoid = jax.nn.sigmoid(gate)
    silu = gate * sigmoid
    hidden_low = (silu * up).astype(low)
    block_sum = middle + partial_rows(hidden_low, down_w, dot)
    block_out = block_sum.astype(low).reshape(tokens.shape)

    grad_hidden = dot_t(upstream_low, down_w)
    slope = sigmoid * (1.0 + gate * (1.0 - sigmoid))
    gate_up_grad = jnp.concatenate(
        [(grad_hidden * up * slope).astype(low), (grad_hidden * silu).astype(low)], axis=1
    )
    grad_ffn = partial_rows(gate_up_grad, gate_up_w, dot_t)
    upstream = own_cotangent.astype(high)
    scaled = gain_ffn * grad_ffn
    inner = mean_last(middle * scaled)
    grad_middle = upstream + factor_ffn * scaled - middle * factor_ffn**3 * inner
    grad_gain_ffn = jnp.sum(grad_ffn * middle * factor_ffn, axis=0)
    middle_low = grad_middle.astype(low)

    mixed_grad = 0.0
    for mask in range(n):
        slot = (mask >> 1) + (mask & 1) * (n // 2)
        mixed_grad = mixed_grad + dot_t(columns_of(middle_low, me ^ mask, out_cols), out_w[slot])
    mixed_grad = mixed_grad.astype(low).reshape(own, n, qw).transpose(1, 0, 2)
    mixed_grad = lax.all_to_all(mixed_grad, "ctx", 0, 0, tiled=True).reshape(total, qw)
    qkv_grad, grad_gains = attend_back(
        total, heads, sources, places, qkv_raw, *tables, query, key, value, logs, mixed_grad
    )
    grad_attn = partial_rows(qkv_grad, qkv_w, dot_t)
    factor_attn = rms_factor(own_features)
    scaled = gain_attn * grad_attn
    inner = mean_last(own_features * scaled)
    input_grad = grad_middle + factor_attn * scaled - own_features * factor_attn**3 * inner
    grad_gain_attn = jnp.sum(grad_attn * own_features * factor_attn, axis=0)
    input_grad = input_grad.reshape(tokens.shape)

    strip = width // (n * m)

    def grad_rows(left, right):
        grads = t_dot(left, right).astype(low).reshape(n, m, strip, right.shape[1])
        grads = grads.transpose(1, 0, 2, 3).reshape(width, right.shape[1])
        grads = scatter_rows(grads).reshape(n, strip, right.shape[1])
        return lax.all_to_all(grads, "ctx", 0, 0, tiled=True).astype(high)

    grad_down = scatter_rows(t_dot(hidden_low, upstream_low))
    targets = []
    for device in range(n * m):
        block = (device % m) * n + device // m
        targets.append((device, block))
    grad_down = lax.ppermute(grad_down, ("ctx", "fsdp"), targets).astype(high)
    grad_gate_up = grad_rows(ffn_low, gate_up_grad).reshape(n, strip, 2, m, piece)
    grad_gate_up = grad_gate_up.transpose(2, 1, 3, 0, 4).reshape(2, strip, -1)
    grad_out = scatter_rows(t_dot(mixed_rel, gather_ctx(middle_low))).astype(high)
    grad_qkv = grad_rows(normed_low, qkv_grad)
    grad_query = grad_qkv[:, :, :qw].transpose(1, 0, 2).reshape(strip, -1)

    def grad_of_kv(grads):
        grads = jnp.sum(grads.reshape(KVH, repeat, strip, HD), axis=1)
        return grads.transpose(1, 0, 2).reshape(strip, -1)

    grad_key = grad_of_kv(grad_qkv[:, :, qw : qw + HD])
    grad_value = grad_of_kv(grad_qkv[:, :, qw + HD :])

    devices = n * m
    partial = jnp.concatenate(
        [
            grad_gain_attn.reshape(devices, -1),
            grad_gain_ffn.reshape(devices, -1),
            grad_gains[0].reshape(devices, -1),
            grad_gains[1].reshape(devices, -1),
        ],
        axis=1,
    )
    gains = jnp.sum(lax.all_to_all(partial, ("ctx", "fsdp"), 0, 0, tiled=True), axis=0)
    end = 2 * strip + HD // devices
    return (
        block_out,
        input_grad,
        gains[:strip],
        grad_query,
        grad_key,
        grad_value,
        gains[2 * strip : end],
        gains[end:],
        grad_out,
        gains[strip : 2 * strip],
        grad_gate_up[0],
        grad_gate_up[1],
        grad_down,
    )


def solution(mesh):
    rows = P("fsdp", None)
    line = P("fsdp")
    blocks = P("fsdp", None, "ctx", None, None)
    both = P(("ctx", "fsdp"), None)
    both_line = P(("ctx", "fsdp"))
    in_specs = (blocks, rows, blocks, line, rows, rows, rows, line, line, rows, line, rows, rows, rows)
    out_specs = (
        blocks,
        blocks,
        both_line,
        both,
        both,
        both,
        both_line,
        both_line,
        both,
        both_line,
        both,
        both,
        both,
    )
    return jax.shard_map(local, mesh=mesh, in_specs=in_specs, out_specs=out_specs, check_vma=False)
```

time: 4450 us -> 710 us (0.16)
  waiting for transfers between devices: 3960 us -> 360 us
  matrix products: 294 us -> 96.1 us
  starting transfers between devices: 1.11 us -> 57.9 us
  blocking collectives: 77.2 us -> 22.6 us
    reduce_scatter x9 -> x4, waiting for transfers between devices: 2320 us -> 164 us  [scatter_rows(): lax.psum_scatter(values.astype(low), 'fsdp', scatter_dimension=0, tiled=T...]
    all_gather x9 -> x4, waiting for transfers between devices: 1630 us -> 48.2 us  [gather_rows(): return lax.all_gather(values, 'fsdp', axis=0, tiled=True)]
    dot_general x77 -> x29, matrix products: 294 us -> 96.1 us  [the longest x13 37.9 us: dot_t(): lax.dot_general(left, right, (((1,), (1,)), ((), ())), preferred_element_...]
    ppermute x0 -> x33, waiting for transfers between devices: none -> 143 us  [the longest x32 143 us: swap(): return lax.ppermute(values, 'ctx', [(i, i ^ mask) for i in range(size)])]
    unnamed x2 -> x0, blocking collectives: 51.6 us -> none
  transfers between devices with their start and end apart: 18 -> 45, of which waited for: 17 -> 18; matrix products, arithmetic and copies ran while one was open for 6% -> 23% of each run, Pallas kernels for 0% -> 1%
where the time goes in v1:
time: 710 us; the launch traced here: 698 us
  waiting for transfers between devices  360 us (51%)
  matrix products  96.1 us (14%)
  local copies, waits for them, and re-layouts  81.2 us (11%)
  starting transfers between devices  57.9 us (8%)
  other arithmetic  44.9 us (6%)
  blocking collectives  22.6 us (3%)
  Pallas kernels  19.5 us (3%)
  between operations  15.4 us (2%)
    reduce_scatter x4, waiting for transfers between devices, scatter_rows(): lax.psum_scatter(values.astype(low), 'fsdp', scatter_dimension=0, tiled=T...  164 us
    ppermute x32, waiting for transfers between devices, swap(): return lax.ppermute(values, 'ctx', [(i, i ^ mask) for i in range(size)])  143 us
    all_gather x4, waiting for transfers between devices, gather_rows(): return lax.all_gather(values, 'fsdp', axis=0, tiled=True)  48.2 us
    dot_general x13, matrix products, dot_t(): lax.dot_general(left, right, (((1,), (1,)), ((), ())), preferred_element_...  37.9 us
    dot_general x12, matrix products, dot(): return jnp.dot(left, right, preferred_element_type=high)  36.2 us
    ppermute x32, starting transfers between devices, swap(): return lax.ppermute(values, 'ctx', [(i, i ^ mask) for i in range(size)])  34.1 us
    unnamed x108, local copies, waits for them, and re-layouts  28.5 us
    dot_general x4, matrix products, t_dot(): lax.dot_general(left, right, (((0,), (0,)), ((), ())), preferred_element_...  21.9 us
  transfers between devices with their start and end apart: 45, of which 18 were waited for; matrix products, arithmetic and copies ran while one was open for 23% of the time, Pallas kernels for 1%

profile of v1, /device:TPU:0, one launch (start us, length us, event | category | flops | bytes accessed | tf_op | source)
XLA Modules:
  0.0 697.6 jit_solution(5728208041415002868)
XLA Ops:
  32.4 8.8 %all-gather.7.cloned.1.call-done = bf16[2048,256]{1,0:T(8,128)(2,1)} async-done(((bf16[512,256]{1,0:T(8,128)(2,1)}), bf16[2048,256]{1,0:T(8,128)(2,1)}) %all-gather.7.cloned.1.call-update) | async-done | bytes 1048592 | tf_op jit(solution)/shard_map/all_gather | solution.py:280
  51.2 51.0 %collective-permute-done.2 = bf16[128,2048]{1,0:T(8,128)(2,1)} collective-permute-done((bf16[128,2048]{1,0:T(8,128)(2,1)S(1)}, bf16[128,2048]{1,0:T(8,128)(2,1)}, u32[]{:S(2)}, u32[]{:S(2)}) %collective-permute-start.2) | collective-permute-done | bytes 524320 | tf_op jit(solution)/shard_map/ppermute | solution.py:239
  130.2 8.8 %attend.1 = (bf16[1024,256]{1,0:T(8,128)(2,1)S(1)}, bf16[1024,256]{1,0:T(8,128)(2,1)S(1)}, bf16[1024,256]{1,0:T(8,128)(2,1)S(1)}, bf16[1024,128]{1,0:T(8,128)(2,...) custom-call(s32[16]{0:T(128)S(1)} %get-tuple-element.162.sources_ref, ...), custom_call_target="tpu_custom_call" | custom-call | tf_op jit(solution)/shard_map/attend/pallas_call | solution.py:207
  181.6 9.5 %collective-permute-done.8 = bf16[128,2048]{1,0:T(8,128)(2,1)} collective-permute-done((bf16[128,2048]{1,0:T(8,128)(2,1)}, bf16[128,2048]{1,0:T(8,128)(2,1)}, u32[]{:S(2)}, u32[]{:S(2)}) %collective-permute-start.8) | collective-permute-done | bytes 524320 | tf_op jit(solution)/shard_map/ppermute | solution.py:239
  191.2 10.6 %collective-permute-done.9 = bf16[128,2048]{1,0:T(8,128)(2,1)} collective-permute-done((bf16[128,2048]{1,0:T(8,128)(2,1)}, bf16[128,2048]{1,0:T(8,128)(2,1)}, u32[]{:S(2)}, u32[]{:S(2)}) %collective-permute-start.9) | collective-permute-done | bytes 524320 | tf_op jit(solution)/shard_map/ppermute | solution.py:239
  217.4 11.7 %fusion.77 = f32[1024,1536]{1,0:T(8,128)} fusion(bf16[1024,2048]{1,0:T(8,128)(2,1)} %constant_dynamic-update-slice_fusion.13, bf16[2048,1536]{1,0:T(8,128)(2,1)} %all-gather.9.cloned.1.call-done), kind=kOutput, calls=%fused_computation.218 | convolution fusion | flops 6442450944 | bytes 16777216 | tf_op jit(solution)/shard_map/dot_general | solution.py:25
  229.2 39.4 %all-gather.11.cloned.1.call-done = bf16[768,2048]{1,0:T(8,128)(2,1)} async-done(((bf16[192,2048]{1,0:T(8,128)(2,1)}), bf16[768,2048]{1,0:T(8,128)(2,1)}) %all-gather.11.cloned.1.call-update) | async-done | bytes 3145744 | tf_op jit(solution)/shard_map/all_gather | solution.py:280
  268.6 9.5 %multiply_convert_fusion = (bf16[1024,768]{1,0:T(8,128)(2,1)S(1)}, bf16[1024,768]{1,0:T(8,128)(2,1)S(1)}, bf16[1024,768]{1,0:T(8,128)(2,1)S(1)}) fusion(f32[1024,1536]{1,0:T(8,128)} %fusion.77, bf16[1024,2048]{1,0:T(8,128)(2,1)} %copy-done.25, bf16[768,2048]{1,0:T(8,128)(2,1)} %all-gather.11.cloned.1.call-done), kind=kOutput, calls=%fused_computation.14 | convolution fusion | flops 3233021952 | bytes 18350080 | tf_op jit(solution)/shard_map/dot_general | solution.py:29
  312.9 9.8 %collective-permute-done.22 = bf16[128,2048]{1,0:T(8,128)(2,1)S(1)} collective-permute-done((bf16[128,2048]{1,0:T(8,128)(2,1)S(1)}, bf16[128,2048]{1,0:T(8,128)(2,1)S(1)}, u32[]{:S(2)}, u32[]{:S(2)}) %collective-permute-start.22) | collective-permute-done | bytes 524320 | tf_op jit(solution)/shard_map/ppermute | solution.py:239
  324.8 9.2 %collective-permute-done.15 = bf16[128,2048]{1,0:T(8,128)(2,1)S(1)} collective-permute-done((bf16[128,2048]{1,0:T(8,128)(2,1)S(1)}, bf16[128,2048]{1,0:T(8,128)(2,1)S(1)}, u32[]{:S(2)}, u32[]{:S(2)}) %collective-permute-start.15) | collective-permute-done | bytes 524320 | tf_op jit(solution)/shard_map/ppermute | solution.py:239
  334.0 10.2 %collective-permute-done.14 = bf16[128,2048]{1,0:T(8,128)(2,1)S(1)} collective-permute-done((bf16[128,2048]{1,0:T(8,128)(2,1)S(1)}, bf16[128,2048]{1,0:T(8,128)(2,1)S(1)}, u32[]{:S(2)}, u32[]{:S(2)}) %collective-permute-start.14) | collective-permute-done | bytes 524320 | tf_op jit(solution)/shard_map/ppermute | solution.py:239
  361.4 12.9 %all_to_all.35 = bf16[8,128,256]{2,1,0:T(8,128)(2,1)S(1)} all-to-all(bf16[8,128,256]{2,1,0:T(8,128)(2,1)S(1)} %bitcast.189), channel_id=1, replica_groups=mesh['ctx'=8,'fsdp'=4] {'ctx'}, dimensions={0} | all-to-all | bytes 1048576 | tf_op jit(solution)/shard_map/all_to_all | solution.py:418
  374.3 10.7 %attend_back.1 = (bf16[1024,512]{1,0:T(8,128)(2,1)S(1)}, f32[2,128]{1,0:T(2,128)S(1)}) custom-call(s32[16]{0:T(128)S(1)} %get-tuple-element.162.sources_ref, s32[16]{0:T(128)S(1)} %get-tuple-element.161.places_ref, f32[1024,512]{1,0:T(8,128)} %fusion.15.raw_ref, f32[1024,128]{1,0:T(8,128)S(1)} %get-tuple-element.165.cos_ref, ...), custom_call_target="tpu_custom_call" | custom-call | tf_op jit(solution)/shard_map/attend_back/pallas_call | solution.py:222
  389.8 7.0 %convolution_convert_fusion.1 = bf16[768,2048]{1,0:T(8,128)(2,1)} fusion(bf16[1024,768]{1,0:T(8,128)(2,1)S(1)} %copy-done.33, bf16[1024,2048]{1,0:T(8,128)(2,1)} %copy-done.25), kind=kOutput, calls=%fused_computation.13 | convolution fusion | flops 3222798336 | bytes 8912896 | tf_op jit(solution)/shard_map/dot_general | solution.py:33
  396.9 10.0 %convolution_convert_fusion = bf16[2048,1536]{1,0:T(8,128)(2,1)S(1)} fusion(bf16[1024,2048]{1,0:T(8,128)(2,1)} %constant_dynamic-update-slice_fusion.13, bf16[1024,768]{1,0:T(8,128)(2,1)} %copy-done.34, bf16[1024,768]{1,0:T(8,128)(2,1)} %copy-done.35), kind=kOutput, calls=%fused_computation.5 | convolution fusion | flops 6451888128 | bytes 13631488 | tf_op jit(solution)/shard_map/dot_general | solution.py:33
  417.7 8.4 %collective-permute-done.28 = bf16[128,2048]{1,0:T(8,128)(2,1)S(1)} collective-permute-done((bf16[128,2048]{1,0:T(8,128)(2,1)S(1)}, bf16[128,2048]{1,0:T(8,128)(2,1)S(1)}, u32[]{:S(2)}, u32[]{:S(2)}) %collective-permute-start.28) | collective-permute-done | bytes 524320 | tf_op jit(solution)/shard_map/ppermute | solution.py:239
  426.1 10.4 %collective-permute-done.29 = bf16[128,2048]{1,0:T(8,128)(2,1)S(1)} collective-permute-done((bf16[128,2048]{1,0:T(8,128)(2,1)S(1)}, bf16[128,2048]{1,0:T(8,128)(2,1)S(1)}, u32[]{:S(2)}, u32[]{:S(2)}) %collective-permute-start.29) | collective-permute-done | bytes 524320 | tf_op jit(solution)/shard_map/ppermute | solution.py:239
  448.4 9.6 %collective-permute-done.27 = bf16[128,2048]{1,0:T(8,128)(2,1)S(1)} collective-permute-done((bf16[128,2048]{1,0:T(8,128)(2,1)}, bf16[128,2048]{1,0:T(8,128)(2,1)S(1)}, u32[]{:S(2)}, u32[]{:S(2)}) %collective-permute-start.27) | collective-permute-done | bytes 524320 | tf_op jit(solution)/shard_map/ppermute | solution.py:239
  458.0 8.4 %collective-permute-done.26 = bf16[128,2048]{1,0:T(8,128)(2,1)S(1)} collective-permute-done((bf16[128,2048]{1,0:T(8,128)(2,1)}, bf16[128,2048]{1,0:T(8,128)(2,1)S(1)}, u32[]{:S(2)}, u32[]{:S(2)}) %collective-permute-start.26) | collective-permute-done | bytes 524320 | tf_op jit(solution)/shard_map/ppermute | solution.py:239
  469.4 9.7 %all_to_all.36 = f32[32,1,136]{2,1,0:T(1,128)S(1)} all-to-all(f32[32,1,136]{2,1,0:T(1,128)S(1)} %all_to_all.25), channel_id=1, replica_groups=mesh['ctx'=8,'fsdp'=4] {'ctx','fsdp'}, dimensions={0} | all-to-all | bytes 34816 | tf_op jit(solution)/shard_map/all_to_all | solution.py:467
  482.6 9.8 %reduce-scatter.11.cloned.1.call-done = bf16[192,2048]{1,0:T(8,128)(2,1)} async-done(((bf16[768,2048]{1,0:T(8,128)(2,1)}), bf16[192,2048]{1,0:T(8,128)(2,1)}) %reduce-scatter.11.cloned.1.call-update) | async-done | bytes 786448 | tf_op jit(solution)/shard_map/reduce_scatter | solution.py:284
  492.4 7.4 %collective-permute-start.32 = (bf16[192,2048]{1,0:T(8,128)(2,1)}, bf16[192,2048]{1,0:T(8,128)(2,1)}, u32[]{:S(2)}, u32[]{:S(2)}) collective-permute-start(bf16[192,2048]{1,0:T(8,128)(2,1)} %reduce-scatter.11.cloned.1.call-done), channel_id=1, source_target_pairs={{0,0},{1,8},{2,16},{3,24},{4,1},{5,9},{6,17},{7,25},{8,2},{9,10},{... | collective-permute-start | bytes 2359304 | tf_op jit(solution)/shard_map/ppermute | solution.py:443
  499.9 127.2 %reduce-scatter.9.cloned.1.call-done = bf16[512,1536]{1,0:T(8,128)(2,1)} async-done(((bf16[2048,1536]{1,0:T(8,128)(2,1)}), bf16[512,1536]{1,0:T(8,128)(2,1)}) %reduce-scatter.9.cloned.1.call-update) | async-done | bytes 1572880 | tf_op jit(solution)/shard_map/reduce_scatter | solution.py:284
  637.1 26.5 %reduce-scatter.7.cloned.1.call-done = bf16[64,2048]{1,0:T(8,128)(2,1)} async-done(((bf16[256,2048]{1,0:T(8,128)(2,1)}), bf16[64,2048]{1,0:T(8,128)(2,1)}) %reduce-scatter.7.cloned.1.call-update) | async-done | bytes 262160 | tf_op jit(solution)/shard_map/reduce_scatter | solution.py:284
  (293 shorter events, 245.6 us)
Async XLA Ops:
  7.2 33.9 %all-gather.7.cloned.1.call-start = ((), (), s32[]{:S(2)}) async-start(), calls=%async_computation.11 | async-start | bytes 1310720 | tf_op jit(solution)/shard_map/all_gather | solution.py:280
  9.5 113.9 %all-gather.5.cloned.1.call-start = ((), (), s32[]{:S(2)}) async-start(), calls=%async_computation.10 | async-start | bytes 2621440 | tf_op jit(solution)/shard_map/all_gather | solution.py:280
  12.4 32.2 %collective-permute-start = (bf16[128,2048]{1,0:T(8,128)(2,1)}, bf16[128,2048]{1,0:T(8,128)(2,1)S(1)}, u32[]{:S(2)}, u32[]{:S(2)}) collective-permute-start(bf16[128,2048]{1,0:T(8,128)(2,1)} %bitcast.178), channel_id=1, source_target_pairs={{0,8},{4,12},{8,0},{12,4},{16,24},{20,28},{24,16},{28,20},{1,9},{5... | collective-permute-start | bytes 1572872 | tf_op jit(solution)/shard_map/ppermute | solution.py:239
  15.4 35.1 %collective-permute-start.1 = (bf16[128,2048]{1,0:T(8,128)(2,1)}, bf16[128,2048]{1,0:T(8,128)(2,1)}, u32[]{:S(2)}, u32[]{:S(2)}) collective-permute-start(bf16[128,2048]{1,0:T(8,128)(2,1)} %bitcast.179), channel_id=1, source_target_pairs={{0,16},{4,20},{8,24},{12,28},{16,0},{20,4},{24,8},{28,12},{1,17},{... | collective-permute-start | bytes 1572872 | tf_op jit(solution)/shard_map/ppermute | solution.py:239
  26.6 190.9 %all-gather.9.cloned.1.call-start = ((), (), s32[]{:S(2)}) async-start(), calls=%async_computation.12 | async-start | bytes 7864320 | tf_op jit(solution)/shard_map/all_gather | solution.py:280
  41.1 64.6 %collective-permute-start.4 = (bf16[2048,256]{1,0:T(8,128)(2,1)}, bf16[2048,256]{1,0:T(8,128)(2,1)}, u32[]{:S(2)}, u32[]{:S(2)}) collective-permute-start(bf16[2048,256]{1,0:T(8,128)(2,1)} %all-gather.7.cloned.1.call-done), channel_id=1, source_target_pairs={{0,8},{4,12},{8,0},{12,4},{16,24},{20,28},{24,16},{28,20},{1,9},{5... | collective-permute-start | bytes 3145736 | tf_op jit(solution)/shard_map/ppermute | solution.py:239
  42.6 65.5 %collective-permute-start.5 = (bf16[2048,256]{1,0:T(8,128)(2,1)}, bf16[2048,256]{1,0:T(8,128)(2,1)}, u32[]{:S(2)}, u32[]{:S(2)}) collective-permute-start(bf16[2048,256]{1,0:T(8,128)(2,1)} %all-gather.7.cloned.1.call-done), channel_id=1, source_target_pairs={{0,16},{4,20},{8,24},{12,28},{16,0},{20,4},{24,8},{28,12},{1,17},{... | collective-permute-start | bytes 3145736 | tf_op jit(solution)/shard_map/ppermute | solution.py:239
  44.1 64.0 %collective-permute-start.6 = (bf16[2048,256]{1,0:T(8,128)(2,1)}, bf16[2048,256]{1,0:T(8,128)(2,1)}, u32[]{:S(2)}, u32[]{:S(2)}) collective-permute-start(bf16[2048,256]{1,0:T(8,128)(2,1)} %all-gather.7.cloned.1.call-done), channel_id=1, source_target_pairs={{0,24},{4,28},{8,16},{12,20},{16,8},{20,12},{24,0},{28,4},{1,25},{... | collective-permute-start | bytes 3145736 | tf_op jit(solution)/shard_map/ppermute | solution.py:239
  44.6 57.5 %collective-permute-start.2 = (bf16[128,2048]{1,0:T(8,128)(2,1)S(1)}, bf16[128,2048]{1,0:T(8,128)(2,1)}, u32[]{:S(2)}, u32[]{:S(2)}) collective-permute-start(bf16[128,2048]{1,0:T(8,128)(2,1)S(1)} %bitcast.180), channel_id=1, source_target_pairs={{0,24},{4,28},{8,16},{12,20},{16,8},{20,12},{24,0},{28,4},{1,25},{... | collective-permute-start | bytes 1572872 | tf_op jit(solution)/shard_map/ppermute | solution.py:239
  50.5 95.0 %collective-permute-start.16 = (bf16[128,2048]{1,0:T(8,128)(2,1)}, bf16[128,2048]{1,0:T(8,128)(2,1)}, u32[]{:S(2)}, u32[]{:S(2)}) collective-permute-start(bf16[128,2048]{1,0:T(8,128)(2,1)} %bitcast.33), channel_id=1, source_target_pairs={{0,8},{4,12},{8,0},{12,4},{16,24},{20,28},{24,16},{28,20},{1,9},{5... | collective-permute-start | bytes 1572872 | tf_op jit(solution)/shard_map/ppermute | solution.py:239
  102.2 43.4 %collective-permute-start.17 = (bf16[128,2048]{1,0:T(8,128)(2,1)}, bf16[128,2048]{1,0:T(8,128)(2,1)}, u32[]{:S(2)}, u32[]{:S(2)}) collective-permute-start(bf16[128,2048]{1,0:T(8,128)(2,1)} %bitcast.33), channel_id=1, source_target_pairs={{0,16},{4,20},{8,24},{12,28},{16,0},{20,4},{24,8},{28,12},{1,17},{... | collective-permute-start | bytes 1572872 | tf_op jit(solution)/shard_map/ppermute | solution.py:239
  105.8 39.8 %collective-permute-start.18 = (bf16[128,2048]{1,0:T(8,128)(2,1)}, bf16[128,2048]{1,0:T(8,128)(2,1)}, u32[]{:S(2)}, u32[]{:S(2)}) collective-permute-start(bf16[128,2048]{1,0:T(8,128)(2,1)} %bitcast.33), channel_id=1, source_target_pairs={{0,24},{4,28},{8,16},{12,20},{16,8},{20,12},{24,0},{28,4},{1,25},{... | collective-permute-start | bytes 1572872 | tf_op jit(solution)/shard_map/ppermute | solution.py:239
  111.7 49.4 %collective-permute-start.7 = (bf16[8192,256]{1,0:T(8,128)(2,1)}, bf16[8192,256]{1,0:T(8,128)(2,1)}, u32[]{:S(2)}, u32[]{:S(2)}) collective-permute-start(bf16[8192,256]{1,0:T(8,128)(2,1)} %pad_maximum_fusion), channel_id=1, source_target_pairs={{0,4},{4,0},{8,12},{12,8},{16,20},{20,16},{24,28},{28,24},{1,5},{5... | collective-permute-start | bytes 12582920 | tf_op jit(solution)/shard_map/ppermute | solution.py:239
  145.0 123.6 %all-gather.11.cloned.1.call-start = ((), (), s32[]{:S(2)}) async-start(), calls=%async_computation.13 | async-start | bytes 3932160 | tf_op jit(solution)/shard_map/all_gather | solution.py:280
  148.8 59.1 %collective-permute-start.19 = (bf16[512,2048]{1,0:T(8,128)(2,1)}, bf16[512,2048]{1,0:T(8,128)(2,1)}, u32[]{:S(2)}, u32[]{:S(2)}) collective-permute-start(bf16[512,2048]{1,0:T(8,128)(2,1)} %pad_maximum_fusion.5), channel_id=1, source_target_pairs={{0,4},{4,0},{8,12},{12,8},{16,20},{20,16},{24,28},{28,24},{1,5},{5... | collective-permute-start | bytes 6291464 | tf_op jit(solution)/shard_map/ppermute | solution.py:239
  181.6 297.5 %reduce-scatter.5.cloned.1.call-start = ((), (), s32[]{:S(2)}) async-start(), calls=%async_computation.14 | async-start | bytes 2621440 | tf_op jit(solution)/shard_map/reduce_scatter | solution.py:284
  303.0 31.0 %collective-permute-start.15 = (bf16[128,2048]{1,0:T(8,128)(2,1)S(1)}, bf16[128,2048]{1,0:T(8,128)(2,1)S(1)}, u32[]{:S(2)}, u32[]{:S(2)}) collective-permute-start(bf16[128,2048]{1,0:T(8,128)(2,1)S(1)} %get-tuple-element.142), channel_id=1, source_target_pairs={{0,24},{4,28},{8,16},{12,20},{16,8},{20,12},{24,0},{28,4},{1,25},{... | collective-permute-start | bytes 1572872 | tf_op jit(solution)/shard_map/ppermute | solution.py:239
  305.4 38.8 %collective-permute-start.14 = (bf16[128,2048]{1,0:T(8,128)(2,1)S(1)}, bf16[128,2048]{1,0:T(8,128)(2,1)S(1)}, u32[]{:S(2)}, u32[]{:S(2)}) collective-permute-start(bf16[128,2048]{1,0:T(8,128)(2,1)S(1)} %get-tuple-element.143), channel_id=1, source_target_pairs={{0,16},{4,20},{8,24},{12,28},{16,0},{20,4},{24,8},{28,12},{1,17},{... | collective-permute-start | bytes 1572872 | tf_op jit(solution)/shard_map/ppermute | solution.py:239
  311.4 32.9 %collective-permute-start.13 = (bf16[128,2048]{1,0:T(8,128)(2,1)S(1)}, bf16[128,2048]{1,0:T(8,128)(2,1)S(1)}, u32[]{:S(2)}, u32[]{:S(2)}) collective-permute-start(bf16[128,2048]{1,0:T(8,128)(2,1)S(1)} %get-tuple-element.141), channel_id=1, source_target_pairs={{0,8},{4,12},{8,0},{12,4},{16,24},{20,28},{24,16},{28,20},{1,9},{5... | collective-permute-start | bytes 1572872 | tf_op jit(solution)/shard_map/ppermute | solution.py:239
  389.2 103.2 %reduce-scatter.11.cloned.1.call-start = ((), (), s32[]{:S(2)}) async-start(), calls=%async_computation.17 | async-start | bytes 3932160 | tf_op jit(solution)/shard_map/reduce_scatter | solution.py:284
  396.9 230.2 %reduce-scatter.9.cloned.1.call-start = ((), (), s32[]{:S(2)}) async-start(), calls=%async_computation.16 | async-start | bytes 7864320 | tf_op jit(solution)/shard_map/reduce_scatter | solution.py:284
  410.2 253.4 %reduce-scatter.7.cloned.1.call-start = ((), (), s32[]{:S(2)}) async-start(), calls=%async_computation.15 | async-start | bytes 1310720 | tf_op jit(solution)/shard_map/reduce_scatter | solution.py:284
  492.4 142.2 %collective-permute-start.32 = (bf16[192,2048]{1,0:T(8,128)(2,1)}, bf16[192,2048]{1,0:T(8,128)(2,1)}, u32[]{:S(2)}, u32[]{:S(2)}) collective-permute-start(bf16[192,2048]{1,0:T(8,128)(2,1)} %reduce-scatter.11.cloned.1.call-done), channel_id=1, source_target_pairs={{0,0},{1,8},{2,16},{3,24},{4,1},{5,9},{6,17},{7,25},{8,2},{9,10},{... | collective-permute-start | bytes 2359304 | tf_op jit(solution)/shard_map/ppermute | solution.py:443
  627.1 41.8 %all-to-all-start.5 = ((bf16[8,64,1536]{2,1,0:T(8,128)(2,1)}), bf16[8,64,1536]{2,1,0:T(8,128)(2,1)S(1)}, u32[]{:S(2)}, u32[]{:S(2)}) async-start(bf16[8,64,1536]{2,1,0:T(8,128)(2,1)} %bitcast.190), calls=%async_computation.8 | async-start | bytes 3145728 | tf_op jit(solution)/shard_map/all_to_all | solution.py:436
  (57 other events, 1013.0 us)
Sparse Core Ops, SparseCore 0:
  10.2 30.8 all-gather.6
  43.3 45.2 all-gather.4
  90.7 114.0 all-gather.8
  206.9 61.7 all-gather.10
  389.3 40.6 reduce-scatter.4
  432.3 60.1 reduce-scatter.10
  494.9 132.1 reduce-scatter.8
  630.0 33.5 reduce-scatter.6

commit v2 on v1

--- a/solution.py
+++ b/solution.py
@@ -1,10 +1,11 @@
-import functools
+import math
 
 import jax
 import jax.numpy as jnp
 from jax import lax
 from jax.experimental import pallas as pl
 from jax.experimental.pallas import tpu as pltpu
+from jax.sharding import Mesh
 from jax.sharding import PartitionSpec as P
 
 H = 16
@@ -234,30 +235,42 @@
     )(*operands)
 
 
-def swap(values, mask):
-    size = lax.axis_size("ctx")
-    return lax.ppermute(values, "ctx", [(i, i ^ mask) for i in range(size)])
-
-
-def gather_ctx(values):
-    size = lax.axis_size("ctx")
-    half = [values] + [swap(values, mask) for mask in range(2, size, 2)]
-    half = jnp.concatenate(half, axis=0)
-    return jnp.concatenate([half, swap(half, 1)], axis=0)
-
-
-def scatter_ctx(keep, give):
-    size = lax.axis_size("ctx")
-    chips = size // 2
-    rows = keep.shape[0] // chips
-    got = swap(give, 1)
-    keep = keep.reshape(chips, rows, -1)
-    got = got.reshape(chips, rows, -1)
-    sums = [keep[i].astype(high) + got[i].astype(high) for i in range(chips)]
-    total = sums[0]
-    for i in range(1, chips):
-        total = total + swap(sums[i].astype(low), 2 * i).astype(high)
-    return total
+CTX = ("chip", "core")
+LAYER = ("hi", "lo")
+
+
+def swap(values, axis, mask=1):
+    size = lax.axis_size(axis)
+    return lax.ppermute(values, axis, [(i, i ^ mask) for i in range(size)])
+
+
+def exchange(values, axis):
+    return lax.all_to_all(values, axis, 0, 0, tiled=True)
+
+
+def gather(values):
+    copies = jnp.broadcast_to(values[None], (lax.axis_size("chip"),) + values.shape)
+    half = exchange(copies, "chip").reshape(-1, values.shape[-1])
+    return half, swap(half, "core")
+
+
+def scatter(keep, give):
+    size = lax.axis_size("chip")
+    sums = (keep.astype(high) + swap(give, "core").astype(high)).astype(low)
+    sums = exchange(sums.reshape(size, keep.shape[0] // size, -1), "chip")
+    return jnp.sum(sums.astype(high), axis=0)
+
+
+def spread(values, axis):
+    return [values] + [swap(values, axis, mask) for mask in range(1, lax.axis_size(axis))]
+
+
+def in_order(pieces, index):
+    rows = pieces[0].shape[0]
+    whole = jnp.zeros((len(pieces) * rows,) + pieces[0].shape[1:], pieces[0].dtype)
+    for mask, piece in enumerate(pieces):
+        whole = lax.dynamic_update_slice_in_dim(whole, piece, (index ^ mask) * rows, axis=0)
+    return whole
 
 
 def halves(values):
@@ -265,23 +278,28 @@
     return values[:middle], values[middle:]
 
 
-def partial_rows(left, right, product):
-    keep, give = halves(left)
-    give = product(give, right).astype(low)
-    keep = product(keep, right).astype(low)
-    return scatter_ctx(keep, give)
+def after(values, *others):
+    return lax.optimization_barrier((values,) + others)
 
 
 def columns_of(values, index, width):
     return lax.dynamic_slice_in_dim(values, index * width, width, axis=1)
 
 
+def rows_of(values, index, height):
+    return lax.dynamic_slice_in_dim(values, index * height, height, axis=0)
+
+
+def sum_parts(lefts, rights):
+    return sum(t_dot(left, right) for left, right in zip(lefts, rights)).astype(low)
+
+
 def gather_rows(values):
-    return lax.all_gather(values, "fsdp", axis=0, tiled=True)
+    return lax.all_gather(values, LAYER, axis=0, tiled=True)
 
 
 def scatter_rows(values):
-    return lax.psum_scatter(values.astype(low), "fsdp", scatter_dimension=0, tiled=True)
+    return lax.psum_scatter(values, LAYER, scatter_dimension=0, tiled=True)
 
 
 def local(
@@ -300,10 +318,12 @@
     w_up,
     w_down,
 ):
-    n = lax.axis_size("ctx")
-    m = lax.axis_size("fsdp")
-    me = lax.axis_index("ctx")
-    layer = lax.axis_index("fsdp")
+    n = lax.axis_size(CTX)
+    m = lax.axis_size(LAYER)
+    me = lax.axis_index(CTX)
+    chip = lax.axis_index("chip")
+    core = lax.axis_index("core")
+    chips = n // 2
     width = tokens.shape[-1]
     own = 2 * BLOCK
     total = n * own
@@ -312,51 +332,66 @@
     qw = heads * HD
     hidden = w_gate.shape[1] // n
     piece = hidden // m
+    strip = width // (n * m)
     assert tokens.shape[0] == 1 and heads * n == H and repeat * KVH == n
 
     own_tokens = tokens.reshape(own, width)
     own_cotangent = cotangent.reshape(own, width)
-    all_tokens = gather_ctx(own_tokens)
+    out_cols = width // n
+    attn_w = jnp.concatenate(
+        [
+            columns_of(w_out, me, out_cols),
+            columns_of(w_query, me, qw),
+            columns_of(w_key, me // repeat, HD),
+            columns_of(w_value, me // repeat, HD),
+        ],
+        axis=1,
+    )
+    own_tokens, attn_w = after(own_tokens, attn_w)
+    layer = lax.axis_index(LAYER)
+    attn_w = gather_rows(attn_w)
+    out_w, qkv_w = attn_w[:, :out_cols], attn_w[:, out_cols:]
 
     small = jnp.concatenate([norm_attn, norm_ffn, q_gain, k_gain]).reshape(1, -1)
-    small = lax.all_to_all(jnp.broadcast_to(small, (m, small.shape[1])), "fsdp", 0, 0, tiled=True)
+    small = in_order(spread(small, LAYER), layer).astype(high)
     part, gain_part = norm_attn.shape[0], q_gain.shape[0]
-    small = small.astype(high)
     gain_attn = small[:, :part].reshape(-1)
     gain_ffn = small[:, part : 2 * part].reshape(-1)
     query_gain = small[:, 2 * part : 2 * part + gain_part].reshape(1, HD)
     key_gain = small[:, 2 * part + gain_part :].reshape(1, HD)
 
-    qkv_w = gather_rows(
-        jnp.concatenate(
-            [
-                columns_of(w_query, me, qw),
-                columns_of(w_key, me // repeat, HD),
-                columns_of(w_value, me // repeat, HD),
-            ],
-            axis=1,
-        )
-    )
-    out_cols = width // n
-    out_w = gather_rows(columns_of(w_out, me, out_cols))
-
     def hidden_columns(weights):
-        starts = [i * n * piece + me * piece for i in range(m)]
+        starts = [(i * n + me) * piece for i in range(m)]
         return [lax.dynamic_slice_in_dim(weights, start, piece, axis=1) for start in starts]
 
-    gate_up_w = gather_rows(jnp.concatenate(hidden_columns(w_gate) + hidden_columns(w_up), axis=1))
-    down_w = gather_rows(lax.dynamic_slice_in_dim(w_down, me * piece, piece, axis=0))
-
-    def slot_of(owner):
-        mask = owner ^ me
-        return (mask >> 1) + (mask & 1) * (n // 2)
-
-    out_w = gather_ctx(out_w).reshape(n, -1, out_cols)
+    gate_up_w = jnp.concatenate(hidden_columns(w_gate) + hidden_columns(w_up), axis=1)
+    down_w = rows_of(w_down, me, piece)
+    token_half = exchange(jnp.broadcast_to(own_tokens, (chips, own, width)), "chip").reshape(-1, width)
+    token_half, gate_up_w, down_w = after(token_half, gate_up_w, down_w)
+    token_parts = (token_half, swap(token_half, "core"))
+    gate_up_w = gather_rows(gate_up_w)
+    down_w = gather_rows(down_w)
+
+    out_half = spread(out_w, "chip")
+    owners = [me ^ (2 * mask) for mask in range(chips)]
+    owners = owners + [owner ^ 1 for owner in owners]
+
+    def by_layer(grads):
+        return grads.reshape(n, m, strip, -1).transpose(1, 0, 2, 3).reshape(width, -1)
+
+    def own_hidden(grads):
+        whole = jnp.zeros_like(grads)
+        for step in range(m):
+            targets = [(i, ((step + i) % m * n + i) // m) for i in range(n)]
+            rows = lax.ppermute(rows_of(grads, (step + me) % m, piece), CTX, targets)
+            place = (me // (n // m) - step) % m * piece
+            whole = lax.dynamic_update_slice_in_dim(whole, rows, place, axis=0)
+        return whole
 
     natural = jnp.arange(2 * n, dtype=jnp.int32)
     side = (natural >= n).astype(jnp.int32)
     owner = jnp.where(side == 0, natural, 2 * n - 1 - natural)
-    sources = 2 * slot_of(owner) + side
+    sources = 2 * (((owner & 1) ^ core) * chips + (owner >> 1)) + side
     places = 2 * owner + side
 
     segments = segment_ids.reshape(total)
@@ -371,38 +406,52 @@
     segment_column = segments.reshape(total, 1)
     segment_row = segments.reshape(1, total)
 
-    features = all_tokens.astype(high)
-    normed_low = (features * rms_factor(features) * gain_attn).astype(low)
-    qkv_raw = dot(normed_low, qkv_w)
+    normed_parts = []
+    for tokens_part in token_parts:
+        features = tokens_part.astype(high)
+        normed_parts.append((features * rms_factor(features) * gain_attn).astype(low))
+    qkv_raw = jnp.concatenate([dot(normed, qkv_w) for normed in normed_parts], axis=0)
     tables = (cosine, sine, query_gain, key_gain, segment_column, segment_row)
     mixed_rel, mixed_abs, query, key, value, logs = attend(
         total, heads, sources, places, qkv_raw, *tables
     )
-    mixed = lax.all_to_all(mixed_abs.reshape(n, own, qw), "ctx", 0, 0, tiled=True)
+    mixed = exchange(mixed_abs.reshape(n, own, qw), CTX)
+    mixed, own_cotangent, *out_half = after(mixed, own_cotangent, *out_half)
+    out_blocks = out_half + [swap(block, "core") for block in out_half]
+    upstream_half = in_order(spread(own_cotangent, "chip"), chip)
     mixed = mixed.transpose(1, 0, 2).reshape(own, n * qw)
     own_features = own_tokens.astype(high)
-    branch = [dot(mixed, out_w[i]) for i in range(n)]
-    branch = jnp.stack(branch)
-    branch = [lax.dynamic_index_in_dim(branch, slot_of(i), axis=0, keepdims=False) for i in range(n)]
-    middle = own_features + jnp.concatenate(branch, axis=1)
+    branch = jnp.zeros((own, width), high)
+    for block_owner, block in zip(owners, out_blocks):
+        branch = lax.dynamic_update_slice_in_dim(branch, dot(mixed, block), block_owner * out_cols, axis=1)
+    middle = own_features + branch
     factor_ffn = rms_factor(middle)
-    ffn_low = gather_ctx((middle * factor_ffn * gain_ffn).astype(low))
-    upstream_low = gather_ctx(own_cotangent)
-
-    gate_up = dot(ffn_low, gate_up_w)
-    gate, up = gate_up[:, :hidden], gate_up[:, hidden:]
-    sigmoid = jax.nn.sigmoid(gate)
-    silu = gate * sigmoid
-    hidden_low = (silu * up).astype(low)
-    block_sum = middle + partial_rows(hidden_low, down_w, dot)
-    block_out = block_sum.astype(low).reshape(tokens.shape)
-
-    grad_hidden = dot_t(upstream_low, down_w)
-    slope = sigmoid * (1.0 + gate * (1.0 - sigmoid))
-    gate_up_grad = jnp.concatenate(
-        [(grad_hidden * up * slope).astype(low), (grad_hidden * silu).astype(low)], axis=1
-    )
-    grad_ffn = partial_rows(gate_up_grad, gate_up_w, dot_t)
+    ffn_own = (middle * factor_ffn * gain_ffn).astype(low)
+    ffn_parts = gather(ffn_own)
+    upstream_parts = (upstream_half, swap(upstream_half, "core"))
+
+    hidden_parts, gates = [], []
+    for ffn_low in ffn_parts:
+        gate_up = dot(ffn_low, gate_up_w)
+        gate, up = gate_up[:, :hidden], gate_up[:, hidden:]
+        sigmoid = jax.nn.sigmoid(gate)
+        silu = gate * sigmoid
+        hidden_parts.append((silu * up).astype(low))
+        gates.append((up * sigmoid * (1.0 + gate * (1.0 - sigmoid)), silu))
+    grad_down = own_hidden(sum_parts(hidden_parts, upstream_parts))
+    grad_down, *upstream_parts = after(grad_down, *upstream_parts)
+    gate_up_grads = []
+    for upstream_low, (gate_slope, silu) in zip(upstream_parts, gates):
+        grad_hidden = dot_t(upstream_low, down_w)
+        grads = [(grad_hidden * gate_slope).astype(low), (grad_hidden * silu).astype(low)]
+        gate_up_grads.append(jnp.concatenate(grads, axis=1))
+    grad_ffn = [dot_t(grads, gate_up_w).astype(low) for grads in gate_up_grads]
+    grad_gate_up = by_layer(sum_parts(ffn_parts, gate_up_grads))
+    grad_ffn = scatter(grad_ffn[0], grad_ffn[1])
+    grad_down = scatter_rows(grad_down)
+    grad_ffn, grad_gate_up, grad_down = after(grad_ffn, grad_gate_up, grad_down)
+    grad_gate_up = scatter_rows(grad_gate_up)
+
     upstream = own_cotangent.astype(high)
     scaled = gain_ffn * grad_ffn
     inner = mean_last(middle * scaled)
@@ -411,15 +460,19 @@
     middle_low = grad_middle.astype(low)
 
     mixed_grad = 0.0
-    for mask in range(n):
-        slot = (mask >> 1) + (mask & 1) * (n // 2)
-        mixed_grad = mixed_grad + dot_t(columns_of(middle_low, me ^ mask, out_cols), out_w[slot])
+    for block_owner, block in zip(owners, out_blocks):
+        mixed_grad = mixed_grad + dot_t(columns_of(middle_low, block_owner, out_cols), block)
     mixed_grad = mixed_grad.astype(low).reshape(own, n, qw).transpose(1, 0, 2)
-    mixed_grad = lax.all_to_all(mixed_grad, "ctx", 0, 0, tiled=True).reshape(total, qw)
+    mixed_grad = exchange(mixed_grad, CTX).reshape(total, qw)
+    mixed_grad, late_low = after(mixed_grad, middle_low)
+    late_half = in_order(spread(late_low, "chip"), chip)
+    grad_out = sum_parts(halves(mixed_rel), (late_half, swap(late_half, "core")))
     qkv_grad, grad_gains = attend_back(
         total, heads, sources, places, qkv_raw, *tables, query, key, value, logs, mixed_grad
     )
-    grad_attn = partial_rows(qkv_grad, qkv_w, dot_t)
+    qkv_grads = halves(qkv_grad)
+    grad_attn = [dot_t(grads, qkv_w).astype(low) for grads in qkv_grads]
+    grad_attn = scatter(grad_attn[0], grad_attn[1])
     factor_attn = rms_factor(own_features)
     scaled = gain_attn * grad_attn
     inner = mean_last(own_features * scaled)
@@ -427,24 +480,27 @@
     grad_gain_attn = jnp.sum(grad_attn * own_features * factor_attn, axis=0)
     input_grad = input_grad.reshape(tokens.shape)
 
-    strip = width // (n * m)
-
-    def grad_rows(left, right):
-        grads = t_dot(left, right).astype(low).reshape(n, m, strip, right.shape[1])
-        grads = grads.transpose(1, 0, 2, 3).reshape(width, right.shape[1])
-        grads = scatter_rows(grads).reshape(n, strip, right.shape[1])
-        return lax.all_to_all(grads, "ctx", 0, 0, tiled=True).astype(high)
-
-    grad_down = scatter_rows(t_dot(hidden_low, upstream_low))
-    targets = []
-    for device in range(n * m):
-        block = (device % m) * n + device // m
-        targets.append((device, block))
-    grad_down = lax.ppermute(grad_down, ("ctx", "fsdp"), targets).astype(high)
-    grad_gate_up = grad_rows(ffn_low, gate_up_grad).reshape(n, strip, 2, m, piece)
-    grad_gate_up = grad_gate_up.transpose(2, 1, 3, 0, 4).reshape(2, strip, -1)
-    grad_out = scatter_rows(t_dot(mixed_rel, gather_ctx(middle_low))).astype(high)
-    grad_qkv = grad_rows(normed_low, qkv_grad)
+    lanes = math.gcd((heads + 2) * HD, width)
+    grad_qkv = by_layer(sum_parts(normed_parts, qkv_grads))
+    grad_late = [grad_qkv.reshape(m, -1, lanes), grad_out.reshape(m, -1, lanes)]
+    grad_late = jnp.concatenate(grad_late, axis=1)
+    grad_attn, grad_gate_up, grad_late, *hidden_late = after(
+        grad_attn, grad_gate_up, grad_late, *hidden_parts
+    )
+    grad_late = scatter_rows(grad_late.reshape(-1, lanes))
+    block_parts = [dot(values, down_w).astype(low) for values in hidden_late]
+    block_out = middle + scatter(block_parts[0], block_parts[1])
+    block_out = block_out.astype(low).reshape(tokens.shape)
+
+    grad_down = grad_down.astype(high)
+    grad_gate_up = exchange(grad_gate_up.reshape(n, strip, -1), CTX).astype(high)
+    grad_gate_up = grad_gate_up.reshape(n, strip, 2, m, piece).transpose(2, 1, 3, 0, 4)
+    grad_gate_up = grad_gate_up.reshape(2, strip, -1)
+
+    late_rows = n * strip * (heads + 2) * HD // lanes
+    grad_qkv, grad_out = grad_late[:late_rows], grad_late[late_rows:]
+    grad_out = grad_out.reshape(-1, width).astype(high)
+    grad_qkv = exchange(grad_qkv.reshape(n, strip, -1), CTX).astype(high)
     grad_query = grad_qkv[:, :, :qw].transpose(1, 0, 2).reshape(strip, -1)
 
     def grad_of_kv(grads):
@@ -464,7 +520,7 @@
         ],
         axis=1,
     )
-    gains = jnp.sum(lax.all_to_all(partial, ("ctx", "fsdp"), 0, 0, tiled=True), axis=0)
+    gains = jnp.sum(exchange(partial, CTX + LAYER), axis=0)
     end = 2 * strip + HD // devices
     return (
         block_out,
@@ -484,11 +540,13 @@
 
 
 def solution(mesh):
-    rows = P("fsdp", None)
-    line = P("fsdp")
-    blocks = P("fsdp", None, "ctx", None, None)
-    both = P(("ctx", "fsdp"), None)
-    both_line = P(("ctx", "fsdp"))
+    n, m = mesh.shape["ctx"], mesh.shape["fsdp"]
+    mesh = Mesh(mesh.devices.reshape(n // 2, 2, m // 2, 2), CTX + LAYER)
+    rows = P(LAYER, None)
+    line = P(LAYER)
+    blocks = P(LAYER, None, CTX, None, None)
+    both = P(CTX + LAYER, None)
+    both_line = P(CTX + LAYER)
     in_specs = (blocks, rows, blocks, line, rows, rows, rows, line, line, rows, line, rows, rows, rows)
     out_specs = (
         blocks,

time: 710 us -> 551 us (0.78)
  waiting for transfers between devices: 360 us -> 171 us
  blocking collectives: 22.6 us -> 55.5 us
  other arithmetic: 44.9 us -> 29.6 us
  matrix products: 96.1 us -> 108 us
    reduce_scatter x4 -> x3, waiting for transfers between devices: 164 us -> 14.2 us  [scatter_rows(): return lax.psum_scatter(values, LAYER, scatter_dimension=0, tiled=True)]
    ppermute x33 -> x27, waiting for transfers between devices: 143 us -> 54.6 us  [the longest x23 39.3 us: swap(): return lax.ppermute(values, axis, [(i, i ^ mask) for i in range(size)])]
    all_to_all x4 -> x7, waiting for transfers between devices: 5.46 us -> 82.8 us  [exchange(): return lax.all_to_all(values, axis, 0, 0, tiled=True)]
    all_to_all x2 -> x3, blocking collectives: 22.6 us -> 55.5 us  [exchange(): return lax.all_to_all(values, axis, 0, 0, tiled=True)]
    all_gather x4 -> x3, waiting for transfers between devices: 48.2 us -> 19.4 us  [gather_rows(): return lax.all_gather(values, LAYER, axis=0, tiled=True)]
    unnamed x108 -> x101, local copies, waits for them, and re-layouts: 28.5 us -> 9.78 us
    dynamic_update_slice x0 -> x16, local copies, waits for them, and re-layouts: none -> 17.7 us  [the longest x12 9.34 us: in_order(): lax.dynamic_update_slice_in_dim(whole, piece, (index ^ mask) * rows, axis=0)]
    all_to_all x4 -> x7, starting transfers between devices: 15.6 us -> 30.4 us  [exchange(): return lax.all_to_all(values, axis, 0, 0, tiled=True)]
  transfers between devices with their start and end apart: 45 -> 40, of which waited for: 18 -> 17; matrix products, arithmetic and copies ran while one was open for 23% -> 37% of each run, Pallas kernels for 1% -> 4%
where the time goes in v2:
time: 551 us; the launch traced here: 544 us
  waiting for transfers between devices  171 us (31%)
  matrix products  108 us (20%)
  local copies, waits for them, and re-layouts  80.4 us (15%)
  starting transfers between devices  63.1 us (11%)
  blocking collectives  55.5 us (10%)
  other arithmetic  29.6 us (5%)
  Pallas kernels  19.7 us (4%)
  between operations  16 us (3%)
    all_to_all x7, waiting for transfers between devices, exchange(): return lax.all_to_all(values, axis, 0, 0, tiled=True)  82.8 us
    all_to_all x3, blocking collectives, exchange(): return lax.all_to_all(values, axis, 0, 0, tiled=True)  55.5 us
    ppermute x23, waiting for transfers between devices, swap(): return lax.ppermute(values, axis, [(i, i ^ mask) for i in range(size)])  39.3 us
    dot_general x14, matrix products, dot(): return jnp.dot(left, right, preferred_element_type=high)  37.6 us
    dot_general x8, matrix products, t_dot(): lax.dot_general(left, right, (((0,), (0,)), ((), ())), preferred_element_...  36.1 us
    dot_general x14, matrix products, dot_t(): lax.dot_general(left, right, (((1,), (1,)), ((), ())), preferred_element_...  34.5 us
    all_to_all x7, starting transfers between devices, exchange(): return lax.all_to_all(values, axis, 0, 0, tiled=True)  30.4 us
    all_gather x3, waiting for transfers between devices, gather_rows(): return lax.all_gather(values, LAYER, axis=0, tiled=True)  19.4 us
  transfers between devices with their start and end apart: 40, of which 17 were waited for; matrix products, arithmetic and copies ran while one was open for 37% of the time, Pallas kernels for 4%

profile of v2, /device:TPU:0, one launch (start us, length us, event | category | flops | bytes accessed | tf_op | source)
XLA Modules:
  0.0 543.6 jit_solution(3152783241518502551)
XLA Ops:
  24.4 18.4 %all-to-all-done = bf16[4,128,2048]{2,1,0:T(8,128)(2,1)} async-done(((bf16[4,128,2048]{2,1,0:T(8,128)(2,1)}), bf16[4,128,2048]{2,1,0:T(8,128)(2,1)}, u32[]{:S(2)}, u32[]{:S(2)}) %all-to-all-start) | async-done | bytes 2097184 | tf_op jit(solution)/shard_map/all_to_all | solution.py:248
  57.7 19.3 %all-gather.4.cloned.1.call-done = bf16[2048,768]{1,0:T(8,128)(2,1)} async-done(((bf16[512,768]{1,0:T(8,128)(2,1)}), bf16[2048,768]{1,0:T(8,128)(2,1)}) %all-gather.4.cloned.1.call-update) | async-done | bytes 3145744 | tf_op jit(solution)/shard_map/all_gather | solution.py:298
  91.4 8.8 %attend.1 = (bf16[1024,256]{1,0:T(8,128)(2,1)S(1)}, bf16[1024,256]{1,0:T(8,128)(2,1)S(1)}, bf16[1024,256]{1,0:T(8,128)(2,1)S(1)}, bf16[1024,128]{1,0:T(8,128)(2,...) custom-call(s32[16]{0:T(128)S(1)} %get-tuple-element.122.sources_ref, ...), custom_call_target="tpu_custom_call" | custom-call | tf_op jit(solution)/shard_map/attend/pallas_call | solution.py:208
  106.4 27.2 %all-to-all-done.1 = bf16[8,128,256]{1,2,0:T(8,128)(2,1)S(1)} async-done(((bf16[8,128,256]{1,2,0:T(8,128)(2,1)}), bf16[8,128,256]{1,2,0:T(8,128)(2,1)S(1)}, u32[]{:S(2)}, u32[]{:S(2)}) %all-to-all-start.1) | async-done | bytes 524320 | tf_op jit(solution)/shard_map/all_to_all | solution.py:248
  146.3 29.3 %all_to_all.54 = bf16[4,128,2048]{2,1,0:T(8,128)(2,1)} all-to-all(bf16[4,128,2048]{2,1,0:T(8,128)(2,1)S(1)} %broadcast_in_dim.14), channel_id=1, replica_groups=mesh['chip'=4,'core'=2,'hi'=2,'lo'=2] {'chip'}, dimensions={0} | all-to-all | bytes 4194304 | tf_op jit(solution)/shard_map/all_to_all | solution.py:248
  181.9 8.5 %collective-permute-done.11 = bf16[128,2048]{1,0:T(8,128)(2,1)} collective-permute-done((bf16[128,2048]{1,0:T(8,128)(2,1)S(1)}, bf16[128,2048]{1,0:T(8,128)(2,1)}, u32[]{:S(2)}, u32[]{:S(2)}) %collective-permute-start.11) | collective-permute-done | bytes 524320 | tf_op jit(solution)/shard_map/ppermute | solution.py:244
  192.2 9.6 %collective-permute-done.12 = bf16[128,2048]{1,0:T(8,128)(2,1)} collective-permute-done((bf16[128,2048]{1,0:T(8,128)(2,1)S(1)}, bf16[128,2048]{1,0:T(8,128)(2,1)}, u32[]{:S(2)}, u32[]{:S(2)}) %collective-permute-start.12) | collective-permute-done | bytes 524320 | tf_op jit(solution)/shard_map/ppermute | solution.py:244
  204.7 6.3 %fusion.77 = f32[512,1536]{1,0:T(8,128)S(1)} fusion(bf16[512,2048]{1,0:T(8,128)(2,1)} %collective-permute-done.14, bf16[2048,1536]{1,0:T(8,128)(2,1)} %all-gather.6.cloned.1.call-done), kind=kOutput, calls=%fused_computation.185 | convolution fusion | flops 3221225472 | bytes 11534336 | tf_op jit(solution)/shard_map/dot_general | solution.py:26
  228.9 7.4 %collective-permute-start.16 = (bf16[192,2048]{1,0:T(8,128)(2,1)}, bf16[192,2048]{1,0:T(8,128)(2,1)}, u32[]{:S(2)}, u32[]{:S(2)}) collective-permute-start(bf16[192,2048]{1,0:T(8,128)(2,1)} %get-tuple-element.102), channel_id=1, source_target_pairs={{0,0},{4,8},{8,16},{12,24},{16,4},{20,12},{24,20},{28,28},{1,1},{5... | collective-permute-start | bytes 2359304 | tf_op jit(solution)/shard_map/ppermute | solution.py:386
  246.9 11.5 %collective-permute-done.17 = bf16[192,2048]{1,0:T(8,128)(2,1)} collective-permute-done((bf16[192,2048]{1,0:T(8,128)(2,1)}, bf16[192,2048]{1,0:T(8,128)(2,1)}, u32[]{:S(2)}, u32[]{:S(2)}) %collective-permute-start.17) | collective-permute-done | bytes 786464 | tf_op jit(solution)/shard_map/ppermute | solution.py:386
  275.4 7.0 %convolution_convert_fusion.4 = bf16[512,2048]{1,0:T(8,128)(2,1)S(1)} fusion(bf16[2048,1536]{1,0:T(8,128)(2,1)} %all-gather.6.cloned.1.call-done, bf16[512,768]{1,0:T(8,128)(2,1)S(1)} %get-tuple-element.96, bf16[512,768]{1,0:T(8,128)(2,1)S(1)} %get-tuple-element.95), kind=kOutput, calls=%fused_computation.25 | convolution fusion | flops 3225419776 | bytes 9961472 | tf_op jit(solution)/shard_map/dot_general | solution.py:30
  297.7 10.2 %fusion.28 = f32[2048,1536]{1,0:T(8,128)} fusion(bf16[512,2048]{1,0:T(8,128)(2,1)} %bitcast.9, bf16[512,768]{1,0:T(8,128)(2,1)} %copy-done.41, bf16[512,768]{1,0:T(8,128)(2,1)} %copy-done.40), kind=kOutput, calls=%fused_computation.81 | convolution fusion | flops 3224371200 | bytes 16252928 | tf_op jit(solution)/shard_map/dot_general | solution.py:34
  308.0 7.3 %add_convert_fusion = bf16[2048,1536]{1,0:T(8,128)(2,1)S(1)} fusion(f32[2048,1536]{1,0:T(8,128)} %fusion.28, bf16[512,2048]{1,0:T(8,128)(2,1)} %collective-permute-done.14, bf16[512,768]{1,0:T(8,128)(2,1)S(1)} %copy-done.45, bf16[512,768]{1,0:T(8,128)(2,1)S(1)} %copy-done.43), kind=kOutput, calls=%fused_computation | convolution fusion | flops 3230662656 | bytes 22544384 | tf_op jit(solution)/shard_map/dot_general | solution.py:34
  318.6 5.8 %all-to-all-done.3 = bf16[4,128,2048]{2,1,0:T(8,128)(2,1)} async-done(((bf16[4,128,2048]{2,1,0:T(8,128)(2,1)}), bf16[4,128,2048]{2,1,0:T(8,128)(2,1)}, u32[]{:S(2)}, u32[]{:S(2)}) %all-to-all-start.3) | async-done | bytes 2097184 | tf_op jit(solution)/shard_map/all_to_all | solution.py:248
  343.9 13.5 %all_to_all.55 = bf16[8,128,256]{2,1,0:T(8,128)(2,1)S(1)} all-to-all(bf16[8,128,256]{2,1,0:T(8,128)(2,1)S(1)} %bitcast.138), channel_id=1, replica_groups=mesh['chip'=4,'core'=2,'hi'=2,'lo'=2] {'chip','core'}, dimensions={0} | all-to-all | bytes 1048576 | tf_op jit(solution)/shard_map/all_to_all | solution.py:248
  357.3 10.9 %attend_back.1 = (bf16[1024,512]{1,0:T(8,128)(2,1)S(1)}, f32[2,128]{1,0:T(2,128)S(1)}) custom-call(s32[16]{0:T(128)S(1)} %get-tuple-element.122.sources_ref, s32[16]{0:T(128)S(1)} %get-tuple-element.121.places_ref, f32[1024,512]{1,0:T(8,128)} %pad_maximum_fusion.1.raw_ref, f32[1024,128]{1,0:T(8,128)S(1)} %get-tuple-element.131.cos_ref, ...), custom_call_target="tpu_custom_call" | custom-call | tf_op jit(solution)/shard_map/attend_back/pallas_call | solution.py:223
  375.6 8.8 %collective-permute-done.22 = bf16[128,2048]{1,0:T(8,128)(2,1)S(1)} collective-permute-done((bf16[128,2048]{1,0:T(8,128)(2,1)S(1)}, bf16[128,2048]{1,0:T(8,128)(2,1)S(1)}, u32[]{:S(2)}, u32[]{:S(2)}) %collective-permute-start.22) | collective-permute-done | bytes 524320 | tf_op jit(solution)/shard_map/ppermute | solution.py:244
  385.2 10.2 %collective-permute-done.23 = bf16[128,2048]{1,0:T(8,128)(2,1)S(1)} collective-permute-done((bf16[128,2048]{1,0:T(8,128)(2,1)S(1)}, bf16[128,2048]{1,0:T(8,128)(2,1)S(1)}, u32[]{:S(2)}, u32[]{:S(2)}) %collective-permute-start.23) | collective-permute-done | bytes 524320 | tf_op jit(solution)/shard_map/ppermute | solution.py:244
  423.1 7.2 %all-to-all-done.5 = bf16[4,128,2048]{2,1,0:T(8,128)(2,1)} async-done(((bf16[4,128,2048]{2,1,0:T(8,128)(2,1)}), bf16[4,128,2048]{2,1,0:T(8,128)(2,1)}, u32[]{:S(2)}, u32[]{:S(2)}) %all-to-all-start.5) | async-done | bytes 2097184 | tf_op jit(solution)/shard_map/all_to_all | solution.py:248
  432.3 11.1 %reduce-scatter.6.cloned.1.call-done = bf16[512,1536]{1,0:T(8,128)(2,1)} async-done(((bf16[2048,1536]{1,0:T(8,128)(2,1)}), bf16[512,1536]{1,0:T(8,128)(2,1)}) %reduce-scatter.6.cloned.1.call-update) | async-done | bytes 1572880 | tf_op jit(solution)/shard_map/reduce_scatter | solution.py:302
  449.4 12.8 %all_to_all.56 = f32[32,1,136]{2,1,0:T(1,128)S(1)} all-to-all(f32[32,1,136]{2,1,0:T(1,128)S(1)} %all_to_all.40), channel_id=1, replica_groups=mesh['chip'=4,'core'=2,'hi'=2,'lo'=2] {'chip','core','hi','lo'}, dimensions={0} | all-to-all | bytes 34816 | tf_op jit(solution)/shard_map/all_to_all | solution.py:248
  467.8 5.8 %add_convert_fusion.2 = bf16[512,2048]{1,0:T(8,128)(2,1)} fusion(bf16[512,2048]{1,0:T(8,128)(2,1)} %collective-permute-done.26, bf16[512,768]{1,0:T(8,128)(2,1)S(1)} %copy-done.31, bf16[768,2048]{1,0:T(8,128)(2,1)} %all-gather.8.cloned.1.call-done), kind=kOutput, calls=%fused_computation.13 | convolution fusion | flops 1615855616 | bytes 8126464 | tf_op jit(solution)/shard_map/dot_general | solution.py:26
  473.6 13.9 %all-to-all-done.9 = bf16[8,64,1536]{2,1,0:T(8,128)(2,1)} async-done(((bf16[8,64,1536]{2,1,0:T(8,128)(2,1)}), bf16[8,64,1536]{2,1,0:T(8,128)(2,1)}, u32[]{:S(2)}, u32[]{:S(2)}) %all-to-all-start.9) | async-done | bytes 1572896 | tf_op jit(solution)/shard_map/all_to_all | solution.py:248
  527.0 6.7 %all-to-all-done.8 = bf16[8,64,512]{2,1,0:T(8,128)(2,1)S(1)} async-done(((bf16[8,64,512]{2,1,0:T(8,128)(2,1)}), bf16[8,64,512]{2,1,0:T(8,128)(2,1)S(1)}, u32[]{:S(2)}, u32[]{:S(2)}) %all-to-all-start.8) | async-done | bytes 524320 | tf_op jit(solution)/shard_map/all_to_all | solution.py:248
  (300 shorter events, 250.0 us)
Async XLA Ops:
  7.2 69.9 %all-gather.4.cloned.1.call-start = ((), (), s32[]{:S(2)}) async-start(), calls=%async_computation.13 | async-start | bytes 3932160 | tf_op jit(solution)/shard_map/all_gather | solution.py:298
  12.0 30.9 %all-to-all-start = ((bf16[4,128,2048]{2,1,0:T(8,128)(2,1)}), bf16[4,128,2048]{2,1,0:T(8,128)(2,1)}, u32[]{:S(2)}, u32[]{:S(2)}) async-start(bf16[4,128,2048]{2,1,0:T(8,128)(2,1)} %broadcast_in_dim.11), calls=%async_computation | async-start | bytes 4194304 | tf_op jit(solution)/shard_map/all_to_all | solution.py:248
  17.1 187.5 %all-gather.6.cloned.1.call-start = ((), (), s32[]{:S(2)}) async-start(), calls=%async_computation.14 | async-start | bytes 7864320 | tf_op jit(solution)/shard_map/all_gather | solution.py:298
  79.3 54.4 %collective-permute-start.4 = (bf16[2048,256]{1,0:T(8,128)(2,1)}, bf16[2048,256]{1,0:T(8,128)(2,1)}, u32[]{:S(2)}, u32[]{:S(2)}) collective-permute-start(bf16[2048,256]{1,0:T(8,128)(2,1)} %slice.114), channel_id=1, source_target_pairs={{0,8},{8,0},{16,24},{24,16},{1,9},{9,1},{17,25},{25,17},{2,10},{10... | collective-permute-start | bytes 3145736 | tf_op jit(solution)/shard_map/ppermute | solution.py:244
  80.8 52.9 %collective-permute-start.5 = (bf16[2048,256]{1,0:T(8,128)(2,1)}, bf16[2048,256]{1,0:T(8,128)(2,1)}, u32[]{:S(2)}, u32[]{:S(2)}) collective-permute-start(bf16[2048,256]{1,0:T(8,128)(2,1)} %slice.114), channel_id=1, source_target_pairs={{0,16},{8,24},{16,0},{24,8},{1,17},{9,25},{17,1},{25,9},{2,18},{10... | collective-permute-start | bytes 3145736 | tf_op jit(solution)/shard_map/ppermute | solution.py:244
  82.3 51.4 %collective-permute-start.6 = (bf16[2048,256]{1,0:T(8,128)(2,1)}, bf16[2048,256]{1,0:T(8,128)(2,1)}, u32[]{:S(2)}, u32[]{:S(2)}) collective-permute-start(bf16[2048,256]{1,0:T(8,128)(2,1)} %slice.114), channel_id=1, source_target_pairs={{0,24},{8,16},{16,8},{24,0},{1,25},{9,17},{17,9},{25,1},{2,26},{10... | collective-permute-start | bytes 3145736 | tf_op jit(solution)/shard_map/ppermute | solution.py:244
  102.7 30.9 %all-to-all-start.1 = ((bf16[8,128,256]{1,2,0:T(8,128)(2,1)}), bf16[8,128,256]{1,2,0:T(8,128)(2,1)S(1)}, u32[]{:S(2)}, u32[]{:S(2)}) async-start(bf16[8,128,256]{1,2,0:T(8,128)(2,1)} %copy.65), calls=%async_computation.1 | async-start | bytes 1048576 | tf_op jit(solution)/shard_map/all_to_all | solution.py:248
  106.3 162.2 %all-gather.8.cloned.1.call-start = ((), (), s32[]{:S(2)}) async-start(), calls=%async_computation.15 | async-start | bytes 3932160 | tf_op jit(solution)/shard_map/all_gather | solution.py:298
  175.5 29.1 %collective-permute-start.14 = (bf16[512,2048]{1,0:T(8,128)(2,1)}, bf16[512,2048]{1,0:T(8,128)(2,1)}, u32[]{:S(2)}, u32[]{:S(2)}) collective-permute-start(bf16[512,2048]{1,0:T(8,128)(2,1)} %bitcast.9), channel_id=1, source_target_pairs={{0,4},{4,0},{1,5},{5,1},{2,6},{6,2},{3,7},{7,3},{8,12},{12,8},{9,1... | collective-permute-start | bytes 6291464 | tf_op jit(solution)/shard_map/ppermute | solution.py:244
  176.4 25.4 %collective-permute-start.12 = (bf16[128,2048]{1,0:T(8,128)(2,1)S(1)}, bf16[128,2048]{1,0:T(8,128)(2,1)}, u32[]{:S(2)}, u32[]{:S(2)}) collective-permute-start(bf16[128,2048]{1,0:T(8,128)(2,1)S(1)} %bitcast.130), channel_id=1, source_target_pairs={{0,16},{8,24},{16,0},{24,8},{1,17},{9,25},{17,1},{25,9},{2,18},{10... | collective-permute-start | bytes 1572872 | tf_op jit(solution)/shard_map/ppermute | solution.py:244
  177.0 153.5 %reduce-scatter.4.cloned.1.call-start = ((), (), s32[]{:S(2)}) async-start(), calls=%async_computation.16 | async-start | bytes 3932160 | tf_op jit(solution)/shard_map/reduce_scatter | solution.py:302
  177.3 26.5 %collective-permute-start.13 = (bf16[128,2048]{1,0:T(8,128)(2,1)S(1)}, bf16[128,2048]{1,0:T(8,128)(2,1)S(1)}, u32[]{:S(2)}, u32[]{:S(2)}) collective-permute-start(bf16[128,2048]{1,0:T(8,128)(2,1)S(1)} %bitcast.131), channel_id=1, source_target_pairs={{0,24},{8,16},{16,8},{24,0},{1,25},{9,17},{17,9},{25,1},{2,26},{10... | collective-permute-start | bytes 1572872 | tf_op jit(solution)/shard_map/ppermute | solution.py:244
  236.3 22.1 %collective-permute-start.17 = (bf16[192,2048]{1,0:T(8,128)(2,1)}, bf16[192,2048]{1,0:T(8,128)(2,1)}, u32[]{:S(2)}, u32[]{:S(2)}) collective-permute-start(bf16[192,2048]{1,0:T(8,128)(2,1)} %get-tuple-element.101), channel_id=1, source_target_pairs={{0,8},{4,16},{8,24},{12,0},{16,12},{20,20},{24,28},{28,4},{1,9},{5... | collective-permute-start | bytes 2359304 | tf_op jit(solution)/shard_map/ppermute | solution.py:386
  238.2 22.3 %collective-permute-start.18 = (bf16[192,2048]{1,0:T(8,128)(2,1)}, bf16[192,2048]{1,0:T(8,128)(2,1)}, u32[]{:S(2)}, u32[]{:S(2)}) collective-permute-start(bf16[192,2048]{1,0:T(8,128)(2,1)} %get-tuple-element.100), channel_id=1, source_target_pairs={{0,16},{4,24},{8,0},{12,8},{16,20},{20,28},{24,4},{28,12},{1,17},{... | collective-permute-start | bytes 2359304 | tf_op jit(solution)/shard_map/ppermute | solution.py:386
  238.3 28.1 %collective-permute-start.19 = (bf16[192,2048]{1,0:T(8,128)(2,1)}, bf16[192,2048]{1,0:T(8,128)(2,1)}, u32[]{:S(2)}, u32[]{:S(2)}) collective-permute-start(bf16[192,2048]{1,0:T(8,128)(2,1)} %get-tuple-element.99), channel_id=1, source_target_pairs={{0,24},{4,0},{8,8},{12,16},{16,28},{20,4},{24,12},{28,20},{1,25},{... | collective-permute-start | bytes 2359304 | tf_op jit(solution)/shard_map/ppermute | solution.py:386
  293.0 31.4 %all-to-all-start.3 = ((bf16[4,128,2048]{2,1,0:T(8,128)(2,1)}), bf16[4,128,2048]{2,1,0:T(8,128)(2,1)}, u32[]{:S(2)}, u32[]{:S(2)}) async-start(bf16[4,128,2048]{2,1,0:T(8,128)(2,1)} %bitcast.136), calls=%async_computation.3 | async-start | bytes 4194304 | tf_op jit(solution)/shard_map/all_to_all | solution.py:248
  297.5 146.0 %reduce-scatter.6.cloned.1.call-start = ((), (), s32[]{:S(2)}) async-start(), calls=%async_computation.17 | async-start | bytes 7864320 | tf_op jit(solution)/shard_map/reduce_scatter | solution.py:302
  369.5 27.6 %collective-permute-start.21 = (bf16[512,2048]{1,0:T(8,128)(2,1)S(1)}, bf16[512,2048]{1,0:T(8,128)(2,1)S(1)}, u32[]{:S(2)}, u32[]{:S(2)}) collective-permute-start(bf16[512,2048]{1,0:T(8,128)(2,1)S(1)} %convolution_convert_fusion.2), channel_id=1, source_target_pairs={{0,4},{4,0},{1,5},{5,1},{2,6},{6,2},{3,7},{7,3},{8,12},{12,8},{9,1... | collective-permute-start | bytes 6291464 | tf_op jit(solution)/shard_map/ppermute | solution.py:244
  370.2 25.2 %collective-permute-start.23 = (bf16[128,2048]{1,0:T(8,128)(2,1)S(1)}, bf16[128,2048]{1,0:T(8,128)(2,1)S(1)}, u32[]{:S(2)}, u32[]{:S(2)}) collective-permute-start(bf16[128,2048]{1,0:T(8,128)(2,1)S(1)} %get-tuple-element.68), channel_id=1, source_target_pairs={{0,16},{8,24},{16,0},{24,8},{1,17},{9,25},{17,1},{25,9},{2,18},{10... | collective-permute-start | bytes 1572872 | tf_op jit(solution)/shard_map/ppermute | solution.py:244
  370.8 25.5 %collective-permute-start.24 = (bf16[128,2048]{1,0:T(8,128)(2,1)S(1)}, bf16[128,2048]{1,0:T(8,128)(2,1)S(1)}, u32[]{:S(2)}, u32[]{:S(2)}) collective-permute-start(bf16[128,2048]{1,0:T(8,128)(2,1)S(1)} %get-tuple-element.68), channel_id=1, source_target_pairs={{0,24},{8,16},{16,8},{24,0},{1,25},{9,17},{17,9},{25,1},{2,26},{10... | collective-permute-start | bytes 1572872 | tf_op jit(solution)/shard_map/ppermute | solution.py:244
  399.8 30.5 %all-to-all-start.5 = ((bf16[4,128,2048]{2,1,0:T(8,128)(2,1)}), bf16[4,128,2048]{2,1,0:T(8,128)(2,1)}, u32[]{:S(2)}, u32[]{:S(2)}) async-start(bf16[4,128,2048]{2,1,0:T(8,128)(2,1)} %bitcast.135), calls=%async_computation.6 | async-start | bytes 4194304 | tf_op jit(solution)/shard_map/all_to_all | solution.py:248
  404.3 114.3 %reduce-scatter.8.cloned.1.call-start = ((), (), s32[]{:S(2)}) async-start(), calls=%async_computation.18 | async-start | bytes 3932160 | tf_op jit(solution)/shard_map/reduce_scatter | solution.py:302
  462.1 25.4 %all-to-all-start.9 = ((bf16[8,64,1536]{2,1,0:T(8,128)(2,1)}), bf16[8,64,1536]{2,1,0:T(8,128)(2,1)}, u32[]{:S(2)}, u32[]{:S(2)}) async-start(bf16[8,64,1536]{2,1,0:T(8,128)(2,1)} %bitcast.139), calls=%async_computation.12 | async-start | bytes 3145728 | tf_op jit(solution)/shard_map/all_to_all | solution.py:248
  487.5 29.1 %all-to-all-start.6 = ((bf16[4,128,2048]{2,1,0:T(8,128)(2,1)}), bf16[4,128,2048]{2,1,0:T(8,128)(2,1)}, u32[]{:S(2)}, u32[]{:S(2)}) async-start(bf16[4,128,2048]{2,1,0:T(8,128)(2,1)} %bitcast.134), calls=%async_computation.8 | async-start | bytes 4194304 | tf_op jit(solution)/shard_map/all_to_all | solution.py:248
  (64 other events, 553.1 us)
Sparse Core Ops, SparseCore 0:
  10.5 66.5 all-gather.3
  79.2 113.8 all-gather.5
  195.3 61.7 all-gather.7
  268.6 61.7 reduce-scatter.3
  332.6 110.7 reduce-scatter.5
  445.6 61.2 reduce-scatter.7

commit v3 on v2

--- a/solution.py
+++ b/solution.py
@@ -1,4 +1,4 @@
-import math
+import functools
 
 import jax
 import jax.numpy as jnp
@@ -235,6 +235,84 @@
     )(*operands)
 
 
+def project_back_kernel(chips, *refs):
+    owners_ref, sums_ref, middle_ref, up_ref, gain_ref = refs[:5]
+    (grad_ref, low_ref, gain_grad_ref, out_ref, weights_ref, sems) = refs[-6:]
+    blocks = refs[5:-6]
+    copies = [
+        pltpu.make_async_copy(block, weights_ref.at[i], sems.at[i]) for i, block in enumerate(blocks)
+    ]
+    for copy in copies:
+        copy.start()
+    upstream = sums_ref[0].astype(high)
+    for chip in range(1, chips):
+        upstream = upstream + sums_ref[chip].astype(high)
+    values = middle_ref[...]
+    factor = rms_factor(values)
+    gain_grad_ref[...] = jnp.sum(upstream * values * factor, axis=0, keepdims=True)
+    scaled = gain_ref[...] * upstream
+    inner = mean_last(values * scaled)
+    back = factor * scaled - values * (factor * factor * factor) * inner
+    grad = up_ref[...].astype(high) + back
+    grad_ref[...] = grad
+    low_ref[...] = grad.astype(low)
+    cols = weights_ref.shape[2]
+    total = 0.0
+    for i, copy in enumerate(copies):
+        start = pl.multiple_of(owners_ref[i] * cols, cols)
+        copy.wait()
+        total = total + dot_t(low_ref[:, pl.ds(start, cols)], weights_ref[i])
+    total = total.astype(low)
+    width = out_ref.shape[2]
+    for i in range(out_ref.shape[0]):
+        out_ref[i] = total[:, i * width : (i + 1) * width]
+
+
+def project_back(owners, sums, middle, upstream, gain, blocks):
+    rows, width = middle.shape
+    count = len(blocks)
+    depth, cols = blocks[0].shape
+    shapes = (
+        jax.ShapeDtypeStruct((rows, width), high),
+        jax.ShapeDtypeStruct((rows, width), low),
+        jax.ShapeDtypeStruct((1, width), high),
+        jax.ShapeDtypeStruct((count, rows, depth // count), low),
+    )
+    return pl.pallas_call(
+        functools.partial(project_back_kernel, sums.shape[0]),
+        out_shape=shapes,
+        in_specs=in_memory([pltpu.SMEM] + [pltpu.VMEM] * 4 + [pl.ANY] * count),
+        out_specs=in_memory([pltpu.VMEM] * len(shapes)),
+        scratch_shapes=[pltpu.VMEM((count, depth, cols), low), pltpu.SemaphoreType.DMA((count,))],
+        compiler_params=pltpu.CompilerParams(vmem_limit_bytes=vmem_bytes),
+        name="project_back",
+    )(owners, sums, middle, upstream, gain, *blocks)
+
+
+def arrange_kernel(piece, in_ref, gate_ref, up_ref):
+    count, _, width = in_ref.shape
+    hidden = width // 2
+    for half, out_ref in enumerate((gate_ref, up_ref)):
+        for layer in range(hidden // piece):
+            start = half * hidden + layer * piece
+            parts = [in_ref[i, :, start : start + piece].astype(high) for i in range(count)]
+            target = layer * count * piece
+            out_ref[:, target : target + count * piece] = jnp.concatenate(parts, axis=1)
+
+
+def arrange(grads, piece):
+    count, rows, width = grads.shape
+    shape = jax.ShapeDtypeStruct((rows, count * width // 2), high)
+    return pl.pallas_call(
+        functools.partial(arrange_kernel, piece),
+        out_shape=(shape, shape),
+        in_specs=in_memory([pltpu.VMEM]),
+        out_specs=in_memory([pltpu.VMEM] * 2),
+        compiler_params=pltpu.CompilerParams(vmem_limit_bytes=vmem_bytes),
+        name="arrange",
+    )(grads)
+
+
 CTX = ("chip", "core")
 LAYER = ("hi", "lo")
 
@@ -254,11 +332,17 @@
     return half, swap(half, "core")
 
 
-def scatter(keep, give):
+def sum_cores(keep, give):
+    return (keep.astype(high) + swap(give, "core").astype(high)).astype(low)
+
+
+def sum_chips(half):
+    return jnp.sum(send_chips(half).astype(high), axis=0)
+
+
+def send_chips(half):
     size = lax.axis_size("chip")
-    sums = (keep.astype(high) + swap(give, "core").astype(high)).astype(low)
-    sums = exchange(sums.reshape(size, keep.shape[0] // size, -1), "chip")
-    return jnp.sum(sums.astype(high), axis=0)
+    return exchange(half.reshape(size, half.shape[0] // size, -1), "chip")
 
 
 def spread(values, axis):
@@ -350,7 +434,6 @@
     own_tokens, attn_w = after(own_tokens, attn_w)
     layer = lax.axis_index(LAYER)
     attn_w = gather_rows(attn_w)
-    out_w, qkv_w = attn_w[:, :out_cols], attn_w[:, out_cols:]
 
     small = jnp.concatenate([norm_attn, norm_ffn, q_gain, k_gain]).reshape(1, -1)
     small = in_order(spread(small, LAYER), layer).astype(high)
@@ -367,7 +450,12 @@
     gate_up_w = jnp.concatenate(hidden_columns(w_gate) + hidden_columns(w_up), axis=1)
     down_w = rows_of(w_down, me, piece)
     token_half = exchange(jnp.broadcast_to(own_tokens, (chips, own, width)), "chip").reshape(-1, width)
-    token_half, gate_up_w, down_w = after(token_half, gate_up_w, down_w)
+    token_half, own_cotangent, gate_up_w, down_w = after(
+        token_half, own_cotangent, gate_up_w, down_w
+    )
+    upstream_half = in_order(spread(own_cotangent, "chip"), chip)
+    upstream_half, attn_w = after(upstream_half, attn_w)
+    out_w, qkv_w = attn_w[:, :out_cols], attn_w[:, out_cols:]
     token_parts = (token_half, swap(token_half, "core"))
     gate_up_w = gather_rows(gate_up_w)
     down_w = gather_rows(down_w)
@@ -416,9 +504,7 @@
         total, heads, sources, places, qkv_raw, *tables
     )
     mixed = exchange(mixed_abs.reshape(n, own, qw), CTX)
-    mixed, own_cotangent, *out_half = after(mixed, own_cotangent, *out_half)
     out_blocks = out_half + [swap(block, "core") for block in out_half]
-    upstream_half = in_order(spread(own_cotangent, "chip"), chip)
     mixed = mixed.transpose(1, 0, 2).reshape(own, n * qw)
     own_features = own_tokens.astype(high)
     branch = jnp.zeros((own, width), high)
@@ -439,7 +525,7 @@
         hidden_parts.append((silu * up).astype(low))
         gates.append((up * sigmoid * (1.0 + gate * (1.0 - sigmoid)), silu))
     grad_down = own_hidden(sum_parts(hidden_parts, upstream_parts))
-    grad_down, *upstream_parts = after(grad_down, *upstream_parts)
+    grad_down, down_w = after(grad_down, down_w)
     gate_up_grads = []
     for upstream_low, (gate_slope, silu) in zip(upstream_parts, gates):
         grad_hidden = dot_t(upstream_low, down_w)
@@ -447,68 +533,58 @@
         gate_up_grads.append(jnp.concatenate(grads, axis=1))
     grad_ffn = [dot_t(grads, gate_up_w).astype(low) for grads in gate_up_grads]
     grad_gate_up = by_layer(sum_parts(ffn_parts, gate_up_grads))
-    grad_ffn = scatter(grad_ffn[0], grad_ffn[1])
+    grad_ffn = send_chips(sum_cores(grad_ffn[0], grad_ffn[1]))
     grad_down = scatter_rows(grad_down)
     grad_ffn, grad_gate_up, grad_down = after(grad_ffn, grad_gate_up, grad_down)
     grad_gate_up = scatter_rows(grad_gate_up)
 
-    upstream = own_cotangent.astype(high)
-    scaled = gain_ffn * grad_ffn
-    inner = mean_last(middle * scaled)
-    grad_middle = upstream + factor_ffn * scaled - middle * factor_ffn**3 * inner
-    grad_gain_ffn = jnp.sum(grad_ffn * middle * factor_ffn, axis=0)
-    middle_low = grad_middle.astype(low)
-
-    mixed_grad = 0.0
-    for block_owner, block in zip(owners, out_blocks):
-        mixed_grad = mixed_grad + dot_t(columns_of(middle_low, block_owner, out_cols), block)
-    mixed_grad = mixed_grad.astype(low).reshape(own, n, qw).transpose(1, 0, 2)
+    grad_middle, middle_low, grad_gain_ffn, mixed_grad = project_back(
+        jnp.stack(owners), grad_ffn, middle, own_cotangent, gain_ffn.reshape(1, -1), out_blocks
+    )
     mixed_grad = exchange(mixed_grad, CTX).reshape(total, qw)
-    mixed_grad, late_low = after(mixed_grad, middle_low)
-    late_half = in_order(spread(late_low, "chip"), chip)
-    grad_out = sum_parts(halves(mixed_rel), (late_half, swap(late_half, "core")))
+    late_half = in_order(spread(middle_low, "chip"), chip)
     qkv_grad, grad_gains = attend_back(
         total, heads, sources, places, qkv_raw, *tables, query, key, value, logs, mixed_grad
     )
+    qkv_grad, late_half = after(qkv_grad, late_half)
+    grad_out = sum_parts(halves(mixed_rel), (late_half, swap(late_half, "core")))
     qkv_grads = halves(qkv_grad)
     grad_attn = [dot_t(grads, qkv_w).astype(low) for grads in qkv_grads]
-    grad_attn = scatter(grad_attn[0], grad_attn[1])
+    grad_attn = sum_chips(sum_cores(grad_attn[0], grad_attn[1]))
+    grad_qkv = sum_parts(normed_parts, qkv_grads).reshape(n, m * strip, -1)
+    grad_qkv = exchange(grad_qkv, CTX).reshape(n, m, strip, -1)
+
+    def all_heads(grads):
+        return grads.transpose(1, 2, 0, 3).reshape(m, strip, -1)
+
+    def grad_of_kv(grads):
+        grads = jnp.sum(grads.reshape(KVH, repeat, m, strip, HD).astype(high), axis=1)
+        return all_heads(grads.astype(low))
+
+    grad_late = [
+        all_heads(grad_qkv[..., :qw]),
+        grad_of_kv(grad_qkv[..., qw : qw + HD]),
+        grad_of_kv(grad_qkv[..., qw + HD :]),
+        grad_out.reshape(m, strip, width),
+    ]
+    grad_late = jnp.concatenate(grad_late, axis=2).reshape(m * strip, -1)
+    grad_late, *hidden_parts = after(grad_late, *hidden_parts)
+    block_parts = [dot(values, down_w).astype(low) for values in hidden_parts]
+    block_half = sum_cores(block_parts[0], block_parts[1])
+    block_sum = rows_of(block_half, chip, own).astype(high)
+    for mask in range(1, chips):
+        block_sum = block_sum + swap(rows_of(block_half, chip ^ mask, own), "chip", mask).astype(high)
+    block_out = (middle + block_sum).astype(low).reshape(tokens.shape)
+    grad_late = scatter_rows(grad_late)
+
+    grad_attn, grad_gate_up = after(grad_attn, grad_gate_up)
+    grad_gate_up = exchange(grad_gate_up.reshape(n, strip, -1), CTX)
     factor_attn = rms_factor(own_features)
     scaled = gain_attn * grad_attn
     inner = mean_last(own_features * scaled)
     input_grad = grad_middle + factor_attn * scaled - own_features * factor_attn**3 * inner
     grad_gain_attn = jnp.sum(grad_attn * own_features * factor_attn, axis=0)
     input_grad = input_grad.reshape(tokens.shape)
-
-    lanes = math.gcd((heads + 2) * HD, width)
-    grad_qkv = by_layer(sum_parts(normed_parts, qkv_grads))
-    grad_late = [grad_qkv.reshape(m, -1, lanes), grad_out.reshape(m, -1, lanes)]
-    grad_late = jnp.concatenate(grad_late, axis=1)
-    grad_attn, grad_gate_up, grad_late, *hidden_late = after(
-        grad_attn, grad_gate_up, grad_late, *hidden_parts
-    )
-    grad_late = scatter_rows(grad_late.reshape(-1, lanes))
-    block_parts = [dot(values, down_w).astype(low) for values in hidden_late]
-    block_out = middle + scatter(block_parts[0], block_parts[1])
-    block_out = block_out.astype(low).reshape(tokens.shape)
-
-    grad_down = grad_down.astype(high)
-    grad_gate_up = exchange(grad_gate_up.reshape(n, strip, -1), CTX).astype(high)
-    grad_gate_up = grad_gate_up.reshape(n, strip, 2, m, piece).transpose(2, 1, 3, 0, 4)
-    grad_gate_up = grad_gate_up.reshape(2, strip, -1)
-
-    late_rows = n * strip * (heads + 2) * HD // lanes
-    grad_qkv, grad_out = grad_late[:late_rows], grad_late[late_rows:]
-    grad_out = grad_out.reshape(-1, width).astype(high)
-    grad_qkv = exchange(grad_qkv.reshape(n, strip, -1), CTX).astype(high)
-    grad_query = grad_qkv[:, :, :qw].transpose(1, 0, 2).reshape(strip, -1)
-
-    def grad_of_kv(grads):
-        grads = jnp.sum(grads.reshape(KVH, repeat, strip, HD), axis=1)
-        return grads.transpose(1, 0, 2).reshape(strip, -1)
-
-    grad_key = grad_of_kv(grad_qkv[:, :, qw : qw + HD])
-    grad_value = grad_of_kv(grad_qkv[:, :, qw + HD :])
 
     devices = n * m
     partial = jnp.concatenate(
@@ -520,7 +596,17 @@
         ],
         axis=1,
     )
-    gains = jnp.sum(exchange(partial, CTX + LAYER), axis=0)
+    grad_gate_up, partial = after(grad_gate_up, partial)
+    gains = exchange(partial, CTX + LAYER)
+    gains = jnp.sum(gains, axis=0)
+    grad_down = grad_down.astype(high)
+    grad_gate, grad_up = arrange(grad_gate_up, piece)
+    grad_late, gains = after(grad_late, gains)
+    ends = [0, n * qw, n * qw + KVH * HD, n * qw + 2 * KVH * HD, grad_late.shape[1]]
+    grad_query, grad_key, grad_value, grad_out = [
+        grad_late[:, start:end].astype(high) for start, end in zip(ends, ends[1:])
+    ]
+
     end = 2 * strip + HD // devices
     return (
         block_out,
@@ -533,8 +619,8 @@
         gains[end:],
         grad_out,
         gains[strip : 2 * strip],
-        grad_gate_up[0],
-        grad_gate_up[1],
+        grad_gate,
+        grad_up,
         grad_down,
     )
 

time: 551 us -> 527 us (0.956)
  blocking collectives: 55.5 us -> 29.5 us
  starting transfers between devices: 63.1 us -> 81.1 us
  local copies, waits for them, and re-layouts: 80.4 us -> 70.5 us
  Pallas kernels: 19.7 us -> 27.8 us
  waiting for transfers between devices: 171 us -> 163 us
    all_to_all x3 -> x1, blocking collectives: 55.5 us -> 29.5 us  [exchange(): return lax.all_to_all(values, axis, 0, 0, tiled=True)]
    all_to_all x7 -> x8, waiting for transfers between devices: 82.8 us -> 107 us  [exchange(): return lax.all_to_all(values, axis, 0, 0, tiled=True)]
    ppermute x23 -> x26, waiting for transfers between devices: 39.3 us -> 24.4 us  [swap(): return lax.ppermute(values, axis, [(i, i ^ mask) for i in range(size)])]
    all_to_all x7 -> x8, starting transfers between devices: 30.4 us -> 40.9 us  [exchange(): return lax.all_to_all(values, axis, 0, 0, tiled=True)]
    slice x4 -> x2, local copies, waits for them, and re-layouts: 10.2 us -> 0.38 us  [the longest x1 0.29 us: local(): grad_qkv[..., qw:qw + HD]]
    reduce_scatter x3, waiting for transfers between devices: 14.2 us -> 5.32 us  [scatter_rows(): return lax.psum_scatter(values, LAYER, scatter_dimension=0, tiled=True)]
    unnamed x101 -> x106, local copies, waits for them, and re-layouts: 9.78 us -> 18.3 us
    all_gather x3, waiting for transfers between devices: 19.4 us -> 11 us  [gather_rows(): return lax.all_gather(values, LAYER, axis=0, tiled=True)]
  transfers between devices with their start and end apart: 40 -> 44, of which waited for: 17 -> 20; matrix products, arithmetic and copies ran while one was open for 37% -> 34% of each run, Pallas kernels for 4% -> 5%
where the time goes in v3:
time: 527 us; the launch traced here: 519 us
  waiting for transfers between devices  163 us (31%)
  matrix products  103 us (20%)
  starting transfers between devices  81.1 us (15%)
  local copies, waits for them, and re-layouts  70.5 us (13%)
  blocking collectives  29.5 us (6%)
  other arithmetic  28.1 us (5%)
  Pallas kernels  27.8 us (5%)
  between operations  15.6 us (3%)
    all_to_all x8, waiting for transfers between devices, exchange(): return lax.all_to_all(values, axis, 0, 0, tiled=True)  107 us
    all_to_all x8, starting transfers between devices, exchange(): return lax.all_to_all(values, axis, 0, 0, tiled=True)  40.9 us
    dot_general x14, matrix products, dot(): return jnp.dot(left, right, preferred_element_type=high)  40 us
    dot_general x8, matrix products, t_dot(): lax.dot_general(left, right, (((0,), (0,)), ((), ())), preferred_element_...  36.6 us
    all_to_all x1, blocking collectives, exchange(): return lax.all_to_all(values, axis, 0, 0, tiled=True)  29.5 us
    dot_general x6, matrix products, dot_t(): lax.dot_general(left, right, (((1,), (1,)), ((), ())), preferred_element_...  26.4 us
    ppermute x26, starting transfers between devices, swap(): return lax.ppermute(values, axis, [(i, i ^ mask) for i in range(size)])  25 us
    ppermute x26, waiting for transfers between devices, swap(): return lax.ppermute(values, axis, [(i, i ^ mask) for i in range(size)])  24.4 us
  transfers between devices with their start and end apart: 44, of which 20 were waited for; matrix products, arithmetic and copies ran while one was open for 34% of the time, Pallas kernels for 5%

profile of v3, /device:TPU:0, one launch (start us, length us, event | category | flops | bytes accessed | tf_op | source)
XLA Modules:
  0.0 519.2 jit_solution(16551362457006481683)
XLA Ops:
  12.0 5.3 %all-to-all-start = ((bf16[4,128,2048]{2,1,0:T(8,128)(2,1)}), bf16[4,128,2048]{2,1,0:T(8,128)(2,1)}, u32[]{:S(2)}, u32[]{:S(2)}) async-start(bf16[4,128,2048]{2,1,0:T(8,128)(2,1)} %broadcast_in_dim.11), calls=%async_computation | async-start | bytes 4194304 | tf_op jit(solution)/shard_map/all_to_all | solution.py:326
  32.2 10.8 %all-to-all-done = bf16[4,128,2048]{2,1,0:T(8,128)(2,1)} async-done(((bf16[4,128,2048]{2,1,0:T(8,128)(2,1)}), bf16[4,128,2048]{2,1,0:T(8,128)(2,1)}, u32[]{:S(2)}, u32[]{:S(2)}) %all-to-all-start) | async-done | bytes 2097184 | tf_op jit(solution)/shard_map/all_to_all | solution.py:326
  52.5 6.7 %collective-permute-done.3 = bf16[128,2048]{1,0:T(8,128)(2,1)} collective-permute-done((bf16[128,2048]{1,0:T(8,128)(2,1)S(1)}, bf16[128,2048]{1,0:T(8,128)(2,1)}, u32[]{:S(2)}, u32[]{:S(2)}) %collective-permute-start.3) | collective-permute-done | bytes 524320 | tf_op jit(solution)/shard_map/ppermute | solution.py:322
  61.1 10.1 %collective-permute-done.4 = bf16[128,2048]{1,0:T(8,128)(2,1)S(1)} collective-permute-done((bf16[128,2048]{1,0:T(8,128)(2,1)S(1)}, bf16[128,2048]{1,0:T(8,128)(2,1)S(1)}, u32[]{:S(2)}, u32[]{:S(2)}) %collective-permute-start.4) | collective-permute-done | bytes 524320 | tf_op jit(solution)/shard_map/ppermute | solution.py:322
  91.1 8.8 %attend.1 = (bf16[1024,256]{1,0:T(8,128)(2,1)S(1)}, bf16[1024,256]{1,0:T(8,128)(2,1)S(1)}, bf16[1024,256]{1,0:T(8,128)(2,1)S(1)}, bf16[1024,128]{1,0:T(8,128)(2,...) custom-call(s32[16]{0:T(128)S(1)} %get-tuple-element.188.sources_ref, ...), custom_call_target="tpu_custom_call" | custom-call | tf_op jit(solution)/shard_map/attend/pallas_call | solution.py:208
  110.5 23.0 %all-to-all-done.1 = bf16[8,128,256]{1,2,0:T(8,128)(2,1)} async-done(((bf16[8,128,256]{1,2,0:T(8,128)(2,1)}), bf16[8,128,256]{1,2,0:T(8,128)(2,1)}, u32[]{:S(2)}, u32[]{:S(2)}) %all-to-all-start.1) | async-done | bytes 524320 | tf_op jit(solution)/shard_map/all_to_all | solution.py:326
  149.8 29.5 %all_to_all.49 = bf16[4,128,2048]{2,1,0:T(8,128)(2,1)} all-to-all(bf16[4,128,2048]{2,1,0:T(8,128)(2,1)S(1)} %broadcast_in_dim.14), channel_id=1, replica_groups=mesh['chip'=4,'core'=2,'hi'=2,'lo'=2] {'chip'}, dimensions={0} | all-to-all | bytes 4194304 | tf_op jit(solution)/shard_map/all_to_all | solution.py:326
  183.8 9.2 %all-gather.6.cloned.1.call-done = bf16[2048,1536]{1,0:T(8,128)(2,1)} async-done(((bf16[512,1536]{1,0:T(8,128)(2,1)}), bf16[2048,1536]{1,0:T(8,128)(2,1)}) %all-gather.6.cloned.1.call-update) | async-done | bytes 6291472 | tf_op jit(solution)/shard_map/all_gather | solution.py:382
  193.0 6.3 %fusion.47 = f32[512,1536]{1,0:T(8,128)S(1)} fusion(bf16[512,2048]{1,0:T(8,128)(2,1)} %collective-permute-done.14, bf16[2048,1536]{1,0:T(8,128)(2,1)} %all-gather.6.cloned.1.call-done), kind=kOutput, calls=%fused_computation.150 | convolution fusion | flops 3221225472 | bytes 11534336 | tf_op jit(solution)/shard_map/dot_general | solution.py:26
  201.6 5.4 %fusion.46 = f32[512,1536]{1,0:T(8,128)S(1)} fusion(bf16[512,2048]{1,0:T(8,128)(2,1)} %bitcast.17, bf16[2048,1536]{1,0:T(8,128)(2,1)S(1)} %copy-done.37), kind=kOutput, calls=%fused_computation.149 | convolution fusion | flops 3221225472 | bytes 11534336 | tf_op jit(solution)/shard_map/dot_general | solution.py:26
  217.5 7.4 %collective-permute-start.16 = (bf16[192,2048]{1,0:T(8,128)(2,1)}, bf16[192,2048]{1,0:T(8,128)(2,1)}, u32[]{:S(2)}, u32[]{:S(2)}) collective-permute-start(bf16[192,2048]{1,0:T(8,128)(2,1)} %get-tuple-element.162), channel_id=1, source_target_pairs={{0,0},{4,8},{8,16},{12,24},{16,4},{20,12},{24,20},{28,28},{1,1},{5... | collective-permute-start | bytes 2359304 | tf_op jit(solution)/shard_map/ppermute | solution.py:474
  235.9 11.2 %collective-permute-done.17 = bf16[192,2048]{1,0:T(8,128)(2,1)} collective-permute-done((bf16[192,2048]{1,0:T(8,128)(2,1)}, bf16[192,2048]{1,0:T(8,128)(2,1)}, u32[]{:S(2)}, u32[]{:S(2)}) %collective-permute-start.17) | collective-permute-done | bytes 786464 | tf_op jit(solution)/shard_map/ppermute | solution.py:474
  257.6 5.6 %multiply_convert_fusion.1 = (bf16[512,768]{1,0:T(8,128)(2,1)S(1)}, bf16[512,768]{1,0:T(8,128)(2,1)S(1)}) fusion(f32[512,1536]{1,0:T(8,128)} %copy-done.26, bf16[512,2048]{1,0:T(8,128)(2,1)} %collective-permute-done.15, bf16[768,2048]{1,0:T(8,128)(2,1)} %all-gather.8.cloned.1.call-done), kind=kOutput, calls=%fused_computation.36 | convolution fusion | flops 1615724544 | bytes 9961472 | tf_op jit(solution)/shard_map/dot_general | solution.py:30
  264.5 6.6 %convolution_convert_fusion.4 = bf16[512,2048]{1,0:T(8,128)(2,1)S(1)} fusion(bf16[2048,1536]{1,0:T(8,128)(2,1)} %all-gather.6.cloned.1.call-done, bf16[512,768]{1,0:T(8,128)(2,1)S(1)} %get-tuple-element.158, bf16[512,768]{1,0:T(8,128)(2,1)S(1)} %get-tuple-element.157), kind=kOutput, calls=%fused_computation.23 | convolution fusion | flops 3225419776 | bytes 9961472 | tf_op jit(solution)/shard_map/dot_general | solution.py:30
  286.8 10.2 %fusion.21 = f32[2048,1536]{1,0:T(8,128)} fusion(bf16[512,2048]{1,0:T(8,128)(2,1)} %bitcast.17, bf16[512,768]{1,0:T(8,128)(2,1)} %copy-done.41, bf16[512,768]{1,0:T(8,128)(2,1)} %copy-done.40), kind=kOutput, calls=%fused_computation.68 | convolution fusion | flops 3224371200 | bytes 16252928 | tf_op jit(solution)/shard_map/dot_general | solution.py:34
  296.9 7.4 %add_convert_fusion = bf16[2048,1536]{1,0:T(8,128)(2,1)S(1)} fusion(f32[2048,1536]{1,0:T(8,128)} %fusion.21, bf16[512,2048]{1,0:T(8,128)(2,1)} %collective-permute-done.14, bf16[512,768]{1,0:T(8,128)(2,1)S(1)} %copy-done.45, bf16[512,768]{1,0:T(8,128)(2,1)S(1)} %copy-done.43), kind=kOutput, calls=%fused_computation | convolution fusion | flops 3230662656 | bytes 22544384 | tf_op jit(solution)/shard_map/dot_general | solution.py:34
  307.6 5.4 %all-to-all-done.3.refs_1_ = bf16[4,128,2048]{2,1,0:T(8,128)(2,1)} async-done(((bf16[4,128,2048]{2,1,0:T(8,128)(2,1)}), bf16[4,128,2048]{2,1,0:T(8,128)(2,1)}, u32[]{:S(2)}, u32[]{:S(2)}) %all-to-all-start.3) | async-done | bytes 2097184 | tf_op jit(solution)/shard_map/all_to_all | solution.py:326
  319.7 6.3 %project_back.1 = (f32[128,2048]{1,0:T(8,128)S(1)}, bf16[128,2048]{1,0:T(8,128)(2,1)}, f32[1,2048]{1,0:T(1,128)S(1)}, bf16[8,128,256]{2,1,0:T(8,128)(2,1)S(1)}) custom-call(s32[8]{0:T(128)S(1)} %stack.35.refs_0_, bf16[4,128,2048]{2,1,0:T(8,128)(2,1)} %all-to-all-done.3.refs_1_, f32[128,2048]{1,0:T(8,128)S(1)} %get-tuple-element.146.refs_2_, ...), custom_call_target="tpu_custom_call" | custom-call | tf_op jit(solution)/shard_map/project_back/pallas_call | solution.py:281
  340.1 9.4 %all-to-all-done.4 = bf16[8,128,256]{2,1,0:T(8,128)(2,1)S(1)} async-done(((bf16[8,128,256]{2,1,0:T(8,128)(2,1)}), bf16[8,128,256]{2,1,0:T(8,128)(2,1)S(1)}, u32[]{:S(2)}, u32[]{:S(2)}) %all-to-all-start.4) | async-done | bytes 524320 | tf_op jit(solution)/shard_map/all_to_all | solution.py:326
  352.5 10.7 %attend_back.1 = (bf16[1024,512]{1,0:T(8,128)(2,1)S(1)}, f32[2,128]{1,0:T(2,128)S(1)}) custom-call(s32[16]{0:T(128)S(1)} %get-tuple-element.188.sources_ref, s32[16]{0:T(128)S(1)} %get-tuple-element.187.places_ref, f32[1024,512]{1,0:T(8,128)} %pad_maximum_fusion.1.raw_ref, f32[1024,128]{1,0:T(8,128)S(1)} %get-tuple-element.197.cos_ref, ...), custom_call_target="tpu_custom_call" | custom-call | tf_op jit(solution)/shard_map/attend_back/pallas_call | solution.py:223
  381.0 25.9 %all-to-all-done.5 = bf16[8,256,512]{2,1,0:T(8,128)(2,1)S(1)} async-done(((bf16[8,256,512]{2,1,0:T(8,128)(2,1)}), bf16[8,256,512]{2,1,0:T(8,128)(2,1)S(1)}, u32[]{:S(2)}, u32[]{:S(2)}) %all-to-all-start.5) | async-done | bytes 2097184 | tf_op jit(solution)/shard_map/all_to_all | solution.py:326
  440.0 17.4 %all-to-all-done.6 = bf16[4,128,2048]{2,1,0:T(8,128)(2,1)S(1)} async-done(((bf16[4,128,2048]{2,1,0:T(8,128)(2,1)}), bf16[4,128,2048]{2,1,0:T(8,128)(2,1)S(1)}, u32[]{:S(2)}, u32[]{:S(2)}) %all-to-all-start.6) | async-done | bytes 2097184 | tf_op jit(solution)/shard_map/all_to_all | solution.py:326
  458.8 13.3 %all-to-all-start.7 = ((bf16[8,64,1536]{2,1,0:T(8,128)(2,1)}), bf16[8,64,1536]{2,1,0:T(8,128)(2,1)S(1)}, u32[]{:S(2)}, u32[]{:S(2)}) async-start(bf16[8,64,1536]{2,1,0:T(8,128)(2,1)} %bitcast.124), calls=%async_computation.10 | async-start | bytes 3145728 | tf_op jit(solution)/shard_map/all_to_all | solution.py:326
  483.7 12.6 %all-to-all-done.7.in_ref = bf16[8,64,1536]{2,1,0:T(8,128)(2,1)S(1)} async-done(((bf16[8,64,1536]{2,1,0:T(8,128)(2,1)}), bf16[8,64,1536]{2,1,0:T(8,128)(2,1)S(1)}, u32[]{:S(2)}, u32[]{:S(2)}) %all-to-all-start.7) | async-done | bytes 1572896 | tf_op jit(solution)/shard_map/all_to_all | solution.py:326
  (292 shorter events, 238.9 us)
Async XLA Ops:
  7.2 69.6 %all-gather.4.cloned.1.call-start = ((), (), s32[]{:S(2)}) async-start(), calls=%async_computation.12 | async-start | bytes 3932160 | tf_op jit(solution)/shard_map/all_gather | solution.py:382
  12.0 31.0 %all-to-all-start = ((bf16[4,128,2048]{2,1,0:T(8,128)(2,1)}), bf16[4,128,2048]{2,1,0:T(8,128)(2,1)}, u32[]{:S(2)}, u32[]{:S(2)}) async-start(bf16[4,128,2048]{2,1,0:T(8,128)(2,1)} %broadcast_in_dim.11), calls=%async_computation | async-start | bytes 4194304 | tf_op jit(solution)/shard_map/all_to_all | solution.py:326
  17.3 175.7 %all-gather.6.cloned.1.call-start = ((), (), s32[]{:S(2)}) async-start(), calls=%async_computation.13 | async-start | bytes 7864320 | tf_op jit(solution)/shard_map/all_gather | solution.py:382
  43.0 29.9 %collective-permute-start.6 = (bf16[512,2048]{1,0:T(8,128)(2,1)}, bf16[512,2048]{1,0:T(8,128)(2,1)}, u32[]{:S(2)}, u32[]{:S(2)}) collective-permute-start(bf16[512,2048]{1,0:T(8,128)(2,1)} %bitcast.1), channel_id=1, source_target_pairs={{0,4},{4,0},{1,5},{5,1},{2,6},{6,2},{3,7},{7,3},{8,12},{12,8},{9,1... | collective-permute-start | bytes 6291464 | tf_op jit(solution)/shard_map/ppermute | solution.py:322
  79.1 56.4 %collective-permute-start.7 = (bf16[2048,256]{1,0:T(8,128)(2,1)}, bf16[2048,256]{1,0:T(8,128)(2,1)S(1)}, u32[]{:S(2)}, u32[]{:S(2)}) collective-permute-start(bf16[2048,256]{1,0:T(8,128)(2,1)} %slice.85.refs_5_), channel_id=1, source_target_pairs={{0,8},{8,0},{16,24},{24,16},{1,9},{9,1},{17,25},{25,17},{2,10},{10... | collective-permute-start | bytes 3145736 | tf_op jit(solution)/shard_map/ppermute | solution.py:322
  80.6 55.0 %collective-permute-start.8 = (bf16[2048,256]{1,0:T(8,128)(2,1)}, bf16[2048,256]{1,0:T(8,128)(2,1)}, u32[]{:S(2)}, u32[]{:S(2)}) collective-permute-start(bf16[2048,256]{1,0:T(8,128)(2,1)} %slice.85.refs_5_), channel_id=1, source_target_pairs={{0,16},{8,24},{16,0},{24,8},{1,17},{9,25},{17,1},{25,9},{2,18},{10... | collective-permute-start | bytes 3145736 | tf_op jit(solution)/shard_map/ppermute | solution.py:322
  82.1 54.0 %collective-permute-start.9 = (bf16[2048,256]{1,0:T(8,128)(2,1)}, bf16[2048,256]{1,0:T(8,128)(2,1)}, u32[]{:S(2)}, u32[]{:S(2)}) collective-permute-start(bf16[2048,256]{1,0:T(8,128)(2,1)} %slice.85.refs_5_), channel_id=1, source_target_pairs={{0,24},{8,16},{16,8},{24,0},{1,25},{9,17},{17,9},{25,1},{2,26},{10... | collective-permute-start | bytes 3145736 | tf_op jit(solution)/shard_map/ppermute | solution.py:322
  110.1 147.5 %all-gather.8.cloned.1.call-start = ((), (), s32[]{:S(2)}) async-start(), calls=%async_computation.14 | async-start | bytes 3932160 | tf_op jit(solution)/shard_map/all_gather | solution.py:382
  110.2 30.9 %collective-permute-start.10 = (bf16[2048,256]{1,0:T(8,128)(2,1)}, bf16[2048,256]{1,0:T(8,128)(2,1)}, u32[]{:S(2)}, u32[]{:S(2)}) collective-permute-start(bf16[2048,256]{1,0:T(8,128)(2,1)} %slice.85.refs_5_), channel_id=1, source_target_pairs={{0,4},{4,0},{1,5},{5,1},{2,6},{6,2},{3,7},{7,3},{8,12},{12,8},{9,1... | collective-permute-start | bytes 3145736 | tf_op jit(solution)/shard_map/ppermute | solution.py:322
  179.3 139.0 %reduce-scatter.4.cloned.1.call-start = ((), (), s32[]{:S(2)}) async-start(), calls=%async_computation.15 | async-start | bytes 3932160 | tf_op jit(solution)/shard_map/reduce_scatter | solution.py:386
  226.9 28.5 %collective-permute-start.19 = (bf16[192,2048]{1,0:T(8,128)(2,1)}, bf16[192,2048]{1,0:T(8,128)(2,1)}, u32[]{:S(2)}, u32[]{:S(2)}) collective-permute-start(bf16[192,2048]{1,0:T(8,128)(2,1)} %get-tuple-element.159), channel_id=1, source_target_pairs={{0,24},{4,0},{8,8},{12,16},{16,28},{20,4},{24,12},{28,20},{1,25},{... | collective-permute-start | bytes 2359304 | tf_op jit(solution)/shard_map/ppermute | solution.py:474
  281.7 31.3 %all-to-all-start.3 = ((bf16[4,128,2048]{2,1,0:T(8,128)(2,1)}), bf16[4,128,2048]{2,1,0:T(8,128)(2,1)}, u32[]{:S(2)}, u32[]{:S(2)}) async-start(bf16[4,128,2048]{2,1,0:T(8,128)(2,1)} %bitcast.120), calls=%async_computation.3 | async-start | bytes 4194304 | tf_op jit(solution)/shard_map/all_to_all | solution.py:326
  286.2 172.6 %reduce-scatter.6.cloned.1.call-start = ((), (), s32[]{:S(2)}) async-start(), calls=%async_computation.16 | async-start | bytes 7864320 | tf_op jit(solution)/shard_map/reduce_scatter | solution.py:386
  327.8 35.4 %collective-permute-start.21 = (bf16[128,2048]{1,0:T(8,128)(2,1)}, bf16[128,2048]{1,0:T(8,128)(2,1)}, u32[]{:S(2)}, u32[]{:S(2)}) collective-permute-start(bf16[128,2048]{1,0:T(8,128)(2,1)} %get-tuple-element.69), channel_id=1, source_target_pairs={{0,8},{8,0},{16,24},{24,16},{1,9},{9,1},{17,25},{25,17},{2,10},{10... | collective-permute-start | bytes 1572872 | tf_op jit(solution)/shard_map/ppermute | solution.py:322
  333.0 32.5 %collective-permute-start.22 = (bf16[128,2048]{1,0:T(8,128)(2,1)}, bf16[128,2048]{1,0:T(8,128)(2,1)}, u32[]{:S(2)}, u32[]{:S(2)}) collective-permute-start(bf16[128,2048]{1,0:T(8,128)(2,1)} %get-tuple-element.69), channel_id=1, source_target_pairs={{0,16},{8,24},{16,0},{24,8},{1,17},{9,25},{17,1},{25,9},{2,18},{10... | collective-permute-start | bytes 1572872 | tf_op jit(solution)/shard_map/ppermute | solution.py:322
  335.0 32.4 %collective-permute-start.23 = (bf16[128,2048]{1,0:T(8,128)(2,1)}, bf16[128,2048]{1,0:T(8,128)(2,1)}, u32[]{:S(2)}, u32[]{:S(2)}) collective-permute-start(bf16[128,2048]{1,0:T(8,128)(2,1)} %get-tuple-element.69), channel_id=1, source_target_pairs={{0,24},{8,16},{16,8},{24,0},{1,25},{9,17},{17,9},{25,1},{2,26},{10... | collective-permute-start | bytes 1572872 | tf_op jit(solution)/shard_map/ppermute | solution.py:322
  376.7 30.2 %all-to-all-start.5 = ((bf16[8,256,512]{2,1,0:T(8,128)(2,1)}), bf16[8,256,512]{2,1,0:T(8,128)(2,1)S(1)}, u32[]{:S(2)}, u32[]{:S(2)}) async-start(bf16[8,256,512]{2,1,0:T(8,128)(2,1)} %bitcast.121), calls=%async_computation.6 | async-start | bytes 4194304 | tf_op jit(solution)/shard_map/all_to_all | solution.py:326
  380.3 126.8 %reduce-scatter.8.cloned.1.call-start = ((), (), s32[]{:S(2)}) async-start(), calls=%async_computation.17 | async-start | bytes 3932160 | tf_op jit(solution)/shard_map/reduce_scatter | solution.py:386
  380.6 28.5 %collective-permute-start.24 = (bf16[512,2048]{1,0:T(8,128)(2,1)}, bf16[512,2048]{1,0:T(8,128)(2,1)}, u32[]{:S(2)}, u32[]{:S(2)}) collective-permute-start(bf16[512,2048]{1,0:T(8,128)(2,1)} %constant_dynamic-update-slice_fusion), channel_id=1, source_target_pairs={{0,4},{4,0},{1,5},{5,1},{2,6},{6,2},{3,7},{7,3},{8,12},{12,8},{9,1... | collective-permute-start | bytes 6291464 | tf_op jit(solution)/shard_map/ppermute | solution.py:322
  427.0 30.5 %all-to-all-start.6 = ((bf16[4,128,2048]{2,1,0:T(8,128)(2,1)}), bf16[4,128,2048]{2,1,0:T(8,128)(2,1)S(1)}, u32[]{:S(2)}, u32[]{:S(2)}) async-start(bf16[4,128,2048]{2,1,0:T(8,128)(2,1)} %bitcast.119), calls=%async_computation.7 | async-start | bytes 4194304 | tf_op jit(solution)/shard_map/all_to_all | solution.py:326
  436.5 39.6 %collective-permute-start.28 = (bf16[128,2048]{1,0:T(8,128)(2,1)}, bf16[128,2048]{1,0:T(8,128)(2,1)}, u32[]{:S(2)}, u32[]{:S(2)}) collective-permute-start(bf16[128,2048]{1,0:T(8,128)(2,1)} %get-tuple-element.164), channel_id=1, source_target_pairs={{0,24},{8,16},{16,8},{24,0},{1,25},{9,17},{17,9},{25,1},{2,26},{10... | collective-permute-start | bytes 1572872 | tf_op jit(solution)/shard_map/ppermute | solution.py:322
  439.3 40.0 %collective-permute-start.27 = (bf16[128,2048]{1,0:T(8,128)(2,1)}, bf16[128,2048]{1,0:T(8,128)(2,1)}, u32[]{:S(2)}, u32[]{:S(2)}) collective-permute-start(bf16[128,2048]{1,0:T(8,128)(2,1)} %get-tuple-element.165), channel_id=1, source_target_pairs={{0,16},{8,24},{16,0},{24,8},{1,17},{9,25},{17,1},{25,9},{2,18},{10... | collective-permute-start | bytes 1572872 | tf_op jit(solution)/shard_map/ppermute | solution.py:322
  439.9 39.5 %collective-permute-start.26 = (bf16[128,2048]{1,0:T(8,128)(2,1)}, bf16[128,2048]{1,0:T(8,128)(2,1)}, u32[]{:S(2)}, u32[]{:S(2)}) collective-permute-start(bf16[128,2048]{1,0:T(8,128)(2,1)} %get-tuple-element.163), channel_id=1, source_target_pairs={{0,8},{8,0},{16,24},{24,16},{1,9},{9,1},{17,25},{25,17},{2,10},{10... | collective-permute-start | bytes 1572872 | tf_op jit(solution)/shard_map/ppermute | solution.py:322
  458.8 37.5 %all-to-all-start.7 = ((bf16[8,64,1536]{2,1,0:T(8,128)(2,1)}), bf16[8,64,1536]{2,1,0:T(8,128)(2,1)S(1)}, u32[]{:S(2)}, u32[]{:S(2)}) async-start(bf16[8,64,1536]{2,1,0:T(8,128)(2,1)} %bitcast.124), calls=%async_computation.10 | async-start | bytes 3145728 | tf_op jit(solution)/shard_map/all_to_all | solution.py:326
  (68 other events, 546.2 us)
Sparse Core Ops, SparseCore 0:
  10.5 66.2 all-gather.3
  78.9 114.0 all-gather.5
  194.6 61.7 all-gather.7
  258.5 59.7 reduce-scatter.3
  320.5 110.7 reduce-scatter.5
  433.5 60.7 reduce-scatter.7

commit v4 on v3

--- a/solution.py
+++ b/solution.py
@@ -337,7 +337,13 @@
 
 
 def sum_chips(half):
-    return jnp.sum(send_chips(half).astype(high), axis=0)
+    size = lax.axis_size("chip")
+    chip = lax.axis_index("chip")
+    rows = half.shape[0] // size
+    total = rows_of(half, chip, rows).astype(high)
+    for mask in range(1, size):
+        total = total + swap(rows_of(half, chip ^ mask, rows), "chip", mask).astype(high)
+    return total
 
 
 def send_chips(half):
@@ -571,10 +577,7 @@
     grad_late, *hidden_parts = after(grad_late, *hidden_parts)
     block_parts = [dot(values, down_w).astype(low) for values in hidden_parts]
     block_half = sum_cores(block_parts[0], block_parts[1])
-    block_sum = rows_of(block_half, chip, own).astype(high)
-    for mask in range(1, chips):
-        block_sum = block_sum + swap(rows_of(block_half, chip ^ mask, own), "chip", mask).astype(high)
-    block_out = (middle + block_sum).astype(low).reshape(tokens.shape)
+    block_out = (middle + sum_chips(block_half)).astype(low).reshape(tokens.shape)
     grad_late = scatter_rows(grad_late)
 
     grad_attn, grad_gate_up = after(grad_attn, grad_gate_up)

time: 527 us -> 522 us (level)
  waiting for transfers between devices: 163 us -> 175 us
  starting transfers between devices: 81.1 us -> 70.3 us
  matrix products: 103 us -> 97.6 us
    ppermute x26 -> x29, waiting for transfers between devices: 24.4 us -> 53.2 us  [swap(): return lax.ppermute(values, axis, [(i, i ^ mask) for i in range(size)])]
    all_to_all x8 -> x7, waiting for transfers between devices: 107 us -> 89.9 us  [exchange(): return lax.all_to_all(values, axis, 0, 0, tiled=True)]
    all_to_all x8 -> x7, starting transfers between devices: 40.9 us -> 27.5 us  [exchange(): return lax.all_to_all(values, axis, 0, 0, tiled=True)]
    ppermute x26 -> x29, starting transfers between devices: 25 us -> 27.6 us  [swap(): return lax.ppermute(values, axis, [(i, i ^ mask) for i in range(size)])]
    unnamed x106 -> x108, local copies, waits for them, and re-layouts: 18.3 us -> 18.3 us
  transfers between devices with their start and end apart: 44 -> 46, of which waited for: 20 -> 21; matrix products, arithmetic and copies ran while one was open for 34% -> 33% of each run, Pallas kernels for 5% -> 5%
where the time goes in v4:
time: 522 us; the launch traced here: 514 us
  waiting for transfers between devices  175 us (34%)
  matrix products  97.6 us (19%)
  local copies, waits for them, and re-layouts  70.6 us (14%)
  starting transfers between devices  70.3 us (13%)
  blocking collectives  29.5 us (6%)
  other arithmetic  28.1 us (5%)
  Pallas kernels  27.7 us (5%)
  between operations  15.7 us (3%)
    all_to_all x7, waiting for transfers between devices, exchange(): return lax.all_to_all(values, axis, 0, 0, tiled=True)  89.9 us
    ppermute x29, waiting for transfers between devices, swap(): return lax.ppermute(values, axis, [(i, i ^ mask) for i in range(size)])  53.2 us
    dot_general x8, matrix products, t_dot(): lax.dot_general(left, right, (((0,), (0,)), ((), ())), preferred_element_...  36.7 us
    dot_general x14, matrix products, dot(): return jnp.dot(left, right, preferred_element_type=high)  35.9 us
    all_to_all x1, blocking collectives, exchange(): return lax.all_to_all(values, axis, 0, 0, tiled=True)  29.5 us
    ppermute x29, starting transfers between devices, swap(): return lax.ppermute(values, axis, [(i, i ^ mask) for i in range(size)])  27.6 us
    all_to_all x7, starting transfers between devices, exchange(): return lax.all_to_all(values, axis, 0, 0, tiled=True)  27.5 us
    dot_general x6, matrix products, dot_t(): lax.dot_general(left, right, (((1,), (1,)), ((), ())), preferred_element_...  25.1 us
  transfers between devices with their start and end apart: 46, of which 21 were waited for; matrix products, arithmetic and copies ran while one was open for 33% of the time, Pallas kernels for 5%

profile of v4, /device:TPU:0, one launch (start us, length us, event | category | flops | bytes accessed | tf_op | source)
XLA Modules:
  0.0 514.3 jit_solution(1088303581188429131)
XLA Ops:
  32.2 10.9 %all-to-all-done = bf16[4,128,2048]{2,1,0:T(8,128)(2,1)} async-done(((bf16[4,128,2048]{2,1,0:T(8,128)(2,1)}), bf16[4,128,2048]{2,1,0:T(8,128)(2,1)}, u32[]{:S(2)}, u32[]{:S(2)}) %all-to-all-start) | async-done | bytes 2097184 | tf_op jit(solution)/shard_map/all_to_all | solution.py:326
  52.5 6.8 %collective-permute-done.3 = bf16[128,2048]{1,0:T(8,128)(2,1)} collective-permute-done((bf16[128,2048]{1,0:T(8,128)(2,1)S(1)}, bf16[128,2048]{1,0:T(8,128)(2,1)}, u32[]{:S(2)}, u32[]{:S(2)}) %collective-permute-start.3) | collective-permute-done | bytes 524320 | tf_op jit(solution)/shard_map/ppermute | solution.py:322
  61.1 10.1 %collective-permute-done.4 = bf16[128,2048]{1,0:T(8,128)(2,1)S(1)} collective-permute-done((bf16[128,2048]{1,0:T(8,128)(2,1)S(1)}, bf16[128,2048]{1,0:T(8,128)(2,1)S(1)}, u32[]{:S(2)}, u32[]{:S(2)}) %collective-permute-start.4) | collective-permute-done | bytes 524320 | tf_op jit(solution)/shard_map/ppermute | solution.py:322
  91.1 8.8 %attend.1 = (bf16[1024,256]{1,0:T(8,128)(2,1)S(1)}, bf16[1024,256]{1,0:T(8,128)(2,1)S(1)}, bf16[1024,256]{1,0:T(8,128)(2,1)S(1)}, bf16[1024,128]{1,0:T(8,128)(2,...) custom-call(s32[16]{0:T(128)S(1)} %get-tuple-element.191.sources_ref, ...), custom_call_target="tpu_custom_call" | custom-call | tf_op jit(solution)/shard_map/attend/pallas_call | solution.py:208
  110.5 23.1 %all-to-all-done.1 = bf16[8,128,256]{1,2,0:T(8,128)(2,1)} async-done(((bf16[8,128,256]{1,2,0:T(8,128)(2,1)}), bf16[8,128,256]{1,2,0:T(8,128)(2,1)}, u32[]{:S(2)}, u32[]{:S(2)}) %all-to-all-start.1) | async-done | bytes 524320 | tf_op jit(solution)/shard_map/all_to_all | solution.py:326
  149.8 29.5 %all_to_all.44 = bf16[4,128,2048]{2,1,0:T(8,128)(2,1)} all-to-all(bf16[4,128,2048]{2,1,0:T(8,128)(2,1)S(1)} %broadcast_in_dim.14), channel_id=1, replica_groups=mesh['chip'=4,'core'=2,'hi'=2,'lo'=2] {'chip'}, dimensions={0} | all-to-all | bytes 4194304 | tf_op jit(solution)/shard_map/all_to_all | solution.py:326
  183.8 9.2 %all-gather.6.cloned.1.call-done = bf16[2048,1536]{1,0:T(8,128)(2,1)} async-done(((bf16[512,1536]{1,0:T(8,128)(2,1)}), bf16[2048,1536]{1,0:T(8,128)(2,1)}) %all-gather.6.cloned.1.call-update) | async-done | bytes 6291472 | tf_op jit(solution)/shard_map/all_gather | solution.py:388
  193.0 6.3 %fusion.47 = f32[512,1536]{1,0:T(8,128)S(1)} fusion(bf16[512,2048]{1,0:T(8,128)(2,1)} %collective-permute-done.14, bf16[2048,1536]{1,0:T(8,128)(2,1)} %all-gather.6.cloned.1.call-done), kind=kOutput, calls=%fused_computation.153 | convolution fusion | flops 3221225472 | bytes 11534336 | tf_op jit(solution)/shard_map/dot_general | solution.py:26
  201.6 5.4 %fusion.46 = f32[512,1536]{1,0:T(8,128)S(1)} fusion(bf16[512,2048]{1,0:T(8,128)(2,1)} %bitcast.17, bf16[2048,1536]{1,0:T(8,128)(2,1)S(1)} %copy-done.38), kind=kOutput, calls=%fused_computation.152 | convolution fusion | flops 3221225472 | bytes 11534336 | tf_op jit(solution)/shard_map/dot_general | solution.py:26
  217.5 7.4 %collective-permute-start.16 = (bf16[192,2048]{1,0:T(8,128)(2,1)}, bf16[192,2048]{1,0:T(8,128)(2,1)}, u32[]{:S(2)}, u32[]{:S(2)}) collective-permute-start(bf16[192,2048]{1,0:T(8,128)(2,1)} %get-tuple-element.162), channel_id=1, source_target_pairs={{0,0},{4,8},{8,16},{12,24},{16,4},{20,12},{24,20},{28,28},{1,1},{5... | collective-permute-start | bytes 2359304 | tf_op jit(solution)/shard_map/ppermute | solution.py:480
  235.9 11.1 %collective-permute-done.17 = bf16[192,2048]{1,0:T(8,128)(2,1)} collective-permute-done((bf16[192,2048]{1,0:T(8,128)(2,1)}, bf16[192,2048]{1,0:T(8,128)(2,1)}, u32[]{:S(2)}, u32[]{:S(2)}) %collective-permute-start.17) | collective-permute-done | bytes 786464 | tf_op jit(solution)/shard_map/ppermute | solution.py:480
  257.6 5.6 %multiply_convert_fusion.1 = (bf16[512,768]{1,0:T(8,128)(2,1)S(1)}, bf16[512,768]{1,0:T(8,128)(2,1)S(1)}) fusion(f32[512,1536]{1,0:T(8,128)} %copy-done.26, bf16[512,2048]{1,0:T(8,128)(2,1)} %collective-permute-done.15, bf16[768,2048]{1,0:T(8,128)(2,1)} %all-gather.8.cloned.1.call-done), kind=kOutput, calls=%fused_computation.35 | convolution fusion | flops 1615724544 | bytes 9961472 | tf_op jit(solution)/shard_map/dot_general | solution.py:30
  264.4 6.6 %convolution_convert_fusion.4 = bf16[512,2048]{1,0:T(8,128)(2,1)S(1)} fusion(bf16[2048,1536]{1,0:T(8,128)(2,1)} %all-gather.6.cloned.1.call-done, bf16[512,768]{1,0:T(8,128)(2,1)S(1)} %get-tuple-element.158, bf16[512,768]{1,0:T(8,128)(2,1)S(1)} %get-tuple-element.157), kind=kOutput, calls=%fused_computation.22 | convolution fusion | flops 3225419776 | bytes 9961472 | tf_op jit(solution)/shard_map/dot_general | solution.py:30
  286.7 10.2 %fusion.21 = f32[2048,1536]{1,0:T(8,128)} fusion(bf16[512,2048]{1,0:T(8,128)(2,1)} %bitcast.17, bf16[512,768]{1,0:T(8,128)(2,1)} %copy-done.42, bf16[512,768]{1,0:T(8,128)(2,1)} %copy-done.41), kind=kOutput, calls=%fused_computation.68 | convolution fusion | flops 3224371200 | bytes 16252928 | tf_op jit(solution)/shard_map/dot_general | solution.py:34
  296.9 7.4 %add_convert_fusion = bf16[2048,1536]{1,0:T(8,128)(2,1)S(1)} fusion(f32[2048,1536]{1,0:T(8,128)} %fusion.21, bf16[512,2048]{1,0:T(8,128)(2,1)} %collective-permute-done.14, bf16[512,768]{1,0:T(8,128)(2,1)S(1)} %copy-done.46, bf16[512,768]{1,0:T(8,128)(2,1)S(1)} %copy-done.44), kind=kOutput, calls=%fused_computation | convolution fusion | flops 3230662656 | bytes 22544384 | tf_op jit(solution)/shard_map/dot_general | solution.py:34
  307.6 5.5 %all-to-all-done.3.refs_1_ = bf16[4,128,2048]{2,1,0:T(8,128)(2,1)} async-done(((bf16[4,128,2048]{2,1,0:T(8,128)(2,1)}), bf16[4,128,2048]{2,1,0:T(8,128)(2,1)}, u32[]{:S(2)}, u32[]{:S(2)}) %all-to-all-start.3) | async-done | bytes 2097184 | tf_op jit(solution)/shard_map/all_to_all | solution.py:326
  319.7 6.3 %project_back.1 = (f32[128,2048]{1,0:T(8,128)S(1)}, bf16[128,2048]{1,0:T(8,128)(2,1)}, f32[1,2048]{1,0:T(1,128)S(1)}, bf16[8,128,256]{2,1,0:T(8,128)(2,1)S(1)}) custom-call(s32[8]{0:T(128)S(1)} %stack.35.refs_0_, bf16[4,128,2048]{2,1,0:T(8,128)(2,1)} %all-to-all-done.3.refs_1_, f32[128,2048]{1,0:T(8,128)S(1)} %get-tuple-element.146.refs_2_, ...), custom_call_target="tpu_custom_call" | custom-call | tf_op jit(solution)/shard_map/project_back/pallas_call | solution.py:281
  340.0 9.5 %all-to-all-done.4 = bf16[8,128,256]{2,1,0:T(8,128)(2,1)S(1)} async-done(((bf16[8,128,256]{2,1,0:T(8,128)(2,1)}), bf16[8,128,256]{2,1,0:T(8,128)(2,1)S(1)}, u32[]{:S(2)}, u32[]{:S(2)}) %all-to-all-start.4) | async-done | bytes 524320 | tf_op jit(solution)/shard_map/all_to_all | solution.py:326
  352.6 10.6 %attend_back.1 = (bf16[1024,512]{1,0:T(8,128)(2,1)S(1)}, f32[2,128]{1,0:T(2,128)S(1)}) custom-call(s32[16]{0:T(128)S(1)} %get-tuple-element.191.sources_ref, s32[16]{0:T(128)S(1)} %get-tuple-element.190.places_ref, f32[1024,512]{1,0:T(8,128)} %pad_maximum_fusion.1.raw_ref, f32[1024,128]{1,0:T(8,128)S(1)} %get-tuple-element.200.cos_ref, ...), custom_call_target="tpu_custom_call" | custom-call | tf_op jit(solution)/shard_map/attend_back/pallas_call | solution.py:223
  381.0 25.9 %all-to-all-done.5 = bf16[8,256,512]{2,1,0:T(8,128)(2,1)S(1)} async-done(((bf16[8,256,512]{2,1,0:T(8,128)(2,1)}), bf16[8,256,512]{2,1,0:T(8,128)(2,1)S(1)}, u32[]{:S(2)}, u32[]{:S(2)}) %all-to-all-start.5) | async-done | bytes 2097184 | tf_op jit(solution)/shard_map/all_to_all | solution.py:326
  434.4 7.2 %collective-permute-done.32 = bf16[128,2048]{1,0:T(8,128)(2,1)S(1)} collective-permute-done((bf16[128,2048]{1,0:T(8,128)(2,1)S(1)}, bf16[128,2048]{1,0:T(8,128)(2,1)S(1)}, u32[]{:S(2)}, u32[]{:S(2)}) %collective-permute-start.32) | collective-permute-done | bytes 524320 | tf_op jit(solution)/shard_map/ppermute | solution.py:322
  442.1 10.8 %collective-permute-done.31 = bf16[128,2048]{1,0:T(8,128)(2,1)S(1)} collective-permute-done((bf16[128,2048]{1,0:T(8,128)(2,1)S(1)}, bf16[128,2048]{1,0:T(8,128)(2,1)S(1)}, u32[]{:S(2)}, u32[]{:S(2)}) %collective-permute-start.31) | collective-permute-done | bytes 524320 | tf_op jit(solution)/shard_map/ppermute | solution.py:322
  464.2 10.5 %collective-permute-done.27 = bf16[128,2048]{1,0:T(8,128)(2,1)} collective-permute-done((bf16[128,2048]{1,0:T(8,128)(2,1)}, bf16[128,2048]{1,0:T(8,128)(2,1)}, u32[]{:S(2)}, u32[]{:S(2)}) %collective-permute-start.27) | collective-permute-done | bytes 524320 | tf_op jit(solution)/shard_map/ppermute | solution.py:322
  479.0 12.5 %all-to-all-done.6.in_ref = bf16[8,64,1536]{2,1,0:T(8,128)(2,1)S(1)} async-done(((bf16[8,64,1536]{2,1,0:T(8,128)(2,1)}), bf16[8,64,1536]{2,1,0:T(8,128)(2,1)S(1)}, u32[]{:S(2)}, u32[]{:S(2)}) %all-to-all-start.6) | async-done | bytes 1572896 | tf_op jit(solution)/shard_map/all_to_all | solution.py:326
  (299 shorter events, 241.6 us)
Async XLA Ops:
  7.2 69.6 %all-gather.4.cloned.1.call-start = ((), (), s32[]{:S(2)}) async-start(), calls=%async_computation.11 | async-start | bytes 3932160 | tf_op jit(solution)/shard_map/all_gather | solution.py:388
  12.0 31.1 %all-to-all-start = ((bf16[4,128,2048]{2,1,0:T(8,128)(2,1)}), bf16[4,128,2048]{2,1,0:T(8,128)(2,1)}, u32[]{:S(2)}, u32[]{:S(2)}) async-start(bf16[4,128,2048]{2,1,0:T(8,128)(2,1)} %broadcast_in_dim.11), calls=%async_computation | async-start | bytes 4194304 | tf_op jit(solution)/shard_map/all_to_all | solution.py:326
  17.3 175.7 %all-gather.6.cloned.1.call-start = ((), (), s32[]{:S(2)}) async-start(), calls=%async_computation.12 | async-start | bytes 7864320 | tf_op jit(solution)/shard_map/all_gather | solution.py:388
  43.0 29.9 %collective-permute-start.6 = (bf16[512,2048]{1,0:T(8,128)(2,1)}, bf16[512,2048]{1,0:T(8,128)(2,1)}, u32[]{:S(2)}, u32[]{:S(2)}) collective-permute-start(bf16[512,2048]{1,0:T(8,128)(2,1)} %bitcast.1), channel_id=1, source_target_pairs={{0,4},{4,0},{1,5},{5,1},{2,6},{6,2},{3,7},{7,3},{8,12},{12,8},{9,1... | collective-permute-start | bytes 6291464 | tf_op jit(solution)/shard_map/ppermute | solution.py:322
  79.1 56.4 %collective-permute-start.7 = (bf16[2048,256]{1,0:T(8,128)(2,1)}, bf16[2048,256]{1,0:T(8,128)(2,1)S(1)}, u32[]{:S(2)}, u32[]{:S(2)}) collective-permute-start(bf16[2048,256]{1,0:T(8,128)(2,1)} %slice.85.refs_5_), channel_id=1, source_target_pairs={{0,8},{8,0},{16,24},{24,16},{1,9},{9,1},{17,25},{25,17},{2,10},{10... | collective-permute-start | bytes 3145736 | tf_op jit(solution)/shard_map/ppermute | solution.py:322
  80.6 55.0 %collective-permute-start.8 = (bf16[2048,256]{1,0:T(8,128)(2,1)}, bf16[2048,256]{1,0:T(8,128)(2,1)}, u32[]{:S(2)}, u32[]{:S(2)}) collective-permute-start(bf16[2048,256]{1,0:T(8,128)(2,1)} %slice.85.refs_5_), channel_id=1, source_target_pairs={{0,16},{8,24},{16,0},{24,8},{1,17},{9,25},{17,1},{25,9},{2,18},{10... | collective-permute-start | bytes 3145736 | tf_op jit(solution)/shard_map/ppermute | solution.py:322
  82.1 54.0 %collective-permute-start.9 = (bf16[2048,256]{1,0:T(8,128)(2,1)}, bf16[2048,256]{1,0:T(8,128)(2,1)}, u32[]{:S(2)}, u32[]{:S(2)}) collective-permute-start(bf16[2048,256]{1,0:T(8,128)(2,1)} %slice.85.refs_5_), channel_id=1, source_target_pairs={{0,24},{8,16},{16,8},{24,0},{1,25},{9,17},{17,9},{25,1},{2,26},{10... | collective-permute-start | bytes 3145736 | tf_op jit(solution)/shard_map/ppermute | solution.py:322
  110.1 147.5 %all-gather.8.cloned.1.call-start = ((), (), s32[]{:S(2)}) async-start(), calls=%async_computation.13 | async-start | bytes 3932160 | tf_op jit(solution)/shard_map/all_gather | solution.py:388
  110.2 31.0 %collective-permute-start.10 = (bf16[2048,256]{1,0:T(8,128)(2,1)}, bf16[2048,256]{1,0:T(8,128)(2,1)}, u32[]{:S(2)}, u32[]{:S(2)}) collective-permute-start(bf16[2048,256]{1,0:T(8,128)(2,1)} %slice.85.refs_5_), channel_id=1, source_target_pairs={{0,4},{4,0},{1,5},{5,1},{2,6},{6,2},{3,7},{7,3},{8,12},{12,8},{9,1... | collective-permute-start | bytes 3145736 | tf_op jit(solution)/shard_map/ppermute | solution.py:322
  179.3 139.0 %reduce-scatter.4.cloned.1.call-start = ((), (), s32[]{:S(2)}) async-start(), calls=%async_computation.14 | async-start | bytes 3932160 | tf_op jit(solution)/shard_map/reduce_scatter | solution.py:392
  179.6 27.9 %collective-permute-start.15 = (bf16[512,2048]{1,0:T(8,128)(2,1)}, bf16[512,2048]{1,0:T(8,128)(2,1)}, u32[]{:S(2)}, u32[]{:S(2)}) collective-permute-start(bf16[512,2048]{1,0:T(8,128)(2,1)} %constant_dynamic-update-slice_fusion.8), channel_id=1, source_target_pairs={{0,4},{4,0},{1,5},{5,1},{2,6},{6,2},{3,7},{7,3},{8,12},{12,8},{9,1... | collective-permute-start | bytes 6291464 | tf_op jit(solution)/shard_map/ppermute | solution.py:322
  227.0 28.5 %collective-permute-start.19 = (bf16[192,2048]{1,0:T(8,128)(2,1)}, bf16[192,2048]{1,0:T(8,128)(2,1)}, u32[]{:S(2)}, u32[]{:S(2)}) collective-permute-start(bf16[192,2048]{1,0:T(8,128)(2,1)} %get-tuple-element.159), channel_id=1, source_target_pairs={{0,24},{4,0},{8,8},{12,16},{16,28},{20,4},{24,12},{28,20},{1,25},{... | collective-permute-start | bytes 2359304 | tf_op jit(solution)/shard_map/ppermute | solution.py:480
  281.7 31.3 %all-to-all-start.3 = ((bf16[4,128,2048]{2,1,0:T(8,128)(2,1)}), bf16[4,128,2048]{2,1,0:T(8,128)(2,1)}, u32[]{:S(2)}, u32[]{:S(2)}) async-start(bf16[4,128,2048]{2,1,0:T(8,128)(2,1)} %bitcast.118), calls=%async_computation.3 | async-start | bytes 4194304 | tf_op jit(solution)/shard_map/all_to_all | solution.py:326
  286.2 168.0 %reduce-scatter.6.cloned.1.call-start = ((), (), s32[]{:S(2)}) async-start(), calls=%async_computation.15 | async-start | bytes 7864320 | tf_op jit(solution)/shard_map/reduce_scatter | solution.py:392
  327.9 35.4 %collective-permute-start.21 = (bf16[128,2048]{1,0:T(8,128)(2,1)}, bf16[128,2048]{1,0:T(8,128)(2,1)}, u32[]{:S(2)}, u32[]{:S(2)}) collective-permute-start(bf16[128,2048]{1,0:T(8,128)(2,1)} %get-tuple-element.69), channel_id=1, source_target_pairs={{0,8},{8,0},{16,24},{24,16},{1,9},{9,1},{17,25},{25,17},{2,10},{10... | collective-permute-start | bytes 1572872 | tf_op jit(solution)/shard_map/ppermute | solution.py:322
  333.0 32.5 %collective-permute-start.22 = (bf16[128,2048]{1,0:T(8,128)(2,1)}, bf16[128,2048]{1,0:T(8,128)(2,1)}, u32[]{:S(2)}, u32[]{:S(2)}) collective-permute-start(bf16[128,2048]{1,0:T(8,128)(2,1)} %get-tuple-element.69), channel_id=1, source_target_pairs={{0,16},{8,24},{16,0},{24,8},{1,17},{9,25},{17,1},{25,9},{2,18},{10... | collective-permute-start | bytes 1572872 | tf_op jit(solution)/shard_map/ppermute | solution.py:322
  335.0 32.4 %collective-permute-start.23 = (bf16[128,2048]{1,0:T(8,128)(2,1)}, bf16[128,2048]{1,0:T(8,128)(2,1)}, u32[]{:S(2)}, u32[]{:S(2)}) collective-permute-start(bf16[128,2048]{1,0:T(8,128)(2,1)} %get-tuple-element.69), channel_id=1, source_target_pairs={{0,24},{8,16},{16,8},{24,0},{1,25},{9,17},{17,9},{25,1},{2,26},{10... | collective-permute-start | bytes 1572872 | tf_op jit(solution)/shard_map/ppermute | solution.py:322
  376.7 30.2 %all-to-all-start.5 = ((bf16[8,256,512]{2,1,0:T(8,128)(2,1)}), bf16[8,256,512]{2,1,0:T(8,128)(2,1)S(1)}, u32[]{:S(2)}, u32[]{:S(2)}) async-start(bf16[8,256,512]{2,1,0:T(8,128)(2,1)} %bitcast.119), calls=%async_computation.6 | async-start | bytes 4194304 | tf_op jit(solution)/shard_map/all_to_all | solution.py:326
  380.4 121.8 %reduce-scatter.8.cloned.1.call-start = ((), (), s32[]{:S(2)}) async-start(), calls=%async_computation.16 | async-start | bytes 3932160 | tf_op jit(solution)/shard_map/reduce_scatter | solution.py:392
  380.6 28.5 %collective-permute-start.24 = (bf16[512,2048]{1,0:T(8,128)(2,1)}, bf16[512,2048]{1,0:T(8,128)(2,1)}, u32[]{:S(2)}, u32[]{:S(2)}) collective-permute-start(bf16[512,2048]{1,0:T(8,128)(2,1)} %constant_dynamic-update-slice_fusion), channel_id=1, source_target_pairs={{0,4},{4,0},{1,5},{5,1},{2,6},{6,2},{3,7},{7,3},{8,12},{12,8},{9,1... | collective-permute-start | bytes 6291464 | tf_op jit(solution)/shard_map/ppermute | solution.py:322
  432.5 31.7 %collective-permute-start.28 = (bf16[128,2048]{1,0:T(8,128)(2,1)}, bf16[128,2048]{1,0:T(8,128)(2,1)}, u32[]{:S(2)}, u32[]{:S(2)}) collective-permute-start(bf16[128,2048]{1,0:T(8,128)(2,1)} %get-tuple-element.167), channel_id=1, source_target_pairs={{0,24},{8,16},{16,8},{24,0},{1,25},{9,17},{17,9},{25,1},{2,26},{10... | collective-permute-start | bytes 1572872 | tf_op jit(solution)/shard_map/ppermute | solution.py:322
  433.1 41.5 %collective-permute-start.27 = (bf16[128,2048]{1,0:T(8,128)(2,1)}, bf16[128,2048]{1,0:T(8,128)(2,1)}, u32[]{:S(2)}, u32[]{:S(2)}) collective-permute-start(bf16[128,2048]{1,0:T(8,128)(2,1)} %get-tuple-element.168), channel_id=1, source_target_pairs={{0,16},{8,24},{16,0},{24,8},{1,17},{9,25},{17,1},{25,9},{2,18},{10... | collective-permute-start | bytes 1572872 | tf_op jit(solution)/shard_map/ppermute | solution.py:322
  441.6 33.1 %collective-permute-start.26 = (bf16[128,2048]{1,0:T(8,128)(2,1)}, bf16[128,2048]{1,0:T(8,128)(2,1)}, u32[]{:S(2)}, u32[]{:S(2)}) collective-permute-start(bf16[128,2048]{1,0:T(8,128)(2,1)} %get-tuple-element.166), channel_id=1, source_target_pairs={{0,8},{8,0},{16,24},{24,16},{1,9},{9,1},{17,25},{25,17},{2,10},{10... | collective-permute-start | bytes 1572872 | tf_op jit(solution)/shard_map/ppermute | solution.py:322
  454.2 37.2 %all-to-all-start.6 = ((bf16[8,64,1536]{2,1,0:T(8,128)(2,1)}), bf16[8,64,1536]{2,1,0:T(8,128)(2,1)S(1)}, u32[]{:S(2)}, u32[]{:S(2)}) async-start(bf16[8,64,1536]{2,1,0:T(8,128)(2,1)} %bitcast.122), calls=%async_computation.9 | async-start | bytes 3145728 | tf_op jit(solution)/shard_map/all_to_all | solution.py:326
  (71 other events, 617.2 us)
Sparse Core Ops, SparseCore 0:
  10.5 66.2 all-gather.3
  78.9 114.0 all-gather.5
  194.6 61.7 all-gather.7
  258.5 59.8 reduce-scatter.3
  320.5 110.7 reduce-scatter.5
  433.5 60.7 reduce-scatter.7

commit v5 on v4

--- a/solution.py
+++ b/solution.py
@@ -547,7 +547,12 @@
     grad_middle, middle_low, grad_gain_ffn, mixed_grad = project_back(
         jnp.stack(owners), grad_ffn, middle, own_cotangent, gain_ffn.reshape(1, -1), out_blocks
     )
-    mixed_grad = exchange(mixed_grad, CTX).reshape(total, qw)
+    mixed_grad, *hidden_parts = after(mixed_grad, *hidden_parts)
+    block_parts = [dot(values, down_w).astype(low) for values in hidden_parts]
+    block_half = sum_cores(block_parts[0], block_parts[1])
+    mixed_grad, block_half = after(exchange(mixed_grad, CTX), block_half)
+    block_sum = sum_chips(block_half)
+    mixed_grad = mixed_grad.reshape(total, qw)
     late_half = in_order(spread(middle_low, "chip"), chip)
     qkv_grad, grad_gains = attend_back(
         total, heads, sources, places, qkv_raw, *tables, query, key, value, logs, mixed_grad
@@ -556,8 +561,10 @@
     grad_out = sum_parts(halves(mixed_rel), (late_half, swap(late_half, "core")))
     qkv_grads = halves(qkv_grad)
     grad_attn = [dot_t(grads, qkv_w).astype(low) for grads in qkv_grads]
-    grad_attn = sum_chips(sum_cores(grad_attn[0], grad_attn[1]))
+    attn_half = sum_cores(grad_attn[0], grad_attn[1])
     grad_qkv = sum_parts(normed_parts, qkv_grads).reshape(n, m * strip, -1)
+    block_sum, grad_qkv = after(block_sum, grad_qkv)
+    block_out = (middle + block_sum).astype(low).reshape(tokens.shape)
     grad_qkv = exchange(grad_qkv, CTX).reshape(n, m, strip, -1)
 
     def all_heads(grads):
@@ -574,10 +581,8 @@
         grad_out.reshape(m, strip, width),
     ]
     grad_late = jnp.concatenate(grad_late, axis=2).reshape(m * strip, -1)
-    grad_late, *hidden_parts = after(grad_late, *hidden_parts)
-    block_parts = [dot(values, down_w).astype(low) for values in hidden_parts]
-    block_half = sum_cores(block_parts[0], block_parts[1])
-    block_out = (middle + sum_chips(block_half)).astype(low).reshape(tokens.shape)
+    grad_late, attn_half = after(grad_late, attn_half)
+    grad_attn = sum_chips(attn_half)
     grad_late = scatter_rows(grad_late)
 
     grad_attn, grad_gate_up = after(grad_attn, grad_gate_up)

time: 522 us -> 516 us (0.989)
  waiting for transfers between devices: 175 us -> 160 us
  matrix products: 97.6 us -> 106 us
    all_to_all x7, waiting for transfers between devices: 89.9 us -> 72.4 us  [exchange(): return lax.all_to_all(values, axis, 0, 0, tiled=True)]
    unnamed x108 -> x116, local copies, waits for them, and re-layouts: 18.3 us -> 14.1 us
  transfers between devices with their start and end apart: 46 -> 46, of which waited for: 21 -> 20; matrix products, arithmetic and copies ran while one was open for 33% -> 36% of each run, Pallas kernels for 5% -> 6%
where the time goes in v5:
time: 516 us; the launch traced here: 509 us
  waiting for transfers between devices  160 us (31%)
  matrix products  106 us (21%)
  starting transfers between devices  71.8 us (14%)
  local copies, waits for them, and re-layouts  68.7 us (13%)
  other arithmetic  29.9 us (6%)
  blocking collectives  29.5 us (6%)
  Pallas kernels  28.1 us (5%)
  between operations  15.7 us (3%)
    all_to_all x7, waiting for transfers between devices, exchange(): return lax.all_to_all(values, axis, 0, 0, tiled=True)  72.4 us
    ppermute x29, waiting for transfers between devices, swap(): return lax.ppermute(values, axis, [(i, i ^ mask) for i in range(size)])  55.8 us
    dot_general x14, matrix products, dot(): return jnp.dot(left, right, preferred_element_type=high)  40.2 us
    dot_general x8, matrix products, t_dot(): lax.dot_general(left, right, (((0,), (0,)), ((), ())), preferred_element_...  37.8 us
    all_to_all x1, blocking collectives, exchange(): return lax.all_to_all(values, axis, 0, 0, tiled=True)  29.5 us
    all_to_all x7, starting transfers between devices, exchange(): return lax.all_to_all(values, axis, 0, 0, tiled=True)  29.1 us
    ppermute x29, starting transfers between devices, swap(): return lax.ppermute(values, axis, [(i, i ^ mask) for i in range(size)])  27.7 us
    dot_general x6, matrix products, dot_t(): lax.dot_general(left, right, (((1,), (1,)), ((), ())), preferred_element_...  27.6 us
  transfers between devices with their start and end apart: 46, of which 20 were waited for; matrix products, arithmetic and copies ran while one was open for 36% of the time, Pallas kernels for 6%

profile of v5, /device:TPU:0, one launch (start us, length us, event | category | flops | bytes accessed | tf_op | source)
XLA Modules:
  0.0 509.2 jit_solution(14070847543440692056)
XLA Ops:
  32.2 10.9 %all-to-all-done = bf16[4,128,2048]{2,1,0:T(8,128)(2,1)} async-done(((bf16[4,128,2048]{2,1,0:T(8,128)(2,1)}), bf16[4,128,2048]{2,1,0:T(8,128)(2,1)}, u32[]{:S(2)}, u32[]{:S(2)}) %all-to-all-start) | async-done | bytes 2097184 | tf_op jit(solution)/shard_map/all_to_all | solution.py:326
  52.5 6.8 %collective-permute-done.3 = bf16[128,2048]{1,0:T(8,128)(2,1)} collective-permute-done((bf16[128,2048]{1,0:T(8,128)(2,1)S(1)}, bf16[128,2048]{1,0:T(8,128)(2,1)}, u32[]{:S(2)}, u32[]{:S(2)}) %collective-permute-start.3) | collective-permute-done | bytes 524320 | tf_op jit(solution)/shard_map/ppermute | solution.py:322
  61.2 10.1 %collective-permute-done.4 = bf16[128,2048]{1,0:T(8,128)(2,1)S(1)} collective-permute-done((bf16[128,2048]{1,0:T(8,128)(2,1)S(1)}, bf16[128,2048]{1,0:T(8,128)(2,1)S(1)}, u32[]{:S(2)}, u32[]{:S(2)}) %collective-permute-start.4) | collective-permute-done | bytes 524320 | tf_op jit(solution)/shard_map/ppermute | solution.py:322
  91.2 8.8 %attend.1 = (bf16[1024,256]{1,0:T(8,128)(2,1)S(1)}, bf16[1024,256]{1,0:T(8,128)(2,1)S(1)}, bf16[1024,256]{1,0:T(8,128)(2,1)S(1)}, bf16[1024,128]{1,0:T(8,128)(2,...) custom-call(s32[16]{0:T(128)S(1)} %get-tuple-element.203.sources_ref, ...), custom_call_target="tpu_custom_call" | custom-call | tf_op jit(solution)/shard_map/attend/pallas_call | solution.py:208
  110.5 23.0 %all-to-all-done.1 = bf16[8,128,256]{1,2,0:T(8,128)(2,1)} async-done(((bf16[8,128,256]{1,2,0:T(8,128)(2,1)}), bf16[8,128,256]{1,2,0:T(8,128)(2,1)}, u32[]{:S(2)}, u32[]{:S(2)}) %all-to-all-start.1) | async-done | bytes 524320 | tf_op jit(solution)/shard_map/all_to_all | solution.py:326
  149.8 29.5 %all_to_all.44 = bf16[4,128,2048]{2,1,0:T(8,128)(2,1)} all-to-all(bf16[4,128,2048]{2,1,0:T(8,128)(2,1)S(1)} %broadcast_in_dim.14), channel_id=1, replica_groups=mesh['chip'=4,'core'=2,'hi'=2,'lo'=2] {'chip'}, dimensions={0} | all-to-all | bytes 4194304 | tf_op jit(solution)/shard_map/all_to_all | solution.py:326
  183.8 9.2 %all-gather.6.cloned.1.call-done = bf16[2048,1536]{1,0:T(8,128)(2,1)} async-done(((bf16[512,1536]{1,0:T(8,128)(2,1)}), bf16[2048,1536]{1,0:T(8,128)(2,1)}) %all-gather.6.cloned.1.call-update) | async-done | bytes 6291472 | tf_op jit(solution)/shard_map/all_gather | solution.py:388
  193.0 6.3 %fusion.47 = f32[512,1536]{1,0:T(8,128)S(1)} fusion(bf16[512,2048]{1,0:T(8,128)(2,1)} %collective-permute-done.14, bf16[2048,1536]{1,0:T(8,128)(2,1)} %all-gather.6.cloned.1.call-done), kind=kOutput, calls=%fused_computation.154 | convolution fusion | flops 3221225472 | bytes 11534336 | tf_op jit(solution)/shard_map/dot_general | solution.py:26
  201.6 5.4 %fusion.46 = f32[512,1536]{1,0:T(8,128)S(1)} fusion(bf16[512,2048]{1,0:T(8,128)(2,1)} %bitcast.17, bf16[2048,1536]{1,0:T(8,128)(2,1)S(1)} %copy-done.41), kind=kOutput, calls=%fused_computation.153 | convolution fusion | flops 3221225472 | bytes 11534336 | tf_op jit(solution)/shard_map/dot_general | solution.py:26
  217.5 7.4 %collective-permute-start.16 = (bf16[192,2048]{1,0:T(8,128)(2,1)}, bf16[192,2048]{1,0:T(8,128)(2,1)}, u32[]{:S(2)}, u32[]{:S(2)}) collective-permute-start(bf16[192,2048]{1,0:T(8,128)(2,1)} %get-tuple-element.174), channel_id=1, source_target_pairs={{0,0},{4,8},{8,16},{12,24},{16,4},{20,12},{24,20},{28,28},{1,1},{5... | collective-permute-start | bytes 2359304 | tf_op jit(solution)/shard_map/ppermute | solution.py:480
  236.1 11.0 %collective-permute-done.17 = bf16[192,2048]{1,0:T(8,128)(2,1)} collective-permute-done((bf16[192,2048]{1,0:T(8,128)(2,1)}, bf16[192,2048]{1,0:T(8,128)(2,1)}, u32[]{:S(2)}, u32[]{:S(2)}) %collective-permute-start.17) | collective-permute-done | bytes 786464 | tf_op jit(solution)/shard_map/ppermute | solution.py:480
  257.6 5.7 %multiply_convert_fusion.1 = (bf16[512,768]{1,0:T(8,128)(2,1)S(1)}, bf16[512,768]{1,0:T(8,128)(2,1)S(1)}) fusion(f32[512,1536]{1,0:T(8,128)} %copy-done.28, bf16[512,2048]{1,0:T(8,128)(2,1)} %collective-permute-done.15, bf16[768,2048]{1,0:T(8,128)(2,1)} %all-gather.8.cloned.1.call-done), kind=kOutput, calls=%fused_computation.35 | convolution fusion | flops 1615724544 | bytes 9961472 | tf_op jit(solution)/shard_map/dot_general | solution.py:30
  264.4 6.6 %convolution_convert_fusion.4 = bf16[512,2048]{1,0:T(8,128)(2,1)S(1)} fusion(bf16[2048,1536]{1,0:T(8,128)(2,1)} %all-gather.6.cloned.1.call-done, bf16[512,768]{1,0:T(8,128)(2,1)S(1)} %get-tuple-element.170, bf16[512,768]{1,0:T(8,128)(2,1)S(1)} %get-tuple-element.169), kind=kOutput, calls=%fused_computation.22 | convolution fusion | flops 3225419776 | bytes 9961472 | tf_op jit(solution)/shard_map/dot_general | solution.py:30
  286.4 10.2 %fusion.21 = f32[2048,1536]{1,0:T(8,128)} fusion(bf16[512,2048]{1,0:T(8,128)(2,1)} %bitcast.17, bf16[512,768]{1,0:T(8,128)(2,1)} %copy-done.46, bf16[512,768]{1,0:T(8,128)(2,1)} %copy-done.45), kind=kOutput, calls=%fused_computation.69 | convolution fusion | flops 3224371200 | bytes 16252928 | tf_op jit(solution)/shard_map/dot_general | solution.py:34
  296.6 7.4 %add_convert_fusion = bf16[2048,1536]{1,0:T(8,128)(2,1)S(1)} fusion(f32[2048,1536]{1,0:T(8,128)} %fusion.21, bf16[512,2048]{1,0:T(8,128)(2,1)} %collective-permute-done.14, bf16[512,768]{1,0:T(8,128)(2,1)S(1)} %copy-done.50, bf16[512,768]{1,0:T(8,128)(2,1)S(1)} %copy-done.48), kind=kOutput, calls=%fused_computation | convolution fusion | flops 3230662656 | bytes 22544384 | tf_op jit(solution)/shard_map/dot_general | solution.py:34
  307.2 5.8 %all-to-all-done.3.refs_1_ = bf16[4,128,2048]{2,1,0:T(8,128)(2,1)} async-done(((bf16[4,128,2048]{2,1,0:T(8,128)(2,1)}), bf16[4,128,2048]{2,1,0:T(8,128)(2,1)}, u32[]{:S(2)}, u32[]{:S(2)}) %all-to-all-start.3) | async-done | bytes 2097184 | tf_op jit(solution)/shard_map/all_to_all | solution.py:326
  313.0 5.3 %reduce-scatter.4.cloned.1.call-done = bf16[192,2048]{1,0:T(8,128)(2,1)} async-done(((bf16[768,2048]{1,0:T(8,128)(2,1)}), bf16[192,2048]{1,0:T(8,128)(2,1)}) %reduce-scatter.4.cloned.1.call-update) | async-done | bytes 786448 | tf_op jit(solution)/shard_map/reduce_scatter | solution.py:392
  319.7 6.5 %project_back.1 = (f32[128,2048]{1,0:T(8,128)S(1)}, bf16[128,2048]{1,0:T(8,128)(2,1)}, f32[1,2048]{1,0:T(1,128)S(1)}, bf16[8,128,256]{2,1,0:T(8,128)(2,1)S(1)}) custom-call(s32[8]{0:T(128)S(1)} %stack.35.refs_0_, bf16[4,128,2048]{2,1,0:T(8,128)(2,1)} %all-to-all-done.3.refs_1_, f32[128,2048]{1,0:T(8,128)S(1)} %get-tuple-element.158.refs_2_, ...), custom_call_target="tpu_custom_call" | custom-call | tf_op jit(solution)/shard_map/project_back/pallas_call | solution.py:281
  346.5 10.9 %collective-permute-done.26 = bf16[128,2048]{1,0:T(8,128)(2,1)} collective-permute-done((bf16[128,2048]{1,0:T(8,128)(2,1)}, bf16[128,2048]{1,0:T(8,128)(2,1)}, u32[]{:S(2)}, u32[]{:S(2)}) %collective-permute-start.26) | collective-permute-done | bytes 524320 | tf_op jit(solution)/shard_map/ppermute | solution.py:322
  372.0 10.8 %attend_back.1 = (bf16[1024,512]{1,0:T(8,128)(2,1)S(1)}, f32[2,128]{1,0:T(2,128)S(1)}) custom-call(s32[16]{0:T(128)S(1)} %get-tuple-element.203.sources_ref, s32[16]{0:T(128)S(1)} %get-tuple-element.202.places_ref, f32[1024,512]{1,0:T(8,128)} %pad_maximum_fusion.1.raw_ref, f32[1024,128]{1,0:T(8,128)S(1)} %get-tuple-element.212.cos_ref, ...), custom_call_target="tpu_custom_call" | custom-call | tf_op jit(solution)/shard_map/attend_back/pallas_call | solution.py:223
  410.7 16.3 %all-to-all-done.5 = bf16[8,256,512]{2,1,0:T(8,128)(2,1)} async-done(((bf16[8,256,512]{2,1,0:T(8,128)(2,1)}), bf16[8,256,512]{2,1,0:T(8,128)(2,1)}, u32[]{:S(2)}, u32[]{:S(2)}) %all-to-all-start.5) | async-done | bytes 2097184 | tf_op jit(solution)/shard_map/all_to_all | solution.py:326
  439.0 12.3 %collective-permute-done.32 = bf16[128,2048]{1,0:T(8,128)(2,1)S(1)} collective-permute-done((bf16[128,2048]{1,0:T(8,128)(2,1)S(1)}, bf16[128,2048]{1,0:T(8,128)(2,1)S(1)}, u32[]{:S(2)}, u32[]{:S(2)}) %collective-permute-start.32) | collective-permute-done | bytes 524320 | tf_op jit(solution)/shard_map/ppermute | solution.py:322
  451.3 7.8 %collective-permute-done.31 = bf16[128,2048]{1,0:T(8,128)(2,1)S(1)} collective-permute-done((bf16[128,2048]{1,0:T(8,128)(2,1)S(1)}, bf16[128,2048]{1,0:T(8,128)(2,1)S(1)}, u32[]{:S(2)}, u32[]{:S(2)}) %collective-permute-start.31) | collective-permute-done | bytes 524320 | tf_op jit(solution)/shard_map/ppermute | solution.py:322
  472.4 13.2 %all-to-all-done.6.in_ref = bf16[8,64,1536]{2,1,0:T(8,128)(2,1)S(1)} async-done(((bf16[8,64,1536]{2,1,0:T(8,128)(2,1)}), bf16[8,64,1536]{2,1,0:T(8,128)(2,1)S(1)}, u32[]{:S(2)}, u32[]{:S(2)}) %all-to-all-start.6) | async-done | bytes 1572896 | tf_op jit(solution)/shard_map/all_to_all | solution.py:326
  (308 shorter events, 246.4 us)
Async XLA Ops:
  7.2 69.6 %all-gather.4.cloned.1.call-start = ((), (), s32[]{:S(2)}) async-start(), calls=%async_computation.11 | async-start | bytes 3932160 | tf_op jit(solution)/shard_map/all_gather | solution.py:388
  12.0 31.1 %all-to-all-start = ((bf16[4,128,2048]{2,1,0:T(8,128)(2,1)}), bf16[4,128,2048]{2,1,0:T(8,128)(2,1)}, u32[]{:S(2)}, u32[]{:S(2)}) async-start(bf16[4,128,2048]{2,1,0:T(8,128)(2,1)} %broadcast_in_dim.11), calls=%async_computation | async-start | bytes 4194304 | tf_op jit(solution)/shard_map/all_to_all | solution.py:326
  17.3 175.7 %all-gather.6.cloned.1.call-start = ((), (), s32[]{:S(2)}) async-start(), calls=%async_computation.12 | async-start | bytes 7864320 | tf_op jit(solution)/shard_map/all_gather | solution.py:388
  17.4 26.4 %collective-permute-start = (bf16[1,1088]{1,0:T(2,128)(2,1)S(1)}, bf16[1,1088]{1,0:T(2,128)(2,1)S(1)}, u32[]{:S(2)}, u32[]{:S(2)}) collective-permute-start(bf16[1,1088]{1,0:T(2,128)(2,1)S(1)} %reshape.172), channel_id=1, source_target_pairs={{0,1},{1,0},{2,3},{3,2},{4,5},{5,4},{6,7},{7,6},{8,9},{9,8},{10,11... | collective-permute-start | bytes 6536 | tf_op jit(solution)/shard_map/ppermute | solution.py:322
  43.0 29.9 %collective-permute-start.6 = (bf16[512,2048]{1,0:T(8,128)(2,1)}, bf16[512,2048]{1,0:T(8,128)(2,1)}, u32[]{:S(2)}, u32[]{:S(2)}) collective-permute-start(bf16[512,2048]{1,0:T(8,128)(2,1)} %bitcast.1), channel_id=1, source_target_pairs={{0,4},{4,0},{1,5},{5,1},{2,6},{6,2},{3,7},{7,3},{8,12},{12,8},{9,1... | collective-permute-start | bytes 6291464 | tf_op jit(solution)/shard_map/ppermute | solution.py:322
  46.4 25.7 %collective-permute-start.5 = (bf16[128,2048]{1,0:T(8,128)(2,1)S(1)}, bf16[128,2048]{1,0:T(8,128)(2,1)S(1)}, u32[]{:S(2)}, u32[]{:S(2)}) collective-permute-start(bf16[128,2048]{1,0:T(8,128)(2,1)S(1)} %bitcast.99), channel_id=1, source_target_pairs={{0,24},{8,16},{16,8},{24,0},{1,25},{9,17},{17,9},{25,1},{2,26},{10... | collective-permute-start | bytes 1572872 | tf_op jit(solution)/shard_map/ppermute | solution.py:322
  79.1 56.4 %collective-permute-start.7 = (bf16[2048,256]{1,0:T(8,128)(2,1)}, bf16[2048,256]{1,0:T(8,128)(2,1)S(1)}, u32[]{:S(2)}, u32[]{:S(2)}) collective-permute-start(bf16[2048,256]{1,0:T(8,128)(2,1)} %slice.85.refs_5_), channel_id=1, source_target_pairs={{0,8},{8,0},{16,24},{24,16},{1,9},{9,1},{17,25},{25,17},{2,10},{10... | collective-permute-start | bytes 3145736 | tf_op jit(solution)/shard_map/ppermute | solution.py:322
  80.6 55.0 %collective-permute-start.8 = (bf16[2048,256]{1,0:T(8,128)(2,1)}, bf16[2048,256]{1,0:T(8,128)(2,1)}, u32[]{:S(2)}, u32[]{:S(2)}) collective-permute-start(bf16[2048,256]{1,0:T(8,128)(2,1)} %slice.85.refs_5_), channel_id=1, source_target_pairs={{0,16},{8,24},{16,0},{24,8},{1,17},{9,25},{17,1},{25,9},{2,18},{10... | collective-permute-start | bytes 3145736 | tf_op jit(solution)/shard_map/ppermute | solution.py:322
  82.1 54.0 %collective-permute-start.9 = (bf16[2048,256]{1,0:T(8,128)(2,1)}, bf16[2048,256]{1,0:T(8,128)(2,1)}, u32[]{:S(2)}, u32[]{:S(2)}) collective-permute-start(bf16[2048,256]{1,0:T(8,128)(2,1)} %slice.85.refs_5_), channel_id=1, source_target_pairs={{0,24},{8,16},{16,8},{24,0},{1,25},{9,17},{17,9},{25,1},{2,26},{10... | collective-permute-start | bytes 3145736 | tf_op jit(solution)/shard_map/ppermute | solution.py:322
  105.9 27.7 %all-to-all-start.1 = ((bf16[8,128,256]{1,2,0:T(8,128)(2,1)}), bf16[8,128,256]{1,2,0:T(8,128)(2,1)}, u32[]{:S(2)}, u32[]{:S(2)}) async-start(bf16[8,128,256]{1,2,0:T(8,128)(2,1)} %copy.52), calls=%async_computation.1 | async-start | bytes 1048576 | tf_op jit(solution)/shard_map/all_to_all | solution.py:326
  110.1 147.5 %all-gather.8.cloned.1.call-start = ((), (), s32[]{:S(2)}) async-start(), calls=%async_computation.13 | async-start | bytes 3932160 | tf_op jit(solution)/shard_map/all_gather | solution.py:388
  110.2 30.9 %collective-permute-start.10 = (bf16[2048,256]{1,0:T(8,128)(2,1)}, bf16[2048,256]{1,0:T(8,128)(2,1)}, u32[]{:S(2)}, u32[]{:S(2)}) collective-permute-start(bf16[2048,256]{1,0:T(8,128)(2,1)} %slice.85.refs_5_), channel_id=1, source_target_pairs={{0,4},{4,0},{1,5},{5,1},{2,6},{6,2},{3,7},{7,3},{8,12},{12,8},{9,1... | collective-permute-start | bytes 3145736 | tf_op jit(solution)/shard_map/ppermute | solution.py:322
  179.3 139.0 %reduce-scatter.4.cloned.1.call-start = ((), (), s32[]{:S(2)}) async-start(), calls=%async_computation.14 | async-start | bytes 3932160 | tf_op jit(solution)/shard_map/reduce_scatter | solution.py:392
  179.6 27.9 %collective-permute-start.15 = (bf16[512,2048]{1,0:T(8,128)(2,1)}, bf16[512,2048]{1,0:T(8,128)(2,1)}, u32[]{:S(2)}, u32[]{:S(2)}) collective-permute-start(bf16[512,2048]{1,0:T(8,128)(2,1)} %constant_dynamic-update-slice_fusion.8), channel_id=1, source_target_pairs={{0,4},{4,0},{1,5},{5,1},{2,6},{6,2},{3,7},{7,3},{8,12},{12,8},{9,1... | collective-permute-start | bytes 6291464 | tf_op jit(solution)/shard_map/ppermute | solution.py:322
  226.9 28.6 %collective-permute-start.19 = (bf16[192,2048]{1,0:T(8,128)(2,1)}, bf16[192,2048]{1,0:T(8,128)(2,1)}, u32[]{:S(2)}, u32[]{:S(2)}) collective-permute-start(bf16[192,2048]{1,0:T(8,128)(2,1)} %get-tuple-element.171), channel_id=1, source_target_pairs={{0,24},{4,0},{8,8},{12,16},{16,28},{20,4},{24,12},{28,20},{1,25},{... | collective-permute-start | bytes 2359304 | tf_op jit(solution)/shard_map/ppermute | solution.py:480
  281.7 31.3 %all-to-all-start.3 = ((bf16[4,128,2048]{2,1,0:T(8,128)(2,1)}), bf16[4,128,2048]{2,1,0:T(8,128)(2,1)}, u32[]{:S(2)}, u32[]{:S(2)}) async-start(bf16[4,128,2048]{2,1,0:T(8,128)(2,1)} %bitcast.117), calls=%async_computation.3 | async-start | bytes 4194304 | tf_op jit(solution)/shard_map/all_to_all | solution.py:326
  286.2 174.5 %reduce-scatter.6.cloned.1.call-start = ((), (), s32[]{:S(2)}) async-start(), calls=%async_computation.15 | async-start | bytes 7864320 | tf_op jit(solution)/shard_map/reduce_scatter | solution.py:392
  329.5 31.7 %collective-permute-start.21 = (bf16[512,2048]{1,0:T(8,128)(2,1)}, bf16[512,2048]{1,0:T(8,128)(2,1)}, u32[]{:S(2)}, u32[]{:S(2)}) collective-permute-start(bf16[512,2048]{1,0:T(8,128)(2,1)} %convolution_convert_fusion.2), channel_id=1, source_target_pairs={{0,4},{4,0},{1,5},{5,1},{2,6},{6,2},{3,7},{7,3},{8,12},{12,8},{9,1... | collective-permute-start | bytes 6291464 | tf_op jit(solution)/shard_map/ppermute | solution.py:322
  331.0 26.4 %collective-permute-start.26 = (bf16[128,2048]{1,0:T(8,128)(2,1)}, bf16[128,2048]{1,0:T(8,128)(2,1)}, u32[]{:S(2)}, u32[]{:S(2)}) collective-permute-start(bf16[128,2048]{1,0:T(8,128)(2,1)} %get-tuple-element.80), channel_id=1, source_target_pairs={{0,16},{8,24},{16,0},{24,8},{1,17},{9,25},{17,1},{25,9},{2,18},{10... | collective-permute-start | bytes 1572872 | tf_op jit(solution)/shard_map/ppermute | solution.py:322
  332.5 26.7 %collective-permute-start.27 = (bf16[128,2048]{1,0:T(8,128)(2,1)}, bf16[128,2048]{1,0:T(8,128)(2,1)}, u32[]{:S(2)}, u32[]{:S(2)}) collective-permute-start(bf16[128,2048]{1,0:T(8,128)(2,1)} %get-tuple-element.80), channel_id=1, source_target_pairs={{0,24},{8,16},{16,8},{24,0},{1,25},{9,17},{17,9},{25,1},{2,26},{10... | collective-permute-start | bytes 1572872 | tf_op jit(solution)/shard_map/ppermute | solution.py:322
  333.1 32.9 %all-to-all-start.4 = ((bf16[8,128,256]{2,1,0:T(8,128)(2,1)}), bf16[8,128,256]{2,1,0:T(8,128)(2,1)S(1)}, u32[]{:S(2)}, u32[]{:S(2)}) async-start(bf16[8,128,256]{2,1,0:T(8,128)(2,1)} %copy-done.9), calls=%async_computation.5 | async-start | bytes 1048576 | tf_op jit(solution)/shard_map/all_to_all | solution.py:326
  367.6 25.9 %collective-permute-start.24 = (bf16[128,2048]{1,0:T(8,128)(2,1)S(1)}, bf16[128,2048]{1,0:T(8,128)(2,1)S(1)}, u32[]{:S(2)}, u32[]{:S(2)}) collective-permute-start(bf16[128,2048]{1,0:T(8,128)(2,1)S(1)} %get-tuple-element.181), channel_id=1, source_target_pairs={{0,24},{8,16},{16,8},{24,0},{1,25},{9,17},{17,9},{25,1},{2,26},{10... | collective-permute-start | bytes 1572872 | tf_op jit(solution)/shard_map/ppermute | solution.py:322
  395.9 31.1 %all-to-all-start.5 = ((bf16[8,256,512]{2,1,0:T(8,128)(2,1)}), bf16[8,256,512]{2,1,0:T(8,128)(2,1)}, u32[]{:S(2)}, u32[]{:S(2)}) async-start(bf16[8,256,512]{2,1,0:T(8,128)(2,1)} %bitcast.116), calls=%async_computation.6 | async-start | bytes 4194304 | tf_op jit(solution)/shard_map/all_to_all | solution.py:326
  400.3 96.7 %reduce-scatter.8.cloned.1.call-start = ((), (), s32[]{:S(2)}) async-start(), calls=%async_computation.16 | async-start | bytes 3932160 | tf_op jit(solution)/shard_map/reduce_scatter | solution.py:392
  (75 other events, 691.8 us)
Sparse Core Ops, SparseCore 0:
  10.5 66.2 all-gather.3
  78.9 114.0 all-gather.5
  194.6 61.7 all-gather.7
  258.5 59.7 reduce-scatter.3
  320.5 110.7 reduce-scatter.5
  433.9 60.3 reduce-scatter.7

commit v6 on v5

--- a/solution.py
+++ b/solution.py
@@ -541,29 +541,28 @@
     grad_gate_up = by_layer(sum_parts(ffn_parts, gate_up_grads))
     grad_ffn = send_chips(sum_cores(grad_ffn[0], grad_ffn[1]))
     grad_down = scatter_rows(grad_down)
-    grad_ffn, grad_gate_up, grad_down = after(grad_ffn, grad_gate_up, grad_down)
+    grad_ffn, grad_gate_up = after(grad_ffn, grad_gate_up)
     grad_gate_up = scatter_rows(grad_gate_up)
 
     grad_middle, middle_low, grad_gain_ffn, mixed_grad = project_back(
         jnp.stack(owners), grad_ffn, middle, own_cotangent, gain_ffn.reshape(1, -1), out_blocks
     )
-    mixed_grad, *hidden_parts = after(mixed_grad, *hidden_parts)
+    mixed_grad, grad_down, *hidden_parts = after(mixed_grad, grad_down, *hidden_parts)
     block_parts = [dot(values, down_w).astype(low) for values in hidden_parts]
     block_half = sum_cores(block_parts[0], block_parts[1])
     mixed_grad, block_half = after(exchange(mixed_grad, CTX), block_half)
     block_sum = sum_chips(block_half)
     mixed_grad = mixed_grad.reshape(total, qw)
-    late_half = in_order(spread(middle_low, "chip"), chip)
     qkv_grad, grad_gains = attend_back(
         total, heads, sources, places, qkv_raw, *tables, query, key, value, logs, mixed_grad
     )
-    qkv_grad, late_half = after(qkv_grad, late_half)
-    grad_out = sum_parts(halves(mixed_rel), (late_half, swap(late_half, "core")))
     qkv_grads = halves(qkv_grad)
     grad_attn = [dot_t(grads, qkv_w).astype(low) for grads in qkv_grads]
     attn_half = sum_cores(grad_attn[0], grad_attn[1])
     grad_qkv = sum_parts(normed_parts, qkv_grads).reshape(n, m * strip, -1)
-    block_sum, grad_qkv = after(block_sum, grad_qkv)
+    block_sum, grad_qkv, late_low = after(block_sum, grad_qkv, middle_low)
+    late_half = in_order(spread(late_low, "chip"), chip)
+    grad_out = sum_parts(halves(mixed_rel), (late_half, swap(late_half, "core")))
     block_out = (middle + block_sum).astype(low).reshape(tokens.shape)
     grad_qkv = exchange(grad_qkv, CTX).reshape(n, m, strip, -1)
 

time: 516 us -> 514 us (level)
    unnamed x116 -> x108, local copies, waits for them, and re-layouts: 14.1 us -> 16.4 us
  transfers between devices with their start and end apart: 46 -> 46, of which waited for: 20 -> 24; matrix products, arithmetic and copies ran while one was open for 36% -> 36% of each run, Pallas kernels for 6% -> 5%
where the time goes in v6:
time: 514 us; the launch traced here: 507 us
  waiting for transfers between devices  157 us (31%)
  matrix products  109 us (21%)
  starting transfers between devices  69.7 us (14%)
  local copies, waits for them, and re-layouts  68.9 us (13%)
  other arithmetic  29.8 us (6%)
  blocking collectives  29.5 us (6%)
  Pallas kernels  27.4 us (5%)
  between operations  15.6 us (3%)
    all_to_all x7, waiting for transfers between devices, exchange(): return lax.all_to_all(values, axis, 0, 0, tiled=True)  74 us
    ppermute x29, waiting for transfers between devices, swap(): return lax.ppermute(values, axis, [(i, i ^ mask) for i in range(size)])  55.1 us
    dot_general x14, matrix products, dot(): return jnp.dot(left, right, preferred_element_type=high)  43.5 us
    dot_general x8, matrix products, t_dot(): lax.dot_general(left, right, (((0,), (0,)), ((), ())), preferred_element_...  37.2 us
    all_to_all x1, blocking collectives, exchange(): return lax.all_to_all(values, axis, 0, 0, tiled=True)  29.5 us
    all_to_all x7, starting transfers between devices, exchange(): return lax.all_to_all(values, axis, 0, 0, tiled=True)  28.4 us
    dot_general x6, matrix products, dot_t(): lax.dot_general(left, right, (((1,), (1,)), ((), ())), preferred_element_...  28.3 us
    ppermute x29, starting transfers between devices, swap(): return lax.ppermute(values, axis, [(i, i ^ mask) for i in range(size)])  26.2 us
  transfers between devices with their start and end apart: 46, of which 24 were waited for; matrix products, arithmetic and copies ran while one was open for 36% of the time, Pallas kernels for 5%

profile of v6, /device:TPU:0, one launch (start us, length us, event | category | flops | bytes accessed | tf_op | source)
XLA Modules:
  0.0 507.0 jit_solution(11529318364435959968)
XLA Ops:
  32.2 10.8 %all-to-all-done = bf16[4,128,2048]{2,1,0:T(8,128)(2,1)} async-done(((bf16[4,128,2048]{2,1,0:T(8,128)(2,1)}), bf16[4,128,2048]{2,1,0:T(8,128)(2,1)}, u32[]{:S(2)}, u32[]{:S(2)}) %all-to-all-start) | async-done | bytes 2097184 | tf_op jit(solution)/shard_map/all_to_all | solution.py:326
  52.5 6.8 %collective-permute-done.3 = bf16[128,2048]{1,0:T(8,128)(2,1)} collective-permute-done((bf16[128,2048]{1,0:T(8,128)(2,1)S(1)}, bf16[128,2048]{1,0:T(8,128)(2,1)}, u32[]{:S(2)}, u32[]{:S(2)}) %collective-permute-start.3) | collective-permute-done | bytes 524320 | tf_op jit(solution)/shard_map/ppermute | solution.py:322
  61.1 10.1 %collective-permute-done.4 = bf16[128,2048]{1,0:T(8,128)(2,1)S(1)} collective-permute-done((bf16[128,2048]{1,0:T(8,128)(2,1)S(1)}, bf16[128,2048]{1,0:T(8,128)(2,1)S(1)}, u32[]{:S(2)}, u32[]{:S(2)}) %collective-permute-start.4) | collective-permute-done | bytes 524320 | tf_op jit(solution)/shard_map/ppermute | solution.py:322
  91.1 8.8 %attend.1 = (bf16[1024,256]{1,0:T(8,128)(2,1)S(1)}, bf16[1024,256]{1,0:T(8,128)(2,1)S(1)}, bf16[1024,256]{1,0:T(8,128)(2,1)S(1)}, bf16[1024,128]{1,0:T(8,128)(2,...) custom-call(s32[16]{0:T(128)S(1)} %get-tuple-element.201.sources_ref, ...), custom_call_target="tpu_custom_call" | custom-call | tf_op jit(solution)/shard_map/attend/pallas_call | solution.py:208
  110.5 23.1 %all-to-all-done.1 = bf16[8,128,256]{1,2,0:T(8,128)(2,1)} async-done(((bf16[8,128,256]{1,2,0:T(8,128)(2,1)}), bf16[8,128,256]{1,2,0:T(8,128)(2,1)}, u32[]{:S(2)}, u32[]{:S(2)}) %all-to-all-start.1) | async-done | bytes 524320 | tf_op jit(solution)/shard_map/all_to_all | solution.py:326
  149.8 29.5 %all_to_all.44 = bf16[4,128,2048]{2,1,0:T(8,128)(2,1)} all-to-all(bf16[4,128,2048]{2,1,0:T(8,128)(2,1)S(1)} %broadcast_in_dim.14), channel_id=1, replica_groups=mesh['chip'=4,'core'=2,'hi'=2,'lo'=2] {'chip'}, dimensions={0} | all-to-all | bytes 4194304 | tf_op jit(solution)/shard_map/all_to_all | solution.py:326
  183.8 9.2 %all-gather.6.cloned.1.call-done = bf16[2048,1536]{1,0:T(8,128)(2,1)} async-done(((bf16[512,1536]{1,0:T(8,128)(2,1)}), bf16[2048,1536]{1,0:T(8,128)(2,1)}) %all-gather.6.cloned.1.call-update) | async-done | bytes 6291472 | tf_op jit(solution)/shard_map/all_gather | solution.py:388
  193.0 6.3 %fusion.47 = f32[512,1536]{1,0:T(8,128)S(1)} fusion(bf16[512,2048]{1,0:T(8,128)(2,1)} %collective-permute-done.14, bf16[2048,1536]{1,0:T(8,128)(2,1)} %all-gather.6.cloned.1.call-done), kind=kOutput, calls=%fused_computation.154 | convolution fusion | flops 3221225472 | bytes 11534336 | tf_op jit(solution)/shard_map/dot_general | solution.py:26
  201.6 5.4 %fusion.46 = f32[512,1536]{1,0:T(8,128)S(1)} fusion(bf16[512,2048]{1,0:T(8,128)(2,1)} %bitcast.17, bf16[2048,1536]{1,0:T(8,128)(2,1)S(1)} %copy-done.39), kind=kOutput, calls=%fused_computation.153 | convolution fusion | flops 3221225472 | bytes 11534336 | tf_op jit(solution)/shard_map/dot_general | solution.py:26
  217.5 7.4 %collective-permute-start.16 = (bf16[192,2048]{1,0:T(8,128)(2,1)}, bf16[192,2048]{1,0:T(8,128)(2,1)}, u32[]{:S(2)}, u32[]{:S(2)}) collective-permute-start(bf16[192,2048]{1,0:T(8,128)(2,1)} %get-tuple-element.172), channel_id=1, source_target_pairs={{0,0},{4,8},{8,16},{12,24},{16,4},{20,12},{24,20},{28,28},{1,1},{5... | collective-permute-start | bytes 2359304 | tf_op jit(solution)/shard_map/ppermute | solution.py:480
  236.1 11.0 %collective-permute-done.17 = bf16[192,2048]{1,0:T(8,128)(2,1)} collective-permute-done((bf16[192,2048]{1,0:T(8,128)(2,1)}, bf16[192,2048]{1,0:T(8,128)(2,1)}, u32[]{:S(2)}, u32[]{:S(2)}) %collective-permute-start.17) | collective-permute-done | bytes 786464 | tf_op jit(solution)/shard_map/ppermute | solution.py:480
  257.6 5.6 %multiply_convert_fusion.1 = (bf16[512,768]{1,0:T(8,128)(2,1)S(1)}, bf16[512,768]{1,0:T(8,128)(2,1)S(1)}) fusion(f32[512,1536]{1,0:T(8,128)} %copy-done.29, bf16[512,2048]{1,0:T(8,128)(2,1)} %collective-permute-done.15, bf16[768,2048]{1,0:T(8,128)(2,1)} %all-gather.8.cloned.1.call-done), kind=kOutput, calls=%fused_computation.35 | convolution fusion | flops 1615724544 | bytes 9961472 | tf_op jit(solution)/shard_map/dot_general | solution.py:30
  264.4 6.6 %convolution_convert_fusion.4 = bf16[512,2048]{1,0:T(8,128)(2,1)S(1)} fusion(bf16[2048,1536]{1,0:T(8,128)(2,1)} %all-gather.6.cloned.1.call-done, bf16[512,768]{1,0:T(8,128)(2,1)S(1)} %get-tuple-element.168, bf16[512,768]{1,0:T(8,128)(2,1)S(1)} %get-tuple-element.167), kind=kOutput, calls=%fused_computation.22 | convolution fusion | flops 3225419776 | bytes 9961472 | tf_op jit(solution)/shard_map/dot_general | solution.py:30
  286.4 10.2 %fusion.21 = f32[2048,1536]{1,0:T(8,128)} fusion(bf16[512,2048]{1,0:T(8,128)(2,1)} %bitcast.17, bf16[512,768]{1,0:T(8,128)(2,1)} %copy-done.42, bf16[512,768]{1,0:T(8,128)(2,1)} %copy-done.41), kind=kOutput, calls=%fused_computation.69 | convolution fusion | flops 3224371200 | bytes 16252928 | tf_op jit(solution)/shard_map/dot_general | solution.py:34
  296.6 7.4 %add_convert_fusion = bf16[2048,1536]{1,0:T(8,128)(2,1)S(1)} fusion(f32[2048,1536]{1,0:T(8,128)} %fusion.21, bf16[512,2048]{1,0:T(8,128)(2,1)} %collective-permute-done.14, bf16[512,768]{1,0:T(8,128)(2,1)S(1)} %copy-done.46, bf16[512,768]{1,0:T(8,128)(2,1)S(1)} %copy-done.44), kind=kOutput, calls=%fused_computation | convolution fusion | flops 3230662656 | bytes 22544384 | tf_op jit(solution)/shard_map/dot_general | solution.py:34
  307.2 5.7 %all-to-all-done.3.refs_1_ = bf16[4,128,2048]{2,1,0:T(8,128)(2,1)} async-done(((bf16[4,128,2048]{2,1,0:T(8,128)(2,1)}), bf16[4,128,2048]{2,1,0:T(8,128)(2,1)}, u32[]{:S(2)}, u32[]{:S(2)}) %all-to-all-start.3) | async-done | bytes 2097184 | tf_op jit(solution)/shard_map/all_to_all | solution.py:326
  314.4 6.0 %project_back.1 = (f32[128,2048]{1,0:T(8,128)S(1)}, bf16[128,2048]{1,0:T(8,128)(2,1)S(1)}, f32[1,2048]{1,0:T(1,128)S(1)}, bf16[8,128,256]{2,1,0:T(8,128)(2,1)S(1)}) custom-call(s32[8]{0:T(128)S(1)} %stack.35.refs_0_, bf16[4,128,2048]{2,1,0:T(8,128)(2,1)} %all-to-all-done.3.refs_1_, f32[128,2048]{1,0:T(8,128)S(1)} %get-tuple-element.156.refs_2_, ...), custom_call_target="tpu_custom_call" | custom-call | tf_op jit(solution)/shard_map/project_back/pallas_call | solution.py:281
  332.7 5.9 %add_convert_fusion.4 = bf16[512,2048]{1,0:T(8,128)(2,1)} fusion(bf16[512,2048]{1,0:T(8,128)(2,1)} %collective-permute-done.21, bf16[512,768]{1,0:T(8,128)(2,1)} %copy-done.34, bf16[768,2048]{1,0:T(8,128)(2,1)} %all-gather.8.cloned.1.call-done), kind=kOutput, calls=%fused_computation.14 | convolution fusion | flops 1615855616 | bytes 8126464 | tf_op jit(solution)/shard_map/dot_general | solution.py:26
  346.8 10.7 %attend_back.1 = (bf16[1024,512]{1,0:T(8,128)(2,1)S(1)}, f32[2,128]{1,0:T(2,128)S(1)}) custom-call(s32[16]{0:T(128)S(1)} %get-tuple-element.201.sources_ref, s32[16]{0:T(128)S(1)} %get-tuple-element.200.places_ref, f32[1024,512]{1,0:T(8,128)} %pad_maximum_fusion.1.raw_ref, f32[1024,128]{1,0:T(8,128)S(1)} %get-tuple-element.210.cos_ref, ...), custom_call_target="tpu_custom_call" | custom-call | tf_op jit(solution)/shard_map/attend_back/pallas_call | solution.py:223
  386.5 8.9 %collective-permute-done.26 = bf16[128,2048]{1,0:T(8,128)(2,1)S(1)} collective-permute-done((bf16[128,2048]{1,0:T(8,128)(2,1)S(1)}, bf16[128,2048]{1,0:T(8,128)(2,1)S(1)}, u32[]{:S(2)}, u32[]{:S(2)}) %collective-permute-start.26) | collective-permute-done | bytes 524320 | tf_op jit(solution)/shard_map/ppermute | solution.py:322
  403.6 14.9 %all-to-all-done.5 = bf16[8,256,512]{2,1,0:T(8,128)(2,1)} async-done(((bf16[8,256,512]{2,1,0:T(8,128)(2,1)}), bf16[8,256,512]{2,1,0:T(8,128)(2,1)}, u32[]{:S(2)}, u32[]{:S(2)}) %all-to-all-start.5) | async-done | bytes 2097184 | tf_op jit(solution)/shard_map/all_to_all | solution.py:326
  434.9 12.3 %collective-permute-done.32 = bf16[128,2048]{1,0:T(8,128)(2,1)S(1)} collective-permute-done((bf16[128,2048]{1,0:T(8,128)(2,1)S(1)}, bf16[128,2048]{1,0:T(8,128)(2,1)S(1)}, u32[]{:S(2)}, u32[]{:S(2)}) %collective-permute-start.32) | collective-permute-done | bytes 524320 | tf_op jit(solution)/shard_map/ppermute | solution.py:322
  447.2 8.7 %collective-permute-done.31 = bf16[128,2048]{1,0:T(8,128)(2,1)S(1)} collective-permute-done((bf16[128,2048]{1,0:T(8,128)(2,1)S(1)}, bf16[128,2048]{1,0:T(8,128)(2,1)S(1)}, u32[]{:S(2)}, u32[]{:S(2)}) %collective-permute-start.31) | collective-permute-done | bytes 524320 | tf_op jit(solution)/shard_map/ppermute | solution.py:322
  468.9 13.2 %all-to-all-done.6.in_ref = bf16[8,64,1536]{2,1,0:T(8,128)(2,1)S(1)} async-done(((bf16[8,64,1536]{2,1,0:T(8,128)(2,1)}), bf16[8,64,1536]{2,1,0:T(8,128)(2,1)S(1)}, u32[]{:S(2)}, u32[]{:S(2)}) %all-to-all-start.6) | async-done | bytes 1572896 | tf_op jit(solution)/shard_map/all_to_all | solution.py:326
  (300 shorter events, 246.9 us)
Async XLA Ops:
  7.2 69.6 %all-gather.4.cloned.1.call-start = ((), (), s32[]{:S(2)}) async-start(), calls=%async_computation.11 | async-start | bytes 3932160 | tf_op jit(solution)/shard_map/all_gather | solution.py:388
  12.0 31.1 %all-to-all-start = ((bf16[4,128,2048]{2,1,0:T(8,128)(2,1)}), bf16[4,128,2048]{2,1,0:T(8,128)(2,1)}, u32[]{:S(2)}, u32[]{:S(2)}) async-start(bf16[4,128,2048]{2,1,0:T(8,128)(2,1)} %broadcast_in_dim.11), calls=%async_computation | async-start | bytes 4194304 | tf_op jit(solution)/shard_map/all_to_all | solution.py:326
  17.3 175.7 %all-gather.6.cloned.1.call-start = ((), (), s32[]{:S(2)}) async-start(), calls=%async_computation.12 | async-start | bytes 7864320 | tf_op jit(solution)/shard_map/all_gather | solution.py:388
  17.4 26.4 %collective-permute-start = (bf16[1,1088]{1,0:T(2,128)(2,1)S(1)}, bf16[1,1088]{1,0:T(2,128)(2,1)S(1)}, u32[]{:S(2)}, u32[]{:S(2)}) collective-permute-start(bf16[1,1088]{1,0:T(2,128)(2,1)S(1)} %reshape.172), channel_id=1, source_target_pairs={{0,1},{1,0},{2,3},{3,2},{4,5},{5,4},{6,7},{7,6},{8,9},{9,8},{10,11... | collective-permute-start | bytes 6536 | tf_op jit(solution)/shard_map/ppermute | solution.py:322
  19.8 24.0 %collective-permute-start.1 = (bf16[1,1088]{1,0:T(2,128)(2,1)S(1)}, bf16[1,1088]{1,0:T(2,128)(2,1)S(1)}, u32[]{:S(2)}, u32[]{:S(2)}) collective-permute-start(bf16[1,1088]{1,0:T(2,128)(2,1)S(1)} %reshape.172), channel_id=1, source_target_pairs={{0,2},{1,3},{2,0},{3,1},{4,6},{5,7},{6,4},{7,5},{8,10},{9,11},{10,... | collective-permute-start | bytes 6536 | tf_op jit(solution)/shard_map/ppermute | solution.py:322
  43.0 29.9 %collective-permute-start.6 = (bf16[512,2048]{1,0:T(8,128)(2,1)}, bf16[512,2048]{1,0:T(8,128)(2,1)}, u32[]{:S(2)}, u32[]{:S(2)}) collective-permute-start(bf16[512,2048]{1,0:T(8,128)(2,1)} %bitcast.1), channel_id=1, source_target_pairs={{0,4},{4,0},{1,5},{5,1},{2,6},{6,2},{3,7},{7,3},{8,12},{12,8},{9,1... | collective-permute-start | bytes 6291464 | tf_op jit(solution)/shard_map/ppermute | solution.py:322
  45.9 25.3 %collective-permute-start.4 = (bf16[128,2048]{1,0:T(8,128)(2,1)S(1)}, bf16[128,2048]{1,0:T(8,128)(2,1)S(1)}, u32[]{:S(2)}, u32[]{:S(2)}) collective-permute-start(bf16[128,2048]{1,0:T(8,128)(2,1)S(1)} %bitcast.98), channel_id=1, source_target_pairs={{0,16},{8,24},{16,0},{24,8},{1,17},{9,25},{17,1},{25,9},{2,18},{10... | collective-permute-start | bytes 1572872 | tf_op jit(solution)/shard_map/ppermute | solution.py:322
  46.4 25.7 %collective-permute-start.5 = (bf16[128,2048]{1,0:T(8,128)(2,1)S(1)}, bf16[128,2048]{1,0:T(8,128)(2,1)S(1)}, u32[]{:S(2)}, u32[]{:S(2)}) collective-permute-start(bf16[128,2048]{1,0:T(8,128)(2,1)S(1)} %bitcast.99), channel_id=1, source_target_pairs={{0,24},{8,16},{16,8},{24,0},{1,25},{9,17},{17,9},{25,1},{2,26},{10... | collective-permute-start | bytes 1572872 | tf_op jit(solution)/shard_map/ppermute | solution.py:322
  79.1 56.4 %collective-permute-start.7 = (bf16[2048,256]{1,0:T(8,128)(2,1)}, bf16[2048,256]{1,0:T(8,128)(2,1)S(1)}, u32[]{:S(2)}, u32[]{:S(2)}) collective-permute-start(bf16[2048,256]{1,0:T(8,128)(2,1)} %slice.85.refs_5_), channel_id=1, source_target_pairs={{0,8},{8,0},{16,24},{24,16},{1,9},{9,1},{17,25},{25,17},{2,10},{10... | collective-permute-start | bytes 3145736 | tf_op jit(solution)/shard_map/ppermute | solution.py:322
  80.6 55.0 %collective-permute-start.8 = (bf16[2048,256]{1,0:T(8,128)(2,1)}, bf16[2048,256]{1,0:T(8,128)(2,1)}, u32[]{:S(2)}, u32[]{:S(2)}) collective-permute-start(bf16[2048,256]{1,0:T(8,128)(2,1)} %slice.85.refs_5_), channel_id=1, source_target_pairs={{0,16},{8,24},{16,0},{24,8},{1,17},{9,25},{17,1},{25,9},{2,18},{10... | collective-permute-start | bytes 3145736 | tf_op jit(solution)/shard_map/ppermute | solution.py:322
  82.1 54.0 %collective-permute-start.9 = (bf16[2048,256]{1,0:T(8,128)(2,1)}, bf16[2048,256]{1,0:T(8,128)(2,1)}, u32[]{:S(2)}, u32[]{:S(2)}) collective-permute-start(bf16[2048,256]{1,0:T(8,128)(2,1)} %slice.85.refs_5_), channel_id=1, source_target_pairs={{0,24},{8,16},{16,8},{24,0},{1,25},{9,17},{17,9},{25,1},{2,26},{10... | collective-permute-start | bytes 3145736 | tf_op jit(solution)/shard_map/ppermute | solution.py:322
  105.9 27.7 %all-to-all-start.1 = ((bf16[8,128,256]{1,2,0:T(8,128)(2,1)}), bf16[8,128,256]{1,2,0:T(8,128)(2,1)}, u32[]{:S(2)}, u32[]{:S(2)}) async-start(bf16[8,128,256]{1,2,0:T(8,128)(2,1)} %copy.52), calls=%async_computation.1 | async-start | bytes 1048576 | tf_op jit(solution)/shard_map/all_to_all | solution.py:326
  110.1 147.6 %all-gather.8.cloned.1.call-start = ((), (), s32[]{:S(2)}) async-start(), calls=%async_computation.13 | async-start | bytes 3932160 | tf_op jit(solution)/shard_map/all_gather | solution.py:388
  110.2 31.0 %collective-permute-start.10 = (bf16[2048,256]{1,0:T(8,128)(2,1)}, bf16[2048,256]{1,0:T(8,128)(2,1)}, u32[]{:S(2)}, u32[]{:S(2)}) collective-permute-start(bf16[2048,256]{1,0:T(8,128)(2,1)} %slice.85.refs_5_), channel_id=1, source_target_pairs={{0,4},{4,0},{1,5},{5,1},{2,6},{6,2},{3,7},{7,3},{8,12},{12,8},{9,1... | collective-permute-start | bytes 3145736 | tf_op jit(solution)/shard_map/ppermute | solution.py:322
  179.3 143.6 %reduce-scatter.4.cloned.1.call-start = ((), (), s32[]{:S(2)}) async-start(), calls=%async_computation.14 | async-start | bytes 3932160 | tf_op jit(solution)/shard_map/reduce_scatter | solution.py:392
  179.6 27.9 %collective-permute-start.15 = (bf16[512,2048]{1,0:T(8,128)(2,1)}, bf16[512,2048]{1,0:T(8,128)(2,1)}, u32[]{:S(2)}, u32[]{:S(2)}) collective-permute-start(bf16[512,2048]{1,0:T(8,128)(2,1)} %constant_dynamic-update-slice_fusion.8), channel_id=1, source_target_pairs={{0,4},{4,0},{1,5},{5,1},{2,6},{6,2},{3,7},{7,3},{8,12},{12,8},{9,1... | collective-permute-start | bytes 6291464 | tf_op jit(solution)/shard_map/ppermute | solution.py:322
  226.9 25.3 %collective-permute-start.18 = (bf16[192,2048]{1,0:T(8,128)(2,1)}, bf16[192,2048]{1,0:T(8,128)(2,1)}, u32[]{:S(2)}, u32[]{:S(2)}) collective-permute-start(bf16[192,2048]{1,0:T(8,128)(2,1)} %get-tuple-element.170), channel_id=1, source_target_pairs={{0,16},{4,24},{8,0},{12,8},{16,20},{20,28},{24,4},{28,12},{1,17},{... | collective-permute-start | bytes 2359304 | tf_op jit(solution)/shard_map/ppermute | solution.py:480
  227.0 28.5 %collective-permute-start.19 = (bf16[192,2048]{1,0:T(8,128)(2,1)}, bf16[192,2048]{1,0:T(8,128)(2,1)}, u32[]{:S(2)}, u32[]{:S(2)}) collective-permute-start(bf16[192,2048]{1,0:T(8,128)(2,1)} %get-tuple-element.169), channel_id=1, source_target_pairs={{0,24},{4,0},{8,8},{12,16},{16,28},{20,4},{24,12},{28,20},{1,25},{... | collective-permute-start | bytes 2359304 | tf_op jit(solution)/shard_map/ppermute | solution.py:480
  281.7 31.3 %all-to-all-start.3 = ((bf16[4,128,2048]{2,1,0:T(8,128)(2,1)}), bf16[4,128,2048]{2,1,0:T(8,128)(2,1)}, u32[]{:S(2)}, u32[]{:S(2)}) async-start(bf16[4,128,2048]{2,1,0:T(8,128)(2,1)} %bitcast.117), calls=%async_computation.3 | async-start | bytes 4194304 | tf_op jit(solution)/shard_map/all_to_all | solution.py:326
  286.1 171.1 %reduce-scatter.6.cloned.1.call-start = ((), (), s32[]{:S(2)}) async-start(), calls=%async_computation.15 | async-start | bytes 7864320 | tf_op jit(solution)/shard_map/reduce_scatter | solution.py:392
  378.4 40.0 %all-to-all-start.5 = ((bf16[8,256,512]{2,1,0:T(8,128)(2,1)}), bf16[8,256,512]{2,1,0:T(8,128)(2,1)}, u32[]{:S(2)}, u32[]{:S(2)}) async-start(bf16[8,256,512]{2,1,0:T(8,128)(2,1)} %bitcast.116), calls=%async_computation.6 | async-start | bytes 4194304 | tf_op jit(solution)/shard_map/all_to_all | solution.py:326
  382.8 112.0 %reduce-scatter.8.cloned.1.call-start = ((), (), s32[]{:S(2)}) async-start(), calls=%async_computation.16 | async-start | bytes 3932160 | tf_op jit(solution)/shard_map/reduce_scatter | solution.py:392
  398.6 24.3 %collective-permute-start.28 = (bf16[512,2048]{1,0:T(8,128)(2,1)}, bf16[512,2048]{1,0:T(8,128)(2,1)}, u32[]{:S(2)}, u32[]{:S(2)}) collective-permute-start(bf16[512,2048]{1,0:T(8,128)(2,1)} %constant_dynamic-update-slice_fusion), channel_id=1, source_target_pairs={{0,4},{4,0},{1,5},{5,1},{2,6},{6,2},{3,7},{7,3},{8,12},{12,8},{9,1... | collective-permute-start | bytes 6291464 | tf_op jit(solution)/shard_map/ppermute | solution.py:322
  457.2 24.9 %all-to-all-start.6 = ((bf16[8,64,1536]{2,1,0:T(8,128)(2,1)}), bf16[8,64,1536]{2,1,0:T(8,128)(2,1)S(1)}, u32[]{:S(2)}, u32[]{:S(2)}) async-start(bf16[8,64,1536]{2,1,0:T(8,128)(2,1)} %bitcast.120), calls=%async_computation.9 | async-start | bytes 3145728 | tf_op jit(solution)/shard_map/all_to_all | solution.py:326
  (71 other events, 613.5 us)
Sparse Core Ops, SparseCore 0:
  10.5 66.2 all-gather.3
  78.9 114.0 all-gather.5
  194.6 61.7 all-gather.7
  258.5 59.8 reduce-scatter.3
  320.5 110.7 reduce-scatter.5
  433.5 61.2 reduce-scatter.7

commit v7 on v6

--- a/solution.py
+++ b/solution.py
@@ -313,6 +313,26 @@
     )(grads)
 
 
+def widen_kernel(in_ref, *out_refs):
+    start = 0
+    for out_ref in out_refs:
+        end = start + out_ref.shape[1]
+        out_ref[...] = in_ref[:, start:end].astype(high)
+        start = end
+
+
+def widen(values, widths):
+    rows = values.shape[0]
+    return pl.pallas_call(
+        widen_kernel,
+        out_shape=tuple(jax.ShapeDtypeStruct((rows, width), high) for width in widths),
+        in_specs=in_memory([pltpu.VMEM]),
+        out_specs=in_memory([pltpu.VMEM] * len(widths)),
+        compiler_params=pltpu.CompilerParams(vmem_limit_bytes=vmem_bytes),
+        name="widen",
+    )(values)
+
+
 CTX = ("chip", "core")
 LAYER = ("hi", "lo")
 
@@ -608,24 +628,23 @@
     gains = jnp.sum(gains, axis=0)
     grad_down = grad_down.astype(high)
     grad_gate, grad_up = arrange(grad_gate_up, piece)
-    grad_late, gains = after(grad_late, gains)
-    ends = [0, n * qw, n * qw + KVH * HD, n * qw + 2 * KVH * HD, grad_late.shape[1]]
-    grad_query, grad_key, grad_value, grad_out = [
-        grad_late[:, start:end].astype(high) for start, end in zip(ends, ends[1:])
-    ]
-
     end = 2 * strip + HD // devices
+    gains = (gains[:strip], gains[strip : 2 * strip], gains[2 * strip : end], gains[end:])
+    grad_late, *gains = after(grad_late, *gains)
+    widths = (n * qw, KVH * HD, KVH * HD, width)
+    grad_query, grad_key, grad_value, grad_out = widen(grad_late, widths)
+
     return (
         block_out,
         input_grad,
-        gains[:strip],
+        gains[0],
         grad_query,
         grad_key,
         grad_value,
-        gains[2 * strip : end],
-        gains[end:],
+        gains[2],
+        gains[3],
         grad_out,
-        gains[strip : 2 * strip],
+        gains[1],
         grad_gate,
         grad_up,
         grad_down,

time: 514 us -> 511 us (level)
    unnamed x108 -> x107, local copies, waits for them, and re-layouts: 16.4 us -> 16.7 us
  transfers between devices with their start and end apart: 46 -> 46, of which waited for: 24 -> 25; matrix products, arithmetic and copies ran while one was open for 36% -> 37% of each run, Pallas kernels for 5% -> 5%
where the time goes in v7:
time: 511 us; the launch traced here: 504 us
  waiting for transfers between devices  156 us (31%)
  matrix products  109 us (21%)
  starting transfers between devices  69.7 us (14%)
  local copies, waits for them, and re-layouts  69.5 us (14%)
  blocking collectives  29.5 us (6%)
  Pallas kernels  28.6 us (6%)
  other arithmetic  26 us (5%)
  between operations  15.6 us (3%)
    all_to_all x7, waiting for transfers between devices, exchange(): return lax.all_to_all(values, axis, 0, 0, tiled=True)  74 us
    ppermute x29, waiting for transfers between devices, swap(): return lax.ppermute(values, axis, [(i, i ^ mask) for i in range(size)])  55.1 us
    dot_general x14, matrix products, dot(): return jnp.dot(left, right, preferred_element_type=high)  43.5 us
    dot_general x8, matrix products, t_dot(): lax.dot_general(left, right, (((0,), (0,)), ((), ())), preferred_element_...  37.3 us
    all_to_all x1, blocking collectives, exchange(): return lax.all_to_all(values, axis, 0, 0, tiled=True)  29.5 us
    all_to_all x7, starting transfers between devices, exchange(): return lax.all_to_all(values, axis, 0, 0, tiled=True)  28.5 us
    dot_general x6, matrix products, dot_t(): lax.dot_general(left, right, (((1,), (1,)), ((), ())), preferred_element_...  28.3 us
    ppermute x29, starting transfers between devices, swap(): return lax.ppermute(values, axis, [(i, i ^ mask) for i in range(size)])  26.2 us
  transfers between devices with their start and end apart: 46, of which 25 were waited for; matrix products, arithmetic and copies ran while one was open for 37% of the time, Pallas kernels for 5%

profile of v7, /device:TPU:0, one launch (start us, length us, event | category | flops | bytes accessed | tf_op | source)
XLA Modules:
  0.0 504.2 jit_solution(14636991717292070820)
XLA Ops:
  32.2 10.8 %all-to-all-done = bf16[4,128,2048]{2,1,0:T(8,128)(2,1)} async-done(((bf16[4,128,2048]{2,1,0:T(8,128)(2,1)}), bf16[4,128,2048]{2,1,0:T(8,128)(2,1)}, u32[]{:S(2)}, u32[]{:S(2)}) %all-to-all-start) | async-done | bytes 2097184 | tf_op jit(solution)/shard_map/all_to_all | solution.py:346
  52.5 6.8 %collective-permute-done.3 = bf16[128,2048]{1,0:T(8,128)(2,1)} collective-permute-done((bf16[128,2048]{1,0:T(8,128)(2,1)S(1)}, bf16[128,2048]{1,0:T(8,128)(2,1)}, u32[]{:S(2)}, u32[]{:S(2)}) %collective-permute-start.3) | collective-permute-done | bytes 524320 | tf_op jit(solution)/shard_map/ppermute | solution.py:342
  61.1 10.1 %collective-permute-done.4 = bf16[128,2048]{1,0:T(8,128)(2,1)S(1)} collective-permute-done((bf16[128,2048]{1,0:T(8,128)(2,1)S(1)}, bf16[128,2048]{1,0:T(8,128)(2,1)S(1)}, u32[]{:S(2)}, u32[]{:S(2)}) %collective-permute-start.4) | collective-permute-done | bytes 524320 | tf_op jit(solution)/shard_map/ppermute | solution.py:342
  91.1 8.8 %attend.1 = (bf16[1024,256]{1,0:T(8,128)(2,1)S(1)}, bf16[1024,256]{1,0:T(8,128)(2,1)S(1)}, bf16[1024,256]{1,0:T(8,128)(2,1)S(1)}, bf16[1024,128]{1,0:T(8,128)(2,...) custom-call(s32[16]{0:T(128)S(1)} %get-tuple-element.211.sources_ref, ...), custom_call_target="tpu_custom_call" | custom-call | tf_op jit(solution)/shard_map/attend/pallas_call | solution.py:208
  110.5 23.1 %all-to-all-done.1 = bf16[8,128,256]{1,2,0:T(8,128)(2,1)} async-done(((bf16[8,128,256]{1,2,0:T(8,128)(2,1)}), bf16[8,128,256]{1,2,0:T(8,128)(2,1)}, u32[]{:S(2)}, u32[]{:S(2)}) %all-to-all-start.1) | async-done | bytes 524320 | tf_op jit(solution)/shard_map/all_to_all | solution.py:346
  149.8 29.5 %all_to_all.44 = bf16[4,128,2048]{2,1,0:T(8,128)(2,1)} all-to-all(bf16[4,128,2048]{2,1,0:T(8,128)(2,1)S(1)} %broadcast_in_dim.14), channel_id=1, replica_groups=mesh['chip'=4,'core'=2,'hi'=2,'lo'=2] {'chip'}, dimensions={0} | all-to-all | bytes 4194304 | tf_op jit(solution)/shard_map/all_to_all | solution.py:346
  183.8 9.2 %all-gather.6.cloned.1.call-done = bf16[2048,1536]{1,0:T(8,128)(2,1)} async-done(((bf16[512,1536]{1,0:T(8,128)(2,1)}), bf16[2048,1536]{1,0:T(8,128)(2,1)}) %all-gather.6.cloned.1.call-update) | async-done | bytes 6291472 | tf_op jit(solution)/shard_map/all_gather | solution.py:408
  193.0 6.3 %fusion.47 = f32[512,1536]{1,0:T(8,128)S(1)} fusion(bf16[512,2048]{1,0:T(8,128)(2,1)} %collective-permute-done.14, bf16[2048,1536]{1,0:T(8,128)(2,1)} %all-gather.6.cloned.1.call-done), kind=kOutput, calls=%fused_computation.150 | convolution fusion | flops 3221225472 | bytes 11534336 | tf_op jit(solution)/shard_map/dot_general | solution.py:26
  201.6 5.4 %fusion.46 = f32[512,1536]{1,0:T(8,128)S(1)} fusion(bf16[512,2048]{1,0:T(8,128)(2,1)} %bitcast.17, bf16[2048,1536]{1,0:T(8,128)(2,1)S(1)} %copy-done.40), kind=kOutput, calls=%fused_computation.149 | convolution fusion | flops 3221225472 | bytes 11534336 | tf_op jit(solution)/shard_map/dot_general | solution.py:26
  217.5 7.4 %collective-permute-start.16 = (bf16[192,2048]{1,0:T(8,128)(2,1)}, bf16[192,2048]{1,0:T(8,128)(2,1)}, u32[]{:S(2)}, u32[]{:S(2)}) collective-permute-start(bf16[192,2048]{1,0:T(8,128)(2,1)} %get-tuple-element.186), channel_id=1, source_target_pairs={{0,0},{4,8},{8,16},{12,24},{16,4},{20,12},{24,20},{28,28},{1,1},{5... | collective-permute-start | bytes 2359304 | tf_op jit(solution)/shard_map/ppermute | solution.py:500
  236.1 11.0 %collective-permute-done.17 = bf16[192,2048]{1,0:T(8,128)(2,1)} collective-permute-done((bf16[192,2048]{1,0:T(8,128)(2,1)}, bf16[192,2048]{1,0:T(8,128)(2,1)}, u32[]{:S(2)}, u32[]{:S(2)}) %collective-permute-start.17) | collective-permute-done | bytes 786464 | tf_op jit(solution)/shard_map/ppermute | solution.py:500
  257.6 5.6 %multiply_convert_fusion.1 = (bf16[512,768]{1,0:T(8,128)(2,1)S(1)}, bf16[512,768]{1,0:T(8,128)(2,1)S(1)}) fusion(f32[512,1536]{1,0:T(8,128)} %copy-done.30, bf16[512,2048]{1,0:T(8,128)(2,1)} %collective-permute-done.15, bf16[768,2048]{1,0:T(8,128)(2,1)} %all-gather.8.cloned.1.call-done), kind=kOutput, calls=%fused_computation.35 | convolution fusion | flops 1615724544 | bytes 9961472 | tf_op jit(solution)/shard_map/dot_general | solution.py:30
  264.4 6.6 %convolution_convert_fusion.4 = bf16[512,2048]{1,0:T(8,128)(2,1)S(1)} fusion(bf16[2048,1536]{1,0:T(8,128)(2,1)} %all-gather.6.cloned.1.call-done, bf16[512,768]{1,0:T(8,128)(2,1)S(1)} %get-tuple-element.182, bf16[512,768]{1,0:T(8,128)(2,1)S(1)} %get-tuple-element.181), kind=kOutput, calls=%fused_computation.22 | convolution fusion | flops 3225419776 | bytes 9961472 | tf_op jit(solution)/shard_map/dot_general | solution.py:30
  286.4 10.2 %fusion.21 = f32[2048,1536]{1,0:T(8,128)} fusion(bf16[512,2048]{1,0:T(8,128)(2,1)} %bitcast.17, bf16[512,768]{1,0:T(8,128)(2,1)} %copy-done.43, bf16[512,768]{1,0:T(8,128)(2,1)} %copy-done.42), kind=kOutput, calls=%fused_computation.69 | convolution fusion | flops 3224371200 | bytes 16252928 | tf_op jit(solution)/shard_map/dot_general | solution.py:34
  296.6 7.4 %add_convert_fusion = bf16[2048,1536]{1,0:T(8,128)(2,1)S(1)} fusion(f32[2048,1536]{1,0:T(8,128)} %fusion.21, bf16[512,2048]{1,0:T(8,128)(2,1)} %collective-permute-done.14, bf16[512,768]{1,0:T(8,128)(2,1)S(1)} %copy-done.47, bf16[512,768]{1,0:T(8,128)(2,1)S(1)} %copy-done.45), kind=kOutput, calls=%fused_computation | convolution fusion | flops 3230662656 | bytes 22544384 | tf_op jit(solution)/shard_map/dot_general | solution.py:34
  307.2 5.7 %all-to-all-done.3.refs_1_ = bf16[4,128,2048]{2,1,0:T(8,128)(2,1)} async-done(((bf16[4,128,2048]{2,1,0:T(8,128)(2,1)}), bf16[4,128,2048]{2,1,0:T(8,128)(2,1)}, u32[]{:S(2)}, u32[]{:S(2)}) %all-to-all-start.3) | async-done | bytes 2097184 | tf_op jit(solution)/shard_map/all_to_all | solution.py:346
  314.4 6.0 %project_back.1 = (f32[128,2048]{1,0:T(8,128)S(1)}, bf16[128,2048]{1,0:T(8,128)(2,1)S(1)}, f32[1,2048]{1,0:T(1,128)S(1)}, bf16[8,128,256]{2,1,0:T(8,128)(2,1)S(1)}) custom-call(s32[8]{0:T(128)S(1)} %stack.35.refs_0_, bf16[4,128,2048]{2,1,0:T(8,128)(2,1)} %all-to-all-done.3.refs_1_, f32[128,2048]{1,0:T(8,128)S(1)} %get-tuple-element.170.refs_2_, ...), custom_call_target="tpu_custom_call" | custom-call | tf_op jit(solution)/shard_map/project_back/pallas_call | solution.py:281
  332.7 5.9 %add_convert_fusion.4 = bf16[512,2048]{1,0:T(8,128)(2,1)} fusion(bf16[512,2048]{1,0:T(8,128)(2,1)} %collective-permute-done.21, bf16[512,768]{1,0:T(8,128)(2,1)} %copy-done.35, bf16[768,2048]{1,0:T(8,128)(2,1)} %all-gather.8.cloned.1.call-done), kind=kOutput, calls=%fused_computation.14 | convolution fusion | flops 1615855616 | bytes 8126464 | tf_op jit(solution)/shard_map/dot_general | solution.py:26
  346.8 10.7 %attend_back.1 = (bf16[1024,512]{1,0:T(8,128)(2,1)S(1)}, f32[2,128]{1,0:T(2,128)S(1)}) custom-call(s32[16]{0:T(128)S(1)} %get-tuple-element.211.sources_ref, s32[16]{0:T(128)S(1)} %get-tuple-element.210.places_ref, f32[1024,512]{1,0:T(8,128)} %pad_maximum_fusion.1.raw_ref, f32[1024,128]{1,0:T(8,128)S(1)} %get-tuple-element.220.cos_ref, ...), custom_call_target="tpu_custom_call" | custom-call | tf_op jit(solution)/shard_map/attend_back/pallas_call | solution.py:223
  386.5 8.9 %collective-permute-done.26 = bf16[128,2048]{1,0:T(8,128)(2,1)S(1)} collective-permute-done((bf16[128,2048]{1,0:T(8,128)(2,1)S(1)}, bf16[128,2048]{1,0:T(8,128)(2,1)S(1)}, u32[]{:S(2)}, u32[]{:S(2)}) %collective-permute-start.26) | collective-permute-done | bytes 524320 | tf_op jit(solution)/shard_map/ppermute | solution.py:342
  403.6 14.9 %all-to-all-done.5 = bf16[8,256,512]{2,1,0:T(8,128)(2,1)} async-done(((bf16[8,256,512]{2,1,0:T(8,128)(2,1)}), bf16[8,256,512]{2,1,0:T(8,128)(2,1)}, u32[]{:S(2)}, u32[]{:S(2)}) %all-to-all-start.5) | async-done | bytes 2097184 | tf_op jit(solution)/shard_map/all_to_all | solution.py:346
  434.5 12.3 %collective-permute-done.32 = bf16[128,2048]{1,0:T(8,128)(2,1)S(1)} collective-permute-done((bf16[128,2048]{1,0:T(8,128)(2,1)S(1)}, bf16[128,2048]{1,0:T(8,128)(2,1)S(1)}, u32[]{:S(2)}, u32[]{:S(2)}) %collective-permute-start.32) | collective-permute-done | bytes 524320 | tf_op jit(solution)/shard_map/ppermute | solution.py:342
  446.8 8.5 %collective-permute-done.31 = bf16[128,2048]{1,0:T(8,128)(2,1)S(1)} collective-permute-done((bf16[128,2048]{1,0:T(8,128)(2,1)S(1)}, bf16[128,2048]{1,0:T(8,128)(2,1)S(1)}, u32[]{:S(2)}, u32[]{:S(2)}) %collective-permute-start.31) | collective-permute-done | bytes 524320 | tf_op jit(solution)/shard_map/ppermute | solution.py:342
  468.4 13.2 %all-to-all-done.6.in_ref = bf16[8,64,1536]{2,1,0:T(8,128)(2,1)S(1)} async-done(((bf16[8,64,1536]{2,1,0:T(8,128)(2,1)}), bf16[8,64,1536]{2,1,0:T(8,128)(2,1)S(1)}, u32[]{:S(2)}, u32[]{:S(2)}) %all-to-all-start.6) | async-done | bytes 1572896 | tf_op jit(solution)/shard_map/all_to_all | solution.py:346
  (299 shorter events, 244.3 us)
Async XLA Ops:
  7.2 69.6 %all-gather.4.cloned.1.call-start = ((), (), s32[]{:S(2)}) async-start(), calls=%async_computation.11 | async-start | bytes 3932160 | tf_op jit(solution)/shard_map/all_gather | solution.py:408
  12.0 31.1 %all-to-all-start = ((bf16[4,128,2048]{2,1,0:T(8,128)(2,1)}), bf16[4,128,2048]{2,1,0:T(8,128)(2,1)}, u32[]{:S(2)}, u32[]{:S(2)}) async-start(bf16[4,128,2048]{2,1,0:T(8,128)(2,1)} %broadcast_in_dim.11), calls=%async_computation | async-start | bytes 4194304 | tf_op jit(solution)/shard_map/all_to_all | solution.py:346
  17.3 175.7 %all-gather.6.cloned.1.call-start = ((), (), s32[]{:S(2)}) async-start(), calls=%async_computation.12 | async-start | bytes 7864320 | tf_op jit(solution)/shard_map/all_gather | solution.py:408
  17.4 26.4 %collective-permute-start = (bf16[1,1088]{1,0:T(2,128)(2,1)S(1)}, bf16[1,1088]{1,0:T(2,128)(2,1)S(1)}, u32[]{:S(2)}, u32[]{:S(2)}) collective-permute-start(bf16[1,1088]{1,0:T(2,128)(2,1)S(1)} %reshape.172), channel_id=1, source_target_pairs={{0,1},{1,0},{2,3},{3,2},{4,5},{5,4},{6,7},{7,6},{8,9},{9,8},{10,11... | collective-permute-start | bytes 6536 | tf_op jit(solution)/shard_map/ppermute | solution.py:342
  19.8 24.0 %collective-permute-start.1 = (bf16[1,1088]{1,0:T(2,128)(2,1)S(1)}, bf16[1,1088]{1,0:T(2,128)(2,1)S(1)}, u32[]{:S(2)}, u32[]{:S(2)}) collective-permute-start(bf16[1,1088]{1,0:T(2,128)(2,1)S(1)} %reshape.172), channel_id=1, source_target_pairs={{0,2},{1,3},{2,0},{3,1},{4,6},{5,7},{6,4},{7,5},{8,10},{9,11},{10,... | collective-permute-start | bytes 6536 | tf_op jit(solution)/shard_map/ppermute | solution.py:342
  43.0 29.9 %collective-permute-start.6 = (bf16[512,2048]{1,0:T(8,128)(2,1)}, bf16[512,2048]{1,0:T(8,128)(2,1)}, u32[]{:S(2)}, u32[]{:S(2)}) collective-permute-start(bf16[512,2048]{1,0:T(8,128)(2,1)} %bitcast.1), channel_id=1, source_target_pairs={{0,4},{4,0},{1,5},{5,1},{2,6},{6,2},{3,7},{7,3},{8,12},{12,8},{9,1... | collective-permute-start | bytes 6291464 | tf_op jit(solution)/shard_map/ppermute | solution.py:342
  45.9 25.3 %collective-permute-start.4 = (bf16[128,2048]{1,0:T(8,128)(2,1)S(1)}, bf16[128,2048]{1,0:T(8,128)(2,1)S(1)}, u32[]{:S(2)}, u32[]{:S(2)}) collective-permute-start(bf16[128,2048]{1,0:T(8,128)(2,1)S(1)} %bitcast.98), channel_id=1, source_target_pairs={{0,16},{8,24},{16,0},{24,8},{1,17},{9,25},{17,1},{25,9},{2,18},{10... | collective-permute-start | bytes 1572872 | tf_op jit(solution)/shard_map/ppermute | solution.py:342
  46.4 25.7 %collective-permute-start.5 = (bf16[128,2048]{1,0:T(8,128)(2,1)S(1)}, bf16[128,2048]{1,0:T(8,128)(2,1)S(1)}, u32[]{:S(2)}, u32[]{:S(2)}) collective-permute-start(bf16[128,2048]{1,0:T(8,128)(2,1)S(1)} %bitcast.99), channel_id=1, source_target_pairs={{0,24},{8,16},{16,8},{24,0},{1,25},{9,17},{17,9},{25,1},{2,26},{10... | collective-permute-start | bytes 1572872 | tf_op jit(solution)/shard_map/ppermute | solution.py:342
  79.1 56.4 %collective-permute-start.7 = (bf16[2048,256]{1,0:T(8,128)(2,1)}, bf16[2048,256]{1,0:T(8,128)(2,1)S(1)}, u32[]{:S(2)}, u32[]{:S(2)}) collective-permute-start(bf16[2048,256]{1,0:T(8,128)(2,1)} %slice.73.refs_5_), channel_id=1, source_target_pairs={{0,8},{8,0},{16,24},{24,16},{1,9},{9,1},{17,25},{25,17},{2,10},{10... | collective-permute-start | bytes 3145736 | tf_op jit(solution)/shard_map/ppermute | solution.py:342
  80.6 55.0 %collective-permute-start.8 = (bf16[2048,256]{1,0:T(8,128)(2,1)}, bf16[2048,256]{1,0:T(8,128)(2,1)}, u32[]{:S(2)}, u32[]{:S(2)}) collective-permute-start(bf16[2048,256]{1,0:T(8,128)(2,1)} %slice.73.refs_5_), channel_id=1, source_target_pairs={{0,16},{8,24},{16,0},{24,8},{1,17},{9,25},{17,1},{25,9},{2,18},{10... | collective-permute-start | bytes 3145736 | tf_op jit(solution)/shard_map/ppermute | solution.py:342
  82.1 54.0 %collective-permute-start.9 = (bf16[2048,256]{1,0:T(8,128)(2,1)}, bf16[2048,256]{1,0:T(8,128)(2,1)}, u32[]{:S(2)}, u32[]{:S(2)}) collective-permute-start(bf16[2048,256]{1,0:T(8,128)(2,1)} %slice.73.refs_5_), channel_id=1, source_target_pairs={{0,24},{8,16},{16,8},{24,0},{1,25},{9,17},{17,9},{25,1},{2,26},{10... | collective-permute-start | bytes 3145736 | tf_op jit(solution)/shard_map/ppermute | solution.py:342
  105.9 27.7 %all-to-all-start.1 = ((bf16[8,128,256]{1,2,0:T(8,128)(2,1)}), bf16[8,128,256]{1,2,0:T(8,128)(2,1)}, u32[]{:S(2)}, u32[]{:S(2)}) async-start(bf16[8,128,256]{1,2,0:T(8,128)(2,1)} %copy.46), calls=%async_computation.1 | async-start | bytes 1048576 | tf_op jit(solution)/shard_map/all_to_all | solution.py:346
  110.1 147.6 %all-gather.8.cloned.1.call-start = ((), (), s32[]{:S(2)}) async-start(), calls=%async_computation.13 | async-start | bytes 3932160 | tf_op jit(solution)/shard_map/all_gather | solution.py:408
  110.2 31.0 %collective-permute-start.10 = (bf16[2048,256]{1,0:T(8,128)(2,1)}, bf16[2048,256]{1,0:T(8,128)(2,1)}, u32[]{:S(2)}, u32[]{:S(2)}) collective-permute-start(bf16[2048,256]{1,0:T(8,128)(2,1)} %slice.73.refs_5_), channel_id=1, source_target_pairs={{0,4},{4,0},{1,5},{5,1},{2,6},{6,2},{3,7},{7,3},{8,12},{12,8},{9,1... | collective-permute-start | bytes 3145736 | tf_op jit(solution)/shard_map/ppermute | solution.py:342
  179.3 143.6 %reduce-scatter.4.cloned.1.call-start = ((), (), s32[]{:S(2)}) async-start(), calls=%async_computation.14 | async-start | bytes 3932160 | tf_op jit(solution)/shard_map/reduce_scatter | solution.py:412
  179.6 27.9 %collective-permute-start.15 = (bf16[512,2048]{1,0:T(8,128)(2,1)}, bf16[512,2048]{1,0:T(8,128)(2,1)}, u32[]{:S(2)}, u32[]{:S(2)}) collective-permute-start(bf16[512,2048]{1,0:T(8,128)(2,1)} %constant_dynamic-update-slice_fusion.8), channel_id=1, source_target_pairs={{0,4},{4,0},{1,5},{5,1},{2,6},{6,2},{3,7},{7,3},{8,12},{12,8},{9,1... | collective-permute-start | bytes 6291464 | tf_op jit(solution)/shard_map/ppermute | solution.py:342
  226.9 25.3 %collective-permute-start.18 = (bf16[192,2048]{1,0:T(8,128)(2,1)}, bf16[192,2048]{1,0:T(8,128)(2,1)}, u32[]{:S(2)}, u32[]{:S(2)}) collective-permute-start(bf16[192,2048]{1,0:T(8,128)(2,1)} %get-tuple-element.184), channel_id=1, source_target_pairs={{0,16},{4,24},{8,0},{12,8},{16,20},{20,28},{24,4},{28,12},{1,17},{... | collective-permute-start | bytes 2359304 | tf_op jit(solution)/shard_map/ppermute | solution.py:500
  227.0 28.5 %collective-permute-start.19 = (bf16[192,2048]{1,0:T(8,128)(2,1)}, bf16[192,2048]{1,0:T(8,128)(2,1)}, u32[]{:S(2)}, u32[]{:S(2)}) collective-permute-start(bf16[192,2048]{1,0:T(8,128)(2,1)} %get-tuple-element.183), channel_id=1, source_target_pairs={{0,24},{4,0},{8,8},{12,16},{16,28},{20,4},{24,12},{28,20},{1,25},{... | collective-permute-start | bytes 2359304 | tf_op jit(solution)/shard_map/ppermute | solution.py:500
  281.7 31.3 %all-to-all-start.3 = ((bf16[4,128,2048]{2,1,0:T(8,128)(2,1)}), bf16[4,128,2048]{2,1,0:T(8,128)(2,1)}, u32[]{:S(2)}, u32[]{:S(2)}) async-start(bf16[4,128,2048]{2,1,0:T(8,128)(2,1)} %bitcast.119), calls=%async_computation.3 | async-start | bytes 4194304 | tf_op jit(solution)/shard_map/all_to_all | solution.py:346
  286.1 170.6 %reduce-scatter.6.cloned.1.call-start = ((), (), s32[]{:S(2)}) async-start(), calls=%async_computation.15 | async-start | bytes 7864320 | tf_op jit(solution)/shard_map/reduce_scatter | solution.py:412
  371.5 23.9 %collective-permute-start.26 = (bf16[128,2048]{1,0:T(8,128)(2,1)S(1)}, bf16[128,2048]{1,0:T(8,128)(2,1)S(1)}, u32[]{:S(2)}, u32[]{:S(2)}) collective-permute-start(bf16[128,2048]{1,0:T(8,128)(2,1)S(1)} %copy-done.13), channel_id=1, source_target_pairs={{0,16},{8,24},{16,0},{24,8},{1,17},{9,25},{17,1},{25,9},{2,18},{10... | collective-permute-start | bytes 1572872 | tf_op jit(solution)/shard_map/ppermute | solution.py:342
  378.4 40.0 %all-to-all-start.5 = ((bf16[8,256,512]{2,1,0:T(8,128)(2,1)}), bf16[8,256,512]{2,1,0:T(8,128)(2,1)}, u32[]{:S(2)}, u32[]{:S(2)}) async-start(bf16[8,256,512]{2,1,0:T(8,128)(2,1)} %bitcast.118), calls=%async_computation.6 | async-start | bytes 4194304 | tf_op jit(solution)/shard_map/all_to_all | solution.py:346
  382.8 112.0 %reduce-scatter.8.cloned.1.call-start = ((), (), s32[]{:S(2)}) async-start(), calls=%async_computation.16 | async-start | bytes 3932160 | tf_op jit(solution)/shard_map/reduce_scatter | solution.py:412
  456.7 24.9 %all-to-all-start.6 = ((bf16[8,64,1536]{2,1,0:T(8,128)(2,1)}), bf16[8,64,1536]{2,1,0:T(8,128)(2,1)S(1)}, u32[]{:S(2)}, u32[]{:S(2)}) async-start(bf16[8,64,1536]{2,1,0:T(8,128)(2,1)} %bitcast.122), calls=%async_computation.9 | async-start | bytes 3145728 | tf_op jit(solution)/shard_map/all_to_all | solution.py:346
  (72 other events, 614.0 us)
Sparse Core Ops, SparseCore 0:
  10.5 66.2 all-gather.3
  78.9 114.0 all-gather.5
  194.6 61.7 all-gather.7
  258.5 59.8 reduce-scatter.3
  320.5 110.7 reduce-scatter.5
  433.5 61.2 reduce-scatter.7

commit v8 on v7

--- a/solution.py
+++ b/solution.py
@@ -13,6 +13,7 @@
 HD = 128
 BLOCK = 64
 TILE = 256
+WIDEN_ROWS = 16
 
 epsilon = 1e-06
 theta_base = 1000000.0
@@ -326,8 +327,9 @@
     return pl.pallas_call(
         widen_kernel,
         out_shape=tuple(jax.ShapeDtypeStruct((rows, width), high) for width in widths),
-        in_specs=in_memory([pltpu.VMEM]),
-        out_specs=in_memory([pltpu.VMEM] * len(widths)),
+        grid=(rows // WIDEN_ROWS,),
+        in_specs=[pl.BlockSpec((WIDEN_ROWS, sum(widths)), lambda i: (i, 0))],
+        out_specs=[pl.BlockSpec((WIDEN_ROWS, width), lambda i: (i, 0)) for width in widths],
         compiler_params=pltpu.CompilerParams(vmem_limit_bytes=vmem_bytes),
         name="widen",
     )(values)

time: 511 us -> 512 us (level)
  no operation moved by 1% of the time
where the time goes in v8:
time: 512 us; the launch traced here: 505 us
  waiting for transfers between devices  156 us (30%)
  matrix products  109 us (21%)
  starting transfers between devices  69.7 us (14%)
  local copies, waits for them, and re-layouts  69.5 us (14%)
  blocking collectives  29.5 us (6%)
  Pallas kernels  29.1 us (6%)
  other arithmetic  26 us (5%)
  between operations  15.6 us (3%)
    all_to_all x7, waiting for transfers between devices, exchange(): return lax.all_to_all(values, axis, 0, 0, tiled=True)  74 us
    ppermute x29, waiting for transfers between devices, swap(): return lax.ppermute(values, axis, [(i, i ^ mask) for i in range(size)])  55.1 us
    dot_general x14, matrix products, dot(): return jnp.dot(left, right, preferred_element_type=high)  43.5 us
    dot_general x8, matrix products, t_dot(): lax.dot_general(left, right, (((0,), (0,)), ((), ())), preferred_element_...  37.3 us
    all_to_all x1, blocking collectives, exchange(): return lax.all_to_all(values, axis, 0, 0, tiled=True)  29.5 us
    all_to_all x7, starting transfers between devices, exchange(): return lax.all_to_all(values, axis, 0, 0, tiled=True)  28.5 us
    dot_general x6, matrix products, dot_t(): lax.dot_general(left, right, (((1,), (1,)), ((), ())), preferred_element_...  28.3 us
    ppermute x29, starting transfers between devices, swap(): return lax.ppermute(values, axis, [(i, i ^ mask) for i in range(size)])  26.2 us
  transfers between devices with their start and end apart: 46, of which 25 were waited for; matrix products, arithmetic and copies ran while one was open for 37% of the time, Pallas kernels for 5%

profile of v8, /device:TPU:0, one launch (start us, length us, event | category | flops | bytes accessed | tf_op | source)
XLA Modules:
  0.0 504.7 jit_solution(17090479551789415430)
XLA Ops:
  32.2 10.8 %all-to-all-done = bf16[4,128,2048]{2,1,0:T(8,128)(2,1)} async-done(((bf16[4,128,2048]{2,1,0:T(8,128)(2,1)}), bf16[4,128,2048]{2,1,0:T(8,128)(2,1)}, u32[]{:S(2)}, u32[]{:S(2)}) %all-to-all-start) | async-done | bytes 2097184 | tf_op jit(solution)/shard_map/all_to_all | solution.py:348
  52.5 6.8 %collective-permute-done.3 = bf16[128,2048]{1,0:T(8,128)(2,1)} collective-permute-done((bf16[128,2048]{1,0:T(8,128)(2,1)S(1)}, bf16[128,2048]{1,0:T(8,128)(2,1)}, u32[]{:S(2)}, u32[]{:S(2)}) %collective-permute-start.3) | collective-permute-done | bytes 524320 | tf_op jit(solution)/shard_map/ppermute | solution.py:344
  61.1 10.1 %collective-permute-done.4 = bf16[128,2048]{1,0:T(8,128)(2,1)S(1)} collective-permute-done((bf16[128,2048]{1,0:T(8,128)(2,1)S(1)}, bf16[128,2048]{1,0:T(8,128)(2,1)S(1)}, u32[]{:S(2)}, u32[]{:S(2)}) %collective-permute-start.4) | collective-permute-done | bytes 524320 | tf_op jit(solution)/shard_map/ppermute | solution.py:344
  91.1 8.8 %attend.1 = (bf16[1024,256]{1,0:T(8,128)(2,1)S(1)}, bf16[1024,256]{1,0:T(8,128)(2,1)S(1)}, bf16[1024,256]{1,0:T(8,128)(2,1)S(1)}, bf16[1024,128]{1,0:T(8,128)(2,...) custom-call(s32[16]{0:T(128)S(1)} %get-tuple-element.211.sources_ref, ...), custom_call_target="tpu_custom_call" | custom-call | tf_op jit(solution)/shard_map/attend/pallas_call | solution.py:209
  110.5 23.1 %all-to-all-done.1 = bf16[8,128,256]{1,2,0:T(8,128)(2,1)} async-done(((bf16[8,128,256]{1,2,0:T(8,128)(2,1)}), bf16[8,128,256]{1,2,0:T(8,128)(2,1)}, u32[]{:S(2)}, u32[]{:S(2)}) %all-to-all-start.1) | async-done | bytes 524320 | tf_op jit(solution)/shard_map/all_to_all | solution.py:348
  149.8 29.5 %all_to_all.44 = bf16[4,128,2048]{2,1,0:T(8,128)(2,1)} all-to-all(bf16[4,128,2048]{2,1,0:T(8,128)(2,1)S(1)} %broadcast_in_dim.14), channel_id=1, replica_groups=mesh['chip'=4,'core'=2,'hi'=2,'lo'=2] {'chip'}, dimensions={0} | all-to-all | bytes 4194304 | tf_op jit(solution)/shard_map/all_to_all | solution.py:348
  183.8 9.2 %all-gather.6.cloned.1.call-done = bf16[2048,1536]{1,0:T(8,128)(2,1)} async-done(((bf16[512,1536]{1,0:T(8,128)(2,1)}), bf16[2048,1536]{1,0:T(8,128)(2,1)}) %all-gather.6.cloned.1.call-update) | async-done | bytes 6291472 | tf_op jit(solution)/shard_map/all_gather | solution.py:410
  193.0 6.3 %fusion.47 = f32[512,1536]{1,0:T(8,128)S(1)} fusion(bf16[512,2048]{1,0:T(8,128)(2,1)} %collective-permute-done.14, bf16[2048,1536]{1,0:T(8,128)(2,1)} %all-gather.6.cloned.1.call-done), kind=kOutput, calls=%fused_computation.150 | convolution fusion | flops 3221225472 | bytes 11534336 | tf_op jit(solution)/shard_map/dot_general | solution.py:27
  201.6 5.4 %fusion.46 = f32[512,1536]{1,0:T(8,128)S(1)} fusion(bf16[512,2048]{1,0:T(8,128)(2,1)} %bitcast.17, bf16[2048,1536]{1,0:T(8,128)(2,1)S(1)} %copy-done.40), kind=kOutput, calls=%fused_computation.149 | convolution fusion | flops 3221225472 | bytes 11534336 | tf_op jit(solution)/shard_map/dot_general | solution.py:27
  217.5 7.4 %collective-permute-start.16 = (bf16[192,2048]{1,0:T(8,128)(2,1)}, bf16[192,2048]{1,0:T(8,128)(2,1)}, u32[]{:S(2)}, u32[]{:S(2)}) collective-permute-start(bf16[192,2048]{1,0:T(8,128)(2,1)} %get-tuple-element.186), channel_id=1, source_target_pairs={{0,0},{4,8},{8,16},{12,24},{16,4},{20,12},{24,20},{28,28},{1,1},{5... | collective-permute-start | bytes 2359304 | tf_op jit(solution)/shard_map/ppermute | solution.py:502
  236.1 11.0 %collective-permute-done.17 = bf16[192,2048]{1,0:T(8,128)(2,1)} collective-permute-done((bf16[192,2048]{1,0:T(8,128)(2,1)}, bf16[192,2048]{1,0:T(8,128)(2,1)}, u32[]{:S(2)}, u32[]{:S(2)}) %collective-permute-start.17) | collective-permute-done | bytes 786464 | tf_op jit(solution)/shard_map/ppermute | solution.py:502
  257.6 5.6 %multiply_convert_fusion.1 = (bf16[512,768]{1,0:T(8,128)(2,1)S(1)}, bf16[512,768]{1,0:T(8,128)(2,1)S(1)}) fusion(f32[512,1536]{1,0:T(8,128)} %copy-done.30, bf16[512,2048]{1,0:T(8,128)(2,1)} %collective-permute-done.15, bf16[768,2048]{1,0:T(8,128)(2,1)} %all-gather.8.cloned.1.call-done), kind=kOutput, calls=%fused_computation.35 | convolution fusion | flops 1615724544 | bytes 9961472 | tf_op jit(solution)/shard_map/dot_general | solution.py:31
  264.4 6.6 %convolution_convert_fusion.4 = bf16[512,2048]{1,0:T(8,128)(2,1)S(1)} fusion(bf16[2048,1536]{1,0:T(8,128)(2,1)} %all-gather.6.cloned.1.call-done, bf16[512,768]{1,0:T(8,128)(2,1)S(1)} %get-tuple-element.182, bf16[512,768]{1,0:T(8,128)(2,1)S(1)} %get-tuple-element.181), kind=kOutput, calls=%fused_computation.22 | convolution fusion | flops 3225419776 | bytes 9961472 | tf_op jit(solution)/shard_map/dot_general | solution.py:31
  286.4 10.2 %fusion.21 = f32[2048,1536]{1,0:T(8,128)} fusion(bf16[512,2048]{1,0:T(8,128)(2,1)} %bitcast.17, bf16[512,768]{1,0:T(8,128)(2,1)} %copy-done.43, bf16[512,768]{1,0:T(8,128)(2,1)} %copy-done.42), kind=kOutput, calls=%fused_computation.69 | convolution fusion | flops 3224371200 | bytes 16252928 | tf_op jit(solution)/shard_map/dot_general | solution.py:35
  296.6 7.4 %add_convert_fusion = bf16[2048,1536]{1,0:T(8,128)(2,1)S(1)} fusion(f32[2048,1536]{1,0:T(8,128)} %fusion.21, bf16[512,2048]{1,0:T(8,128)(2,1)} %collective-permute-done.14, bf16[512,768]{1,0:T(8,128)(2,1)S(1)} %copy-done.47, bf16[512,768]{1,0:T(8,128)(2,1)S(1)} %copy-done.45), kind=kOutput, calls=%fused_computation | convolution fusion | flops 3230662656 | bytes 22544384 | tf_op jit(solution)/shard_map/dot_general | solution.py:35
  307.2 5.7 %all-to-all-done.3.refs_1_ = bf16[4,128,2048]{2,1,0:T(8,128)(2,1)} async-done(((bf16[4,128,2048]{2,1,0:T(8,128)(2,1)}), bf16[4,128,2048]{2,1,0:T(8,128)(2,1)}, u32[]{:S(2)}, u32[]{:S(2)}) %all-to-all-start.3) | async-done | bytes 2097184 | tf_op jit(solution)/shard_map/all_to_all | solution.py:348
  314.4 6.0 %project_back.1 = (f32[128,2048]{1,0:T(8,128)S(1)}, bf16[128,2048]{1,0:T(8,128)(2,1)S(1)}, f32[1,2048]{1,0:T(1,128)S(1)}, bf16[8,128,256]{2,1,0:T(8,128)(2,1)S(1)}) custom-call(s32[8]{0:T(128)S(1)} %stack.35.refs_0_, bf16[4,128,2048]{2,1,0:T(8,128)(2,1)} %all-to-all-done.3.refs_1_, f32[128,2048]{1,0:T(8,128)S(1)} %get-tuple-element.170.refs_2_, ...), custom_call_target="tpu_custom_call" | custom-call | tf_op jit(solution)/shard_map/project_back/pallas_call | solution.py:282
  332.7 5.9 %add_convert_fusion.4 = bf16[512,2048]{1,0:T(8,128)(2,1)} fusion(bf16[512,2048]{1,0:T(8,128)(2,1)} %collective-permute-done.21, bf16[512,768]{1,0:T(8,128)(2,1)} %copy-done.35, bf16[768,2048]{1,0:T(8,128)(2,1)} %all-gather.8.cloned.1.call-done), kind=kOutput, calls=%fused_computation.14 | convolution fusion | flops 1615855616 | bytes 8126464 | tf_op jit(solution)/shard_map/dot_general | solution.py:27
  346.8 10.7 %attend_back.1 = (bf16[1024,512]{1,0:T(8,128)(2,1)S(1)}, f32[2,128]{1,0:T(2,128)S(1)}) custom-call(s32[16]{0:T(128)S(1)} %get-tuple-element.211.sources_ref, s32[16]{0:T(128)S(1)} %get-tuple-element.210.places_ref, f32[1024,512]{1,0:T(8,128)} %pad_maximum_fusion.1.raw_ref, f32[1024,128]{1,0:T(8,128)S(1)} %get-tuple-element.220.cos_ref, ...), custom_call_target="tpu_custom_call" | custom-call | tf_op jit(solution)/shard_map/attend_back/pallas_call | solution.py:224
  386.5 8.9 %collective-permute-done.26 = bf16[128,2048]{1,0:T(8,128)(2,1)S(1)} collective-permute-done((bf16[128,2048]{1,0:T(8,128)(2,1)S(1)}, bf16[128,2048]{1,0:T(8,128)(2,1)S(1)}, u32[]{:S(2)}, u32[]{:S(2)}) %collective-permute-start.26) | collective-permute-done | bytes 524320 | tf_op jit(solution)/shard_map/ppermute | solution.py:344
  403.6 14.9 %all-to-all-done.5 = bf16[8,256,512]{2,1,0:T(8,128)(2,1)} async-done(((bf16[8,256,512]{2,1,0:T(8,128)(2,1)}), bf16[8,256,512]{2,1,0:T(8,128)(2,1)}, u32[]{:S(2)}, u32[]{:S(2)}) %all-to-all-start.5) | async-done | bytes 2097184 | tf_op jit(solution)/shard_map/all_to_all | solution.py:348
  434.5 12.3 %collective-permute-done.32 = bf16[128,2048]{1,0:T(8,128)(2,1)S(1)} collective-permute-done((bf16[128,2048]{1,0:T(8,128)(2,1)S(1)}, bf16[128,2048]{1,0:T(8,128)(2,1)S(1)}, u32[]{:S(2)}, u32[]{:S(2)}) %collective-permute-start.32) | collective-permute-done | bytes 524320 | tf_op jit(solution)/shard_map/ppermute | solution.py:344
  446.8 8.5 %collective-permute-done.31 = bf16[128,2048]{1,0:T(8,128)(2,1)S(1)} collective-permute-done((bf16[128,2048]{1,0:T(8,128)(2,1)S(1)}, bf16[128,2048]{1,0:T(8,128)(2,1)S(1)}, u32[]{:S(2)}, u32[]{:S(2)}) %collective-permute-start.31) | collective-permute-done | bytes 524320 | tf_op jit(solution)/shard_map/ppermute | solution.py:344
  468.4 13.2 %all-to-all-done.6.in_ref = bf16[8,64,1536]{2,1,0:T(8,128)(2,1)S(1)} async-done(((bf16[8,64,1536]{2,1,0:T(8,128)(2,1)}), bf16[8,64,1536]{2,1,0:T(8,128)(2,1)S(1)}, u32[]{:S(2)}, u32[]{:S(2)}) %all-to-all-start.6) | async-done | bytes 1572896 | tf_op jit(solution)/shard_map/all_to_all | solution.py:348
  (299 shorter events, 244.8 us)
Async XLA Ops:
  7.2 69.6 %all-gather.4.cloned.1.call-start = ((), (), s32[]{:S(2)}) async-start(), calls=%async_computation.11 | async-start | bytes 3932160 | tf_op jit(solution)/shard_map/all_gather | solution.py:410
  12.0 31.1 %all-to-all-start = ((bf16[4,128,2048]{2,1,0:T(8,128)(2,1)}), bf16[4,128,2048]{2,1,0:T(8,128)(2,1)}, u32[]{:S(2)}, u32[]{:S(2)}) async-start(bf16[4,128,2048]{2,1,0:T(8,128)(2,1)} %broadcast_in_dim.11), calls=%async_computation | async-start | bytes 4194304 | tf_op jit(solution)/shard_map/all_to_all | solution.py:348
  17.3 175.7 %all-gather.6.cloned.1.call-start = ((), (), s32[]{:S(2)}) async-start(), calls=%async_computation.12 | async-start | bytes 7864320 | tf_op jit(solution)/shard_map/all_gather | solution.py:410
  17.4 26.4 %collective-permute-start = (bf16[1,1088]{1,0:T(2,128)(2,1)S(1)}, bf16[1,1088]{1,0:T(2,128)(2,1)S(1)}, u32[]{:S(2)}, u32[]{:S(2)}) collective-permute-start(bf16[1,1088]{1,0:T(2,128)(2,1)S(1)} %reshape.172), channel_id=1, source_target_pairs={{0,1},{1,0},{2,3},{3,2},{4,5},{5,4},{6,7},{7,6},{8,9},{9,8},{10,11... | collective-permute-start | bytes 6536 | tf_op jit(solution)/shard_map/ppermute | solution.py:344
  19.8 24.0 %collective-permute-start.1 = (bf16[1,1088]{1,0:T(2,128)(2,1)S(1)}, bf16[1,1088]{1,0:T(2,128)(2,1)S(1)}, u32[]{:S(2)}, u32[]{:S(2)}) collective-permute-start(bf16[1,1088]{1,0:T(2,128)(2,1)S(1)} %reshape.172), channel_id=1, source_target_pairs={{0,2},{1,3},{2,0},{3,1},{4,6},{5,7},{6,4},{7,5},{8,10},{9,11},{10,... | collective-permute-start | bytes 6536 | tf_op jit(solution)/shard_map/ppermute | solution.py:344
  43.0 29.9 %collective-permute-start.6 = (bf16[512,2048]{1,0:T(8,128)(2,1)}, bf16[512,2048]{1,0:T(8,128)(2,1)}, u32[]{:S(2)}, u32[]{:S(2)}) collective-permute-start(bf16[512,2048]{1,0:T(8,128)(2,1)} %bitcast.1), channel_id=1, source_target_pairs={{0,4},{4,0},{1,5},{5,1},{2,6},{6,2},{3,7},{7,3},{8,12},{12,8},{9,1... | collective-permute-start | bytes 6291464 | tf_op jit(solution)/shard_map/ppermute | solution.py:344
  45.9 25.3 %collective-permute-start.4 = (bf16[128,2048]{1,0:T(8,128)(2,1)S(1)}, bf16[128,2048]{1,0:T(8,128)(2,1)S(1)}, u32[]{:S(2)}, u32[]{:S(2)}) collective-permute-start(bf16[128,2048]{1,0:T(8,128)(2,1)S(1)} %bitcast.98), channel_id=1, source_target_pairs={{0,16},{8,24},{16,0},{24,8},{1,17},{9,25},{17,1},{25,9},{2,18},{10... | collective-permute-start | bytes 1572872 | tf_op jit(solution)/shard_map/ppermute | solution.py:344
  46.4 25.7 %collective-permute-start.5 = (bf16[128,2048]{1,0:T(8,128)(2,1)S(1)}, bf16[128,2048]{1,0:T(8,128)(2,1)S(1)}, u32[]{:S(2)}, u32[]{:S(2)}) collective-permute-start(bf16[128,2048]{1,0:T(8,128)(2,1)S(1)} %bitcast.99), channel_id=1, source_target_pairs={{0,24},{8,16},{16,8},{24,0},{1,25},{9,17},{17,9},{25,1},{2,26},{10... | collective-permute-start | bytes 1572872 | tf_op jit(solution)/shard_map/ppermute | solution.py:344
  79.1 56.4 %collective-permute-start.7 = (bf16[2048,256]{1,0:T(8,128)(2,1)}, bf16[2048,256]{1,0:T(8,128)(2,1)S(1)}, u32[]{:S(2)}, u32[]{:S(2)}) collective-permute-start(bf16[2048,256]{1,0:T(8,128)(2,1)} %slice.73.refs_5_), channel_id=1, source_target_pairs={{0,8},{8,0},{16,24},{24,16},{1,9},{9,1},{17,25},{25,17},{2,10},{10... | collective-permute-start | bytes 3145736 | tf_op jit(solution)/shard_map/ppermute | solution.py:344
  80.6 55.0 %collective-permute-start.8 = (bf16[2048,256]{1,0:T(8,128)(2,1)}, bf16[2048,256]{1,0:T(8,128)(2,1)}, u32[]{:S(2)}, u32[]{:S(2)}) collective-permute-start(bf16[2048,256]{1,0:T(8,128)(2,1)} %slice.73.refs_5_), channel_id=1, source_target_pairs={{0,16},{8,24},{16,0},{24,8},{1,17},{9,25},{17,1},{25,9},{2,18},{10... | collective-permute-start | bytes 3145736 | tf_op jit(solution)/shard_map/ppermute | solution.py:344
  82.1 54.0 %collective-permute-start.9 = (bf16[2048,256]{1,0:T(8,128)(2,1)}, bf16[2048,256]{1,0:T(8,128)(2,1)}, u32[]{:S(2)}, u32[]{:S(2)}) collective-permute-start(bf16[2048,256]{1,0:T(8,128)(2,1)} %slice.73.refs_5_), channel_id=1, source_target_pairs={{0,24},{8,16},{16,8},{24,0},{1,25},{9,17},{17,9},{25,1},{2,26},{10... | collective-permute-start | bytes 3145736 | tf_op jit(solution)/shard_map/ppermute | solution.py:344
  105.9 27.7 %all-to-all-start.1 = ((bf16[8,128,256]{1,2,0:T(8,128)(2,1)}), bf16[8,128,256]{1,2,0:T(8,128)(2,1)}, u32[]{:S(2)}, u32[]{:S(2)}) async-start(bf16[8,128,256]{1,2,0:T(8,128)(2,1)} %copy.46), calls=%async_computation.1 | async-start | bytes 1048576 | tf_op jit(solution)/shard_map/all_to_all | solution.py:348
  110.1 147.6 %all-gather.8.cloned.1.call-start = ((), (), s32[]{:S(2)}) async-start(), calls=%async_computation.13 | async-start | bytes 3932160 | tf_op jit(solution)/shard_map/all_gather | solution.py:410
  110.2 31.0 %collective-permute-start.10 = (bf16[2048,256]{1,0:T(8,128)(2,1)}, bf16[2048,256]{1,0:T(8,128)(2,1)}, u32[]{:S(2)}, u32[]{:S(2)}) collective-permute-start(bf16[2048,256]{1,0:T(8,128)(2,1)} %slice.73.refs_5_), channel_id=1, source_target_pairs={{0,4},{4,0},{1,5},{5,1},{2,6},{6,2},{3,7},{7,3},{8,12},{12,8},{9,1... | collective-permute-start | bytes 3145736 | tf_op jit(solution)/shard_map/ppermute | solution.py:344
  179.3 143.6 %reduce-scatter.4.cloned.1.call-start = ((), (), s32[]{:S(2)}) async-start(), calls=%async_computation.14 | async-start | bytes 3932160 | tf_op jit(solution)/shard_map/reduce_scatter | solution.py:414
  179.6 27.9 %collective-permute-start.15 = (bf16[512,2048]{1,0:T(8,128)(2,1)}, bf16[512,2048]{1,0:T(8,128)(2,1)}, u32[]{:S(2)}, u32[]{:S(2)}) collective-permute-start(bf16[512,2048]{1,0:T(8,128)(2,1)} %constant_dynamic-update-slice_fusion.8), channel_id=1, source_target_pairs={{0,4},{4,0},{1,5},{5,1},{2,6},{6,2},{3,7},{7,3},{8,12},{12,8},{9,1... | collective-permute-start | bytes 6291464 | tf_op jit(solution)/shard_map/ppermute | solution.py:344
  226.9 25.3 %collective-permute-start.18 = (bf16[192,2048]{1,0:T(8,128)(2,1)}, bf16[192,2048]{1,0:T(8,128)(2,1)}, u32[]{:S(2)}, u32[]{:S(2)}) collective-permute-start(bf16[192,2048]{1,0:T(8,128)(2,1)} %get-tuple-element.184), channel_id=1, source_target_pairs={{0,16},{4,24},{8,0},{12,8},{16,20},{20,28},{24,4},{28,12},{1,17},{... | collective-permute-start | bytes 2359304 | tf_op jit(solution)/shard_map/ppermute | solution.py:502
  227.0 28.5 %collective-permute-start.19 = (bf16[192,2048]{1,0:T(8,128)(2,1)}, bf16[192,2048]{1,0:T(8,128)(2,1)}, u32[]{:S(2)}, u32[]{:S(2)}) collective-permute-start(bf16[192,2048]{1,0:T(8,128)(2,1)} %get-tuple-element.183), channel_id=1, source_target_pairs={{0,24},{4,0},{8,8},{12,16},{16,28},{20,4},{24,12},{28,20},{1,25},{... | collective-permute-start | bytes 2359304 | tf_op jit(solution)/shard_map/ppermute | solution.py:502
  281.7 31.3 %all-to-all-start.3 = ((bf16[4,128,2048]{2,1,0:T(8,128)(2,1)}), bf16[4,128,2048]{2,1,0:T(8,128)(2,1)}, u32[]{:S(2)}, u32[]{:S(2)}) async-start(bf16[4,128,2048]{2,1,0:T(8,128)(2,1)} %bitcast.119), calls=%async_computation.3 | async-start | bytes 4194304 | tf_op jit(solution)/shard_map/all_to_all | solution.py:348
  286.1 170.6 %reduce-scatter.6.cloned.1.call-start = ((), (), s32[]{:S(2)}) async-start(), calls=%async_computation.15 | async-start | bytes 7864320 | tf_op jit(solution)/shard_map/reduce_scatter | solution.py:414
  371.5 23.9 %collective-permute-start.26 = (bf16[128,2048]{1,0:T(8,128)(2,1)S(1)}, bf16[128,2048]{1,0:T(8,128)(2,1)S(1)}, u32[]{:S(2)}, u32[]{:S(2)}) collective-permute-start(bf16[128,2048]{1,0:T(8,128)(2,1)S(1)} %copy-done.13), channel_id=1, source_target_pairs={{0,16},{8,24},{16,0},{24,8},{1,17},{9,25},{17,1},{25,9},{2,18},{10... | collective-permute-start | bytes 1572872 | tf_op jit(solution)/shard_map/ppermute | solution.py:344
  378.4 40.0 %all-to-all-start.5 = ((bf16[8,256,512]{2,1,0:T(8,128)(2,1)}), bf16[8,256,512]{2,1,0:T(8,128)(2,1)}, u32[]{:S(2)}, u32[]{:S(2)}) async-start(bf16[8,256,512]{2,1,0:T(8,128)(2,1)} %bitcast.118), calls=%async_computation.6 | async-start | bytes 4194304 | tf_op jit(solution)/shard_map/all_to_all | solution.py:348
  382.8 112.0 %reduce-scatter.8.cloned.1.call-start = ((), (), s32[]{:S(2)}) async-start(), calls=%async_computation.16 | async-start | bytes 3932160 | tf_op jit(solution)/shard_map/reduce_scatter | solution.py:414
  456.7 24.9 %all-to-all-start.6 = ((bf16[8,64,1536]{2,1,0:T(8,128)(2,1)}), bf16[8,64,1536]{2,1,0:T(8,128)(2,1)S(1)}, u32[]{:S(2)}, u32[]{:S(2)}) async-start(bf16[8,64,1536]{2,1,0:T(8,128)(2,1)} %bitcast.122), calls=%async_computation.9 | async-start | bytes 3145728 | tf_op jit(solution)/shard_map/all_to_all | solution.py:348
  (72 other events, 614.0 us)
Sparse Core Ops, SparseCore 0:
  10.5 66.2 all-gather.3
  78.9 114.0 all-gather.5
  194.6 61.7 all-gather.7
  258.5 59.8 reduce-scatter.3
  320.5 110.7 reduce-scatter.5
  433.5 61.2 reduce-scatter.7
